TPU v7x, 32 devices: a whole 2x2x4 slice. The times are simulated.
32 devices in a mesh: ctx: 4 (over y, x), tp: 8 (over z, core).
Axes of the slice: x: 2, y: 2, z: 4, core: 2. Of those that a mesh axis runs over, the one named last changes fastest.
Arguments:
- query_proj: bfloat16 [1536, 4096], P('ctx', 'tp'), may hold values from -16 to 16
- key_proj: bfloat16 [1536, 4096], P('ctx', 'tp'), may hold values from -16 to 16
- value_proj: bfloat16 [1536, 4096], P('ctx', 'tp'), may hold values from -6 to 6
- query_gain: float32 [4096], P('tp'), may hold values from 0.1 to 1.9
- key_gain: float32 [4096], P('tp'), may hold values from 0.1 to 1.9
- stripe_of: int32 [8], replicated, may hold values from 0 to 7, as said below
- grad_out: bfloat16 [1536, 4096], P('ctx', 'tp'), may hold values from -6 to 6
Outputs:
- grad_query: bfloat16 [1536, 4096], P('ctx', 'tp')
- grad_key: bfloat16 [1536, 4096], P('ctx', 'tp')
- grad_value: bfloat16 [1536, 4096], P('ctx', 'tp')
- grad_query_gain: float32 [4096], P('tp')
- grad_key_gain: float32 [4096], P('tp')
Inputs may be any that keep to these rules, and one draw needn't show every extreme that they name: `stripe_of`: each number of 0 to 7 appears once, and entries 2 d and 2 d + 1 sum to 7 for every d.
All inputs are finite; a program needn't handle non-finite values.
Results may differ from a plain program's by a relative error of at most 0.012.
The roundings to bfloat16 on the way count: a program that leaves them out, or rounds other values in their place, can miss the bound.
Values may be sent and summed in bfloat16 or wider, within the bound.
No kernel may reach another device: no remote copies, remote signals or barrier semaphores. Data moves between devices by JAX's collectives and lax.ppermute only.
A program may use at most 128 MiB of HBM per device.

v0:
```python
import math

import jax
import jax.numpy as jnp
from jax import lax
from jax.sharding import PartitionSpec as P

HD = 128
D = 4096


EPSILON = 1e-06


def row_positions(stripe_list, offset, count, stripe):
    storage_rows = offset + lax.iota(jnp.int32, count)
    stripe_ids = lax.iota(jnp.int32, stripe_list.shape[0])
    matches = (storage_rows // stripe)[:, None] == stripe_ids[None, :]
    chosen = jnp.sum(jnp.where(matches, stripe_list[None, :], 0), axis=1)
    return chosen * stripe + storage_rows % stripe


def block_scores(query_heads, grad_heads, query_places, key_heads, value_heads, key_places):
    scores = jnp.einsum(
        "thd,khd->htk", query_heads, key_heads, preferred_element_type=jnp.float32
    ) * HD ** (-0.5)
    visible = key_places[None, :] <= query_places[:, None]
    scores = jnp.where(visible[None], scores, -jnp.inf)
    grad_probs = jnp.einsum(
        "thd,khd->htk", grad_heads, value_heads, preferred_element_type=jnp.float32
    )
    return (scores, grad_probs)


def block_weights(scores, grad_probs, log_total, row_delta):
    probs = jnp.exp(scores - log_total[:, :, None])
    grad_scores = probs * (grad_probs - row_delta[:, :, None])
    return (probs.astype(jnp.bfloat16), grad_scores.astype(jnp.bfloat16))


def finish_norm(inverse_norm, unit_rows, unit_grad, mean_terms):
    return (inverse_norm * (unit_grad - unit_rows * (mean_terms / D)[:, None])).astype(jnp.bfloat16)


def per_device(query_proj, key_proj, value_proj, query_gain, key_gain, stripe_of, grad_out):
    token_count, local_width = query_proj.shape
    local_heads = local_width // HD
    stripe = token_count // 2
    device = lax.axis_index("ctx")
    query_rows = query_proj.astype(jnp.float32)
    key_rows = key_proj.astype(jnp.float32)
    query_square, key_square = lax.psum(
        (jnp.sum(query_rows * query_rows, axis=1), jnp.sum(key_rows * key_rows, axis=1)), "tp"
    )
    query_inverse = lax.rsqrt(query_square / D + EPSILON)[:, None]
    key_inverse = lax.rsqrt(key_square / D + EPSILON)[:, None]
    query_unit = query_rows * query_inverse
    key_unit = key_rows * key_inverse
    query_normed = (query_unit * query_gain).astype(jnp.bfloat16)
    key_normed = (key_unit * key_gain).astype(jnp.bfloat16)
    query_places = row_positions(stripe_of, device * token_count, token_count, stripe)
    query_heads = query_normed.reshape(token_count, local_heads, HD)
    grad_heads = grad_out.reshape(token_count, local_heads, HD)
    key_heads = key_normed.reshape(token_count, local_heads, HD)
    value_heads = value_proj.reshape(token_count, local_heads, HD)
    start_best = jnp.full((local_heads, token_count), -1e30, jnp.float32)
    zero_rows = jnp.zeros((local_heads, token_count), jnp.float32)
    key_piece = lax.all_gather(key_normed, "ctx", axis=0, tiled=True)
    value_piece = lax.all_gather(value_proj, "ctx", axis=0, tiled=True)
    row_count = key_piece.shape[0]
    block = math.gcd(row_count, 512)
    key_blocks = key_piece.reshape(row_count // block, block, local_heads, HD)
    value_blocks = value_piece.reshape(row_count // block, block, local_heads, HD)

    def forward_advance(status, entry):
        row_best, row_total, weighted = status
        key_block, value_block, block_index = entry
        key_places = row_positions(stripe_of, block_index * block, block, stripe)
        scores, grad_probs = block_scores(
            query_heads, grad_heads, query_places, key_block, value_block, key_places
        )
        new_best = jnp.maximum(row_best, jnp.max(scores, axis=2))
        decay_factor = jnp.exp(row_best - new_best)
        exponent = jnp.exp(scores - new_best[:, :, None])
        return (
            (
                new_best,
                row_total * decay_factor + jnp.sum(exponent, axis=2),
                weighted * decay_factor + jnp.sum(exponent * grad_probs, axis=2),
            ),
            None,
        )

    block_ids = jnp.arange(row_count // block, dtype=jnp.int32)
    row_best, row_total, weighted = lax.scan(
        forward_advance, (start_best, zero_rows, zero_rows), (key_blocks, value_blocks, block_ids)
    )[0]
    log_total = row_best + jnp.log(row_total)
    row_delta = weighted / row_total
    zero_grads = jnp.zeros((token_count, local_heads, HD), jnp.float32)
    total_all, delta_all = (
        lax.all_gather(log_total, "ctx", axis=1, tiled=True),
        lax.all_gather(row_delta, "ctx", axis=1, tiled=True),
    )

    def query_fold(carry_state, pieces):
        query_piece, grad_piece = pieces
        row_count = query_piece.shape[0]
        block = math.gcd(row_count, 512)
        query_blocks = query_piece.reshape(row_count // block, block, local_heads, HD)
        grad_blocks = grad_piece.reshape(row_count // block, block, local_heads, HD)

        def query_advance(status, entry):
            key_grad, value_grad = status
            query_block, grad_block, block_index = entry
            first_row = block_index * block
            block_places = row_positions(stripe_of, first_row, block, stripe)
            block_total = lax.dynamic_slice_in_dim(total_all, first_row, block, 1)
            block_delta = lax.dynamic_slice_in_dim(delta_all, first_row, block, 1)
            scores, grad_probs = block_scores(
                query_block, grad_block, block_places, key_heads, value_heads, query_places
            )
            probs_rounded, scores_rounded = block_weights(
                scores, grad_probs, block_total, block_delta
            )
            value_grad = value_grad + jnp.einsum(
                "htk,thd->khd", probs_rounded, grad_block, preferred_element_type=jnp.float32
            )
            key_grad = key_grad + jnp.einsum(
                "htk,thd->khd", scores_rounded, query_block, preferred_element_type=jnp.float32
            )
            return ((key_grad, value_grad), None)

        block_ids = jnp.arange(row_count // block, dtype=jnp.int32)
        return lax.scan(query_advance, carry_state, (query_blocks, grad_blocks, block_ids))[0]

    key_grad, value_grad = query_fold(
        (zero_grads, zero_grads),
        (
            lax.all_gather(query_normed, "ctx", axis=0, tiled=True),
            lax.all_gather(grad_out, "ctx", axis=0, tiled=True),
        ),
    )

    def key_fold(carry_state, pieces):
        key_piece, value_piece = pieces
        row_count = key_piece.shape[0]
        block = math.gcd(row_count, 512)
        key_blocks = key_piece.reshape(row_count // block, block, local_heads, HD)
        value_blocks = value_piece.reshape(row_count // block, block, local_heads, HD)

        def key_advance(query_grad, entry):
            key_block, value_block, block_index = entry
            key_places = row_positions(stripe_of, block_index * block, block, stripe)
            scores, grad_probs = block_scores(
                query_heads, grad_heads, query_places, key_block, value_block, key_places
            )
            probs_rounded, scores_rounded = block_weights(scores, grad_probs, log_total, row_delta)
            query_grad = query_grad + jnp.einsum(
                "htk,khd->thd", scores_rounded, key_block, preferred_element_type=jnp.float32
            )
            return (query_grad, None)

        block_ids = jnp.arange(row_count // block, dtype=jnp.int32)
        return lax.scan(key_advance, carry_state, (key_blocks, value_blocks, block_ids))[0]

    query_grad = key_fold(
        zero_grads,
        (
            lax.all_gather(key_normed, "ctx", axis=0, tiled=True),
            lax.all_gather(value_proj, "ctx", axis=0, tiled=True),
        ),
    )
    inverse_root = HD ** (-0.5)
    query_normed_grad = (query_grad * inverse_root).reshape(token_count, local_width)
    key_normed_grad = (key_grad * inverse_root).reshape(token_count, local_width)
    grad_value = value_grad.reshape(token_count, local_width).astype(jnp.bfloat16)
    query_unit_grad = query_normed_grad * query_gain
    key_unit_grad = key_normed_grad * key_gain
    query_mean_terms, key_mean_terms = lax.psum(
        (jnp.sum(query_unit_grad * query_unit, axis=1), jnp.sum(key_unit_grad * key_unit, axis=1)),
        "tp",
    )
    grad_query = finish_norm(query_inverse, query_unit, query_unit_grad, query_mean_terms)
    grad_key = finish_norm(key_inverse, key_unit, key_unit_grad, key_mean_terms)
    grad_query_gain, grad_key_gain = lax.psum(
        (
            jnp.sum(query_normed_grad * query_unit, axis=0),
            jnp.sum(key_normed_grad * key_unit, axis=0),
        ),
        "ctx",
    )
    return (grad_query, grad_key, grad_value, grad_query_gain, grad_key_gain)


def solution(mesh):
    placed = (P("ctx", "tp"), P("ctx", "tp"), P("ctx", "tp"), P("tp"), P("tp"), P(), P("ctx", "tp"))
    return jax.shard_map(
        per_device,
        mesh=mesh,
        in_specs=placed,
        out_specs=(P("ctx", "tp"), P("ctx", "tp"), P("ctx", "tp"), P("tp"), P("tp")),
        check_vma=False,
    )
```

profile of v0, /device:TPU:0, one launch (start us, length us, event | category | flops | bytes accessed | tf_op | source)
XLA Modules:
  0.0 262.4 jit_solution(12094747030671629026)
XLA Ops:
  8.7 18.1 %all-reduce.1 = (f32[384]{0:T(512)S(1)}, f32[384]{0:T(512)S(1)}) all-reduce(f32[384]{0:T(512)S(1)} %get-tuple-element.782, f32[384]{0:T(512)S(1)} %get-tuple-element.781), channel_id=1, replica_groups=mesh['ctx'=4,'tp'=8] {'tp'}, use_global_device_ids=true, to_apply=%region_3.0 | all-reduce | flops 768 | bytes 6144 | tf_op jit(solution)/shard_map/psum | solution.py:52
  37.1 20.9 %all-gather.5.cloned.1.call-done = bf16[1536,512]{1,0:T(8,128)(2,1)} async-done(((bf16[384,512]{1,0:T(8,128)(2,1)}), bf16[1536,512]{1,0:T(8,128)(2,1)}) %all-gather.5.cloned.1.call-update) | async-done | bytes 1572880 | tf_op jit(solution)/shard_map/all_gather | solution.py:170
  61.7 28.9 %all-gather.7.cloned.1.call-done = bf16[1536,512]{1,0:T(8,128)(2,1)} async-done(((bf16[384,512]{1,0:T(8,128)(2,1)}), bf16[1536,512]{1,0:T(8,128)(2,1)}) %all-gather.7.cloned.1.call-update) | async-done | bytes 1572880 | tf_op jit(solution)/shard_map/all_gather | solution.py:171
  95.1 28.7 %while.45 = (s32[]{:T(128)}, f32[4,384]{1,0:T(4,128)S(1)}, f32[4,384]{1,0:T(4,128)}, f32[4,384]{1,0:T(4,128)}, s32[3]{0:T(128)}, /*index=5*/s32[8]{0:T(128)}, s3...) while((s32[]{:T(128)}, f32[4,384]{1,0:T(4,128)S(1)}, ...), condition=%wide.region_10.11_spmd.clone, body=%wide.region_5.10_spmd.clone.sunk | while | flops 412318720 | bytes 13854600 | solution.py:95
  125.6 27.2 %while.46 = (s32[]{:T(128)}, f32[384,4,128]{0,2,1:T(8,128)}, bf16[3,512,4,128]{3,1,2,0:T(8,128)(2,1)}, s32[3]{0:T(128)}, s32[8]{0:T(128)}, /*index=5*/s32[384]{0...) while((s32[]{:T(128)}, f32[384,4,128]{0,2,1:T(8,128)}, ...), condition=%wide.region_13.14_spmd.clone, body=%wide.region_11.13_spmd.clone.sunk | while | flops 609309184 | bytes 10669378 | solution.py:165
  130.8 3.7 %fusion.148 = f32[384,4,128]{0,2,1:T(8,128)} fusion(f32[4,512,384]{2,1,0:T(8,128)S(1)} %fusion.146, bf16[384,4,128]{2,0,1:T(8,128)(2,1)} %get-tuple-element.1085, f32[4,384]{1,0:T(4,128)S(1)} %get-tuple-element.1086, f32[4,384]{1,0:T(4,128)S(1)} %copy-done.28, pred[384,512]{0,1:T(8,128)(4,1)} %broadcast_compare_fusion.7, ...), kind=kOutput, calls=%fused_computation.39.clone.1 | convolution fusion | flops 407764992 | bytes 6370816 | tf_op jit(solution)/shard_map/while/body/eval_jaxpr/htk,khd->thd/dot_general | solution.py:159
  139.7 4.0 %fusion.148 = f32[384,4,128]{0,2,1:T(8,128)} fusion(f32[4,512,384]{2,1,0:T(8,128)S(1)} %fusion.146, bf16[384,4,128]{2,0,1:T(8,128)(2,1)} %get-tuple-element.1085, f32[4,384]{1,0:T(4,128)S(1)} %get-tuple-element.1086, f32[4,384]{1,0:T(4,128)S(1)} %copy-done.28, pred[384,512]{0,1:T(8,128)(4,1)} %broadcast_compare_fusion.7, ...), kind=kOutput, calls=%fused_computation.39.clone.1 | convolution fusion | flops 407764992 | bytes 6370816 | tf_op jit(solution)/shard_map/while/body/eval_jaxpr/htk,khd->thd/dot_general | solution.py:159
  148.9 4.0 %fusion.148 = f32[384,4,128]{0,2,1:T(8,128)} fusion(f32[4,512,384]{2,1,0:T(8,128)S(1)} %fusion.146, bf16[384,4,128]{2,0,1:T(8,128)(2,1)} %get-tuple-element.1085, f32[4,384]{1,0:T(4,128)S(1)} %get-tuple-element.1086, f32[4,384]{1,0:T(4,128)S(1)} %copy-done.28, pred[384,512]{0,1:T(8,128)(4,1)} %broadcast_compare_fusion.7, ...), kind=kOutput, calls=%fused_computation.39.clone.1 | convolution fusion | flops 407764992 | bytes 6370816 | tf_op jit(solution)/shard_map/while/body/eval_jaxpr/htk,khd->thd/dot_general | solution.py:159
  154.4 3.8 %reshape.244 = bf16[3,512,4,128]{3,2,1,0:T(4,128)(2,1)} reshape(bf16[1536,512]{1,0:T(8,128)(2,1)} %all-gather.9.cloned.1.call-done) | data formatting | bytes 3145728 | tf_op jit(solution)/shard_map/reshape | solution.py:110
  158.2 8.8 %all_gather.23 = f32[4,1536]{1,0:T(4,128)} all-gather(f32[4,384]{1,0:T(4,128)S(1)} %copy-done.29), channel_id=1, replica_groups=mesh['ctx'=4,'tp'=8] {'ctx'}, dimensions={1}, use_global_device_ids=true | all-gather | bytes 30720 | tf_op jit(solution)/shard_map/all_gather | solution.py:102
  167.0 8.1 %all_gather.25 = f32[4,1536]{1,0:T(4,128)} all-gather(f32[4,384]{1,0:T(4,128)S(1)} %get-tuple-element.1158), channel_id=1, replica_groups=mesh['ctx'=4,'tp'=8] {'ctx'}, dimensions={1}, use_global_device_ids=true | all-gather | bytes 30720 | tf_op jit(solution)/shard_map/all_gather | solution.py:103
  176.1 3.5 %reshape.246 = bf16[3,512,4,128]{3,2,1,0:T(4,128)(2,1)} reshape(bf16[1536,512]{1,0:T(8,128)(2,1)} %all-gather.11.cloned.1.call-done) | data formatting | bytes 3145728 | tf_op jit(solution)/shard_map/reshape | solution.py:111
  180.1 47.7 %while.47 = (s32[]{:T(128)}, f32[384,4,128]{0,2,1:T(8,128)}, f32[384,4,128]{0,2,1:T(8,128)}, bf16[3,512,4,128]{3,2,1,0:T(4,128)(2,1)}, s32[384]{0:T(512)}, /*ind...) while((s32[]{:T(128)}, f32[384,4,128]{0,2,1:T(8,128)}, ...), condition=%wide.region_18.19_spmd.clone, body=%wide.region_16.18_spmd.clone.sunk | while | flops 814174720 | bytes 20322092 | solution.py:135
  180.1 2.4 constant_dynamic-slice_fusion.6
  188.7 3.9 %fusion.154 = f32[384,4,128]{0,2,1:T(8,128)} fusion(f32[4,512,384]{2,1,0:T(8,128)S(1)} %fusion.152, bf16[384,4,128]{2,0,1:T(8,128)(2,1)} %get-tuple-element.1132, f32[4,512]{1,0:T(4,128)S(1)} %get-tuple-element.1003, f32[4,512]{1,0:T(4,128)S(1)} %get-tuple-element.1004, pred[512,384]{1,0:T(8,128)(4,1)} %broadcast_compare_fusion.8, ...), kind=kOutput, calls=%fused_computation.76.clone.1 | convolution fusion | flops 407764992 | bytes 6373377 | tf_op jit(solution)/shard_map/while/body/eval_jaxpr/htk,thd->khd/dot_general | solution.py:129
  192.6 3.0 %fusion.155 = f32[384,4,128]{0,2,1:T(8,128)} fusion(f32[4,512,384]{2,1,0:T(8,128)S(1)} %fusion.152, f32[4,512]{1,0:T(4,128)S(1)} %get-tuple-element.1004, pred[512,384]{1,0:T(8,128)(4,1)} %broadcast_compare_fusion.8, f32[384,4,128]{0,2,1:T(8,128)} %get-tuple-element.1108, bf16[1,512,4,128]{3,2,1,0:T(4,128)(2,1)} %get-tuple-element.1005, ...), kind=kOutput, calls=%fused_computation.75.clone.1 | convolution fusion | flops 204865536 | bytes 5447681 | tf_op jit(solution)/shard_map/while/body/eval_jaxpr/htk,thd->khd/dot_general | solution.py:126
  195.6 2.4 constant_dynamic-slice_fusion.6
  204.3 4.1 %fusion.154 = f32[384,4,128]{0,2,1:T(8,128)} fusion(f32[4,512,384]{2,1,0:T(8,128)S(1)} %fusion.152, bf16[384,4,128]{2,0,1:T(8,128)(2,1)} %get-tuple-element.1132, f32[4,512]{1,0:T(4,128)S(1)} %get-tuple-element.1003, f32[4,512]{1,0:T(4,128)S(1)} %get-tuple-element.1004, pred[512,384]{1,0:T(8,128)(4,1)} %broadcast_compare_fusion.8, ...), kind=kOutput, calls=%fused_computation.76.clone.1 | convolution fusion | flops 407764992 | bytes 6373377 | tf_op jit(solution)/shard_map/while/body/eval_jaxpr/htk,thd->khd/dot_general | solution.py:129
  208.4 3.3 %fusion.155 = f32[384,4,128]{0,2,1:T(8,128)} fusion(f32[4,512,384]{2,1,0:T(8,128)S(1)} %fusion.152, f32[4,512]{1,0:T(4,128)S(1)} %get-tuple-element.1004, pred[512,384]{1,0:T(8,128)(4,1)} %broadcast_compare_fusion.8, f32[384,4,128]{0,2,1:T(8,128)} %get-tuple-element.1108, bf16[1,512,4,128]{3,2,1,0:T(4,128)(2,1)} %get-tuple-element.1005, ...), kind=kOutput, calls=%fused_computation.75.clone.1 | convolution fusion | flops 204865536 | bytes 5447681 | tf_op jit(solution)/shard_map/while/body/eval_jaxpr/htk,thd->khd/dot_general | solution.py:126
  211.7 2.4 constant_dynamic-slice_fusion.6
  220.3 4.1 %fusion.154 = f32[384,4,128]{0,2,1:T(8,128)} fusion(f32[4,512,384]{2,1,0:T(8,128)S(1)} %fusion.152, bf16[384,4,128]{2,0,1:T(8,128)(2,1)} %get-tuple-element.1132, f32[4,512]{1,0:T(4,128)S(1)} %get-tuple-element.1003, f32[4,512]{1,0:T(4,128)S(1)} %get-tuple-element.1004, pred[512,384]{1,0:T(8,128)(4,1)} %broadcast_compare_fusion.8, ...), kind=kOutput, calls=%fused_computation.76.clone.1 | convolution fusion | flops 407764992 | bytes 6373377 | tf_op jit(solution)/shard_map/while/body/eval_jaxpr/htk,thd->khd/dot_general | solution.py:129
  224.4 3.3 %fusion.155 = f32[384,4,128]{0,2,1:T(8,128)} fusion(f32[4,512,384]{2,1,0:T(8,128)S(1)} %fusion.152, f32[4,512]{1,0:T(4,128)S(1)} %get-tuple-element.1004, pred[512,384]{1,0:T(8,128)(4,1)} %broadcast_compare_fusion.8, f32[384,4,128]{0,2,1:T(8,128)} %get-tuple-element.1108, bf16[1,512,4,128]{3,2,1,0:T(4,128)(2,1)} %get-tuple-element.1005, ...), kind=kOutput, calls=%fused_computation.75.clone.1 | convolution fusion | flops 204865536 | bytes 5447681 | tf_op jit(solution)/shard_map/while/body/eval_jaxpr/htk,thd->khd/dot_general | solution.py:126
  229.8 13.6 %all-reduce = (f32[384]{0:T(512)S(1)}, f32[384]{0:T(512)S(1)}) all-reduce(f32[384]{0:T(512)S(1)} %copy-done.31, f32[384]{0:T(512)S(1)} %get-tuple-element.694), channel_id=1, replica_groups=mesh['ctx'=4,'tp'=8] {'tp'}, use_global_device_ids=true, to_apply=%region_15.16 | all-reduce | flops 768 | bytes 6144 | tf_op jit(solution)/shard_map/psum | solution.py:180
  246.4 9.5 %all-reduce.2 = (f32[512]{0:T(512)}, f32[512]{0:T(512)}) all-reduce(f32[512]{0:T(512)S(1)} %copy-done.30, f32[512]{0:T(512)S(1)} %get-tuple-element.693), channel_id=1, replica_groups=mesh['ctx'=4,'tp'=8] {'ctx'}, use_global_device_ids=true, to_apply=%region_22.23 | all-reduce | flops 1024 | bytes 8192 | tf_op jit(solution)/shard_map/psum | solution.py:186
  (224 shorter events, 86.3 us)
Async XLA Ops:
  7.2 25.0 %copy-start.4 = (bf16[384,512]{1,0:T(8,128)(2,1)S(1)}, bf16[384,512]{1,0:T(8,128)(2,1)}, u32[]{:S(2)}) copy-start(bf16[384,512]{1,0:T(8,128)(2,1)} %param.13) | copy-start | bytes 1179652
  7.2 25.4 %copy-start.7 = (bf16[384,512]{1,0:T(8,128)(2,1)S(1)}, bf16[384,512]{1,0:T(8,128)(2,1)}, u32[]{:S(2)}) copy-start(bf16[384,512]{1,0:T(8,128)(2,1)} %param.14) | copy-start | bytes 1179652
  7.2 25.4 %copy-start.26 = (f32[512]{0:T(512)S(1)}, f32[512]{0:T(512)}, u32[]{:S(2)}) copy-start(f32[512]{0:T(512)} %param.17) | copy-start | bytes 6148
  7.2 24.9 %copy-start.23 = (f32[512]{0:T(512)S(1)}, f32[512]{0:T(512)}, u32[]{:S(2)}) copy-start(f32[512]{0:T(512)} %param.16) | copy-start | bytes 6148
  7.2 25.1 %copy-start.12 = (bf16[384,512]{1,0:T(8,128)(2,1)S(1)}, bf16[384,512]{1,0:T(8,128)(2,1)}, u32[]{:S(2)}) copy-start(bf16[384,512]{1,0:T(8,128)(2,1)} %param.19) | copy-start | bytes 1179652
  7.2 26.3 %copy-start.11 = (bf16[384,512]{1,0:T(8,128)(2,1)S(1)}, bf16[384,512]{1,0:T(8,128)(2,1)}, u32[]{:S(2)}) copy-start(bf16[384,512]{1,0:T(8,128)(2,1)} %param.15) | copy-start | bytes 1179652
  7.2 50.7 %all-gather.5.cloned.1.call-start = ((), (), s32[]{:S(2)}) async-start(), calls=%async_computation | async-start | bytes 1966080 | tf_op jit(solution)/shard_map/all_gather | solution.py:170
  26.8 7.0 %copy-start.18 = (f32[384]{0:T(512)}, f32[384]{0:T(512)S(1)}, u32[]{:S(2)}) copy-start(f32[384]{0:T(512)S(1)} %add_rsqrt_fusion) | copy-start | bytes 4612
  28.8 61.9 %all-gather.7.cloned.1.call-start = ((), (), s32[]{:S(2)}) async-start(), calls=%async_computation.1 | async-start | bytes 1966080 | tf_op jit(solution)/shard_map/all_gather | solution.py:171
  29.5 124.9 %all-gather.9.cloned.1.call-start = ((), (), s32[]{:S(2)}) async-start(), calls=%async_computation.2 | async-start | bytes 1966080 | tf_op jit(solution)/shard_map/all_gather | solution.py:140
  29.6 7.5 %copy-start.20 = (f32[384]{0:T(512)}, f32[384]{0:T(512)S(1)}, u32[]{:S(2)}) copy-start(f32[384]{0:T(512)S(1)} %add_rsqrt_fusion.1) | copy-start | bytes 4612
  31.5 144.5 %all-gather.11.cloned.1.call-start = ((), (), s32[]{:S(2)}) async-start(), calls=%async_computation.3 | async-start | bytes 1966080 | tf_op jit(solution)/shard_map/all_gather | solution.py:141
  152.8 5.4 %copy-start.29 = (f32[4,384]{1,0:T(4,128)S(1)}, f32[4,384]{1,0:T(4,128)}, u32[]{:S(2)}) copy-start(f32[4,384]{1,0:T(4,128)} %get-tuple-element.1159) | copy-start | bytes 18436
  152.8 22.2 %copy-start.5 = (bf16[384,512]{1,0:T(8,128)(2,1)S(1)}, bf16[384,512]{1,0:T(8,128)(2,1)}, u32[]{:S(2)}) copy-start(bf16[384,512]{1,0:T(8,128)(2,1)} %param.13) | copy-start | bytes 1179652
  152.8 22.3 %copy-start.21 = (f32[384]{0:T(512)S(1)}, f32[384]{0:T(512)}, u32[]{:S(2)}) copy-start(f32[384]{0:T(512)} %copy-done.20) | copy-start | bytes 4612
  152.8 22.3 %copy-start.24 = (f32[512]{0:T(512)S(1)}, f32[512]{0:T(512)}, u32[]{:S(2)}) copy-start(f32[512]{0:T(512)} %param.16) | copy-start | bytes 6148
  154.4 25.2 %copy-start.9 = (f32[384,512]{1,0:T(8,128)}, f32[384,512]{1,0:T(8,128)S(1)}, u32[]{:S(2)}) copy-start(f32[384,512]{1,0:T(8,128)S(1)} %copy.74) | copy-start | bytes 2359300
  154.4 25.7 %copy-start.3 = (bf16[384,4,128]{2,0,1:T(8,128)(2,1)S(1)}, bf16[384,4,128]{2,0,1:T(8,128)(2,1)}, u32[]{:S(2)}) copy-start(bf16[384,4,128]{2,0,1:T(8,128)(2,1)} %copy_bitcast_fusion.7) | copy-start | bytes 1179652
  227.8 15.7 %copy-start.6 = (bf16[384,512]{1,0:T(8,128)(2,1)S(1)}, bf16[384,512]{1,0:T(8,128)(2,1)}, u32[]{:S(2)}) copy-start(bf16[384,512]{1,0:T(8,128)(2,1)} %param.13) | copy-start | bytes 1179652
  227.8 15.7 %copy-start.10 = (f32[384,512]{1,0:T(8,128)S(1)}, f32[384,512]{1,0:T(8,128)}, u32[]{:S(2)}) copy-start(f32[384,512]{1,0:T(8,128)} %copy-done.9) | copy-start | bytes 2359300
  227.8 15.7 %copy-start.22 = (f32[384]{0:T(512)S(1)}, f32[384]{0:T(512)}, u32[]{:S(2)}) copy-start(f32[384]{0:T(512)} %copy-done.20) | copy-start | bytes 4612
  227.8 15.7 %copy-start.25 = (f32[512]{0:T(512)S(1)}, f32[512]{0:T(512)}, u32[]{:S(2)}) copy-start(f32[512]{0:T(512)} %param.16) | copy-start | bytes 6148
  229.4 16.0 %copy-start.13 = (f32[384,4,128]{0,2,1:T(8,128)S(1)}, f32[384,4,128]{0,2,1:T(8,128)}, u32[]{:S(2)}) copy-start(f32[384,4,128]{0,2,1:T(8,128)} %get-tuple-element.445) | copy-start | bytes 2359300
  229.4 17.0 %copy-start.30 = (f32[512]{0:T(512)S(1)}, f32[512]{0:T(512)}, u32[]{:S(2)}) copy-start(f32[512]{0:T(512)} %get-tuple-element.695) | copy-start | bytes 6148
  (31 other events, 46.6 us)
Sparse Core Ops, SparseCore 0:
  28.9 29.0 all-gather.4
  59.8 30.8 all-gather.6
  93.1 30.8 all-gather.8
  125.7 30.8 all-gather.10
where the time goes:
time: 264 us; the launch traced here: 262 us
  blocking collectives  58 us (22%)
  matrix products  51.9 us (20%)
  waiting for transfers between devices  51.1 us (19%)
  local copies, waits for them, and re-layouts  45 us (17%)
  other arithmetic  35.8 us (14%)
  between operations  14.2 us (5%)
  loops' own time  6.3 us (2%)
    all_gather x1, waiting for transfers between devices, per_device(): lax.all_gather(value_proj, 'ctx', axis=0, tiled=True)  28.9 us
    all_gather x1, waiting for transfers between devices, per_device(): lax.all_gather(key_normed, 'ctx', axis=0, tiled=True)  20.9 us
    psum x1, blocking collectives, per_device(): lax.psum((jnp.sum(query_rows * query_rows, axis=1), jnp.sum(key_rows * ke...  18.1 us
    dynamic_slice x12, local copies, waits for them, and re-layouts, per_device(): lax.scan(forward_advance, (start_best, zero_rows, zero_rows), (key_blocks...  16.3 us
    psum x1, blocking collectives, per_device(): lax.psum((jnp.sum(query_unit_grad * query_unit, axis=1), jnp.sum(key_unit...  13.6 us
    dot_general x3, matrix products, query_advance(): jnp.einsum('htk,thd->khd', scores_rounded, query_block, preferred_element...  12.1 us
    dot_general x9, matrix products, block_scores(): jnp.einsum('thd,khd->htk', query_heads, key_heads, preferred_element_type...  11.7 us
    le x9, other arithmetic, block_scores(): visible = key_places[None, :] <= query_places[:, None]  11.7 us
  transfers between devices with their start and end apart: 4, of which 2 were waited for; matrix products, arithmetic and copies ran while one was open for 27% of the time, Pallas kernels for 0%

commit v1 on v0

--- a/solution.py
+++ b/solution.py
@@ -1,15 +1,250 @@
+import functools
 import math
 
 import jax
 import jax.numpy as jnp
 from jax import lax
+from jax.experimental import pallas as pl
+from jax.experimental.pallas import tpu as pltpu
 from jax.sharding import PartitionSpec as P
 
 HD = 128
-D = 4096
-
-
 EPSILON = 1e-06
+VMEM = pl.BlockSpec(memory_space=pltpu.VMEM)
+SMEM = pl.BlockSpec(memory_space=pltpu.SMEM)
+ROWS_BY_ROWS = (((1,), (1,)), ((), ()))
+COLUMNS_BY_COLUMNS = (((0,), (0,)), ((), ()))
+
+
+def head_columns(head):
+    return pl.ds(pl.multiple_of(head * HD, HD), HD)
+
+
+def down_rows(row_vector):
+    return jnp.broadcast_to(row_vector, (HD, row_vector.shape[1])).T
+
+
+def lane_folded(squares):
+    total = squares[:, :HD]
+    for start in range(HD, squares.shape[1], HD):
+        total = total + squares[:, start : start + HD]
+    return total
+
+
+def cut_kernel(peers, query_ref, key_ref, value_ref, grad_ref, *out_refs):
+    device = lax.axis_index("ctx")
+    for mask in range(peers):
+        columns = head_columns(device ^ mask)
+        out_refs[mask][0] = value_ref[:, columns]
+        out_refs[mask][1] = grad_ref[:, columns]
+    for row, ref in enumerate((query_ref, key_ref)):
+        rows = ref[...].astype(jnp.float32)
+        folded = lane_folded(rows * rows)
+        out_refs[peers][row : row + 1, :] = jnp.sum(folded.T, axis=0, keepdims=True)
+
+
+def normalize_kernel(peers, width, squares_ref, query_ref, key_ref, query_gain_ref, key_gain_ref, *out_refs):
+    device = lax.axis_index("ctx")
+    inverse = lax.rsqrt(squares_ref[...] / width + EPSILON)
+    sides = ((query_ref, query_gain_ref), (key_ref, key_gain_ref))
+    for side, (ref, gain_ref) in enumerate(sides):
+        scale = down_rows(inverse[side : side + 1, :])
+        for mask in range(peers):
+            columns = head_columns(device ^ mask)
+            unit = ref[:, columns].astype(jnp.float32) * scale
+            out_refs[mask][side] = (unit * gain_ref[:, columns]).astype(jnp.bfloat16)
+
+
+def attend_kernel(peers, block, stripe_ref, *refs):
+    normed_refs, plain_refs = refs[:peers], refs[peers : 2 * peers]
+    grads_refs, sums_refs = refs[2 * peers : 3 * peers], refs[3 * peers : 4 * peers]
+    query, key, value, grad, query_grad, key_grad, value_grad, scores, grad_probs = refs[4 * peers :]
+    device = lax.axis_index("ctx")
+    rows = query.shape[0]
+    token_count = rows // peers
+    stripe = token_count // 2
+    places = []
+    for mask in range(peers):
+        for slot in range(2):
+            number = stripe_ref[2 * (device ^ mask) + slot]
+            places.append((mask, slot, pl.ds(pl.multiple_of(number * stripe, stripe), stripe)))
+    for mask, slot, place in places:
+        local = slice(slot * stripe, (slot + 1) * stripe)
+        query[place, :] = normed_refs[mask][0, local, :]
+        key[place, :] = normed_refs[mask][1, local, :]
+        value[place, :] = plain_refs[mask][0, local, :]
+        grad[place, :] = plain_refs[mask][1, local, :]
+    inverse_root = HD ** (-0.5)
+    exponent_scale = inverse_root * math.log2(math.e)
+    count = rows // block
+    visible = lax.broadcasted_iota(jnp.int32, (block, block), 0) <= lax.broadcasted_iota(
+        jnp.int32, (block, block), 1
+    )
+    for index in range(count):
+        here = slice(index * block, (index + 1) * block)
+        query_block, grad_block = query[here, :], grad[here, :]
+        best = None
+        for other in range(index + 1):
+            there = slice(other * block, (other + 1) * block)
+            tile = lax.dot_general(
+                key[there, :], query_block, ROWS_BY_ROWS, preferred_element_type=jnp.float32
+            )
+            if other == index:
+                tile = jnp.where(visible, tile, -jnp.inf)
+            scores[there, :] = tile
+            tile_best = jnp.max(tile, axis=0, keepdims=True)
+            best = tile_best if best is None else jnp.maximum(best, tile_best)
+        total = delta = None
+        for other in range(index + 1):
+            there = slice(other * block, (other + 1) * block)
+            probs = jnp.exp2((scores[there, :] - best) * exponent_scale)
+            tile = lax.dot_general(
+                value[there, :], grad_block, ROWS_BY_ROWS, preferred_element_type=jnp.float32
+            )
+            scores[there, :] = probs
+            grad_probs[there, :] = tile
+            tile_total = jnp.sum(probs, axis=0, keepdims=True)
+            tile_delta = jnp.sum(probs * tile, axis=0, keepdims=True)
+            total = tile_total if total is None else total + tile_total
+            delta = tile_delta if delta is None else delta + tile_delta
+        inverse_total = 1.0 / total
+        delta = delta * inverse_total
+        query_sum = None
+        for other in range(index + 1):
+            there = slice(other * block, (other + 1) * block)
+            probs = scores[there, :] * inverse_total
+            scores_rounded = (probs * (grad_probs[there, :] - delta)).astype(jnp.bfloat16)
+            value_part = jnp.dot(
+                probs.astype(jnp.bfloat16), grad_block, preferred_element_type=jnp.float32
+            )
+            key_part = jnp.dot(scores_rounded, query_block, preferred_element_type=jnp.float32)
+            query_part = lax.dot_general(
+                scores_rounded, key[there, :], COLUMNS_BY_COLUMNS, preferred_element_type=jnp.float32
+            )
+            if other == index:
+                value_grad[there, :] = value_part
+                key_grad[there, :] = key_part
+            else:
+                value_grad[there, :] += value_part
+                key_grad[there, :] += key_part
+            query_sum = query_part if query_sum is None else query_sum + query_part
+        query_grad[here, :] = query_sum
+    gain_sums = [None, None]
+    for mask, slot, place in places:
+        local = slice(slot * stripe, (slot + 1) * stripe)
+        for side, (grad_rows, normed) in enumerate(((query_grad, query), (key_grad, key))):
+            normed_grad = grad_rows[place, :] * inverse_root
+            grads_refs[mask][side, local, :] = normed_grad.astype(jnp.bfloat16)
+            terms = normed_grad * normed[place, :].astype(jnp.float32)
+            row = 2 * side + slot
+            sums_refs[mask][row : row + 1, :] = jnp.sum(terms.T, axis=0, keepdims=True)
+            part = jnp.sum(terms, axis=0, keepdims=True)
+            gain_sums[side] = part if gain_sums[side] is None else gain_sums[side] + part
+        grads_refs[mask][2, local, :] = value_grad[place, :].astype(jnp.bfloat16)
+    for mask in range(peers):
+        for side in range(2):
+            sums_refs[mask][4 + side : 5 + side, :HD] = gain_sums[side]
+
+
+def finish_kernel(peers, width, squares_ref, means_ref, query_ref, key_ref, query_gain_ref, key_gain_ref, *refs):
+    grads_refs, sums_refs = refs[:peers], refs[peers : 2 * peers]
+    grad_query, grad_key, grad_value, query_gain_grad, key_gain_grad = refs[2 * peers :]
+    device = lax.axis_index("ctx")
+    stripe = means_ref.shape[1]
+    inverse = lax.rsqrt(squares_ref[...] / width + EPSILON)
+    sides = (
+        (query_ref, query_gain_ref, grad_query, query_gain_grad),
+        (key_ref, key_gain_ref, grad_key, key_gain_grad),
+    )
+    for side, (ref, gain_ref, out_ref, gain_out_ref) in enumerate(sides):
+        scale = down_rows(inverse[side : side + 1, :])
+        for slot in range(2):
+            local = slice(slot * stripe, (slot + 1) * stripe)
+            row = 2 * side + slot
+            mean = down_rows(means_ref[row : row + 1, :] / width)
+            for mask in range(peers):
+                columns = head_columns(device ^ mask)
+                unit = ref[local, columns].astype(jnp.float32) * scale[local]
+                unit_grad = grads_refs[mask][side, local, :].astype(jnp.float32) * gain_ref[:, columns]
+                out_ref[local, columns] = (scale[local] * (unit_grad - unit * mean)).astype(jnp.bfloat16)
+        for mask in range(peers):
+            columns = head_columns(device ^ mask)
+            gain_out_ref[:, columns] = sums_refs[mask][4 + side : 5 + side, :HD] / gain_ref[:, columns]
+    for mask in range(peers):
+        grad_value[:, head_columns(device ^ mask)] = grads_refs[mask][2]
+
+
+def swap(array, axis, size, mask):
+    return lax.ppermute(array, axis, [(index, index ^ mask) for index in range(size)])
+
+
+def sum_over(array, axis, size):
+    mask = 1
+    while mask < size:
+        array = array + swap(array, axis, size, mask)
+        mask *= 2
+    return array
+
+
+def call(kernel, name, out_shape, operands, in_specs=None, scratch_shapes=()):
+    return pl.pallas_call(
+        kernel,
+        name=name,
+        out_shape=out_shape,
+        in_specs=in_specs or [VMEM] * len(operands),
+        out_specs=[VMEM] * len(out_shape),
+        scratch_shapes=scratch_shapes,
+    )(*operands)
+
+
+def whole_heads(peers, tp_size, query_proj, key_proj, value_proj, query_gain, key_gain, stripe_of, grad_out):
+    token_count, local_width = query_proj.shape
+    width = local_width * tp_size
+    rows = token_count * peers
+    stripe = token_count // 2
+    shape = jax.ShapeDtypeStruct
+    query_gain_row, key_gain_row = query_gain[None], key_gain[None]
+    pair = shape((2, token_count, HD), jnp.bfloat16)
+    *plain, squares = call(
+        functools.partial(cut_kernel, peers),
+        "cut",
+        [pair] * peers + [shape((2, token_count), jnp.float32)],
+        (query_proj, key_proj, value_proj, grad_out),
+    )
+    plain = [plain[0]] + [swap(plain[mask], "ctx", peers, mask) for mask in range(1, peers)]
+    squares = sum_over(squares, "tp", tp_size)
+    normed = call(
+        functools.partial(normalize_kernel, peers, width),
+        "normalize",
+        [pair] * peers,
+        (squares, query_proj, key_proj, query_gain_row, key_gain_row),
+    )
+    normed = [normed[0]] + [swap(normed[mask], "ctx", peers, mask) for mask in range(1, peers)]
+    block = math.gcd(rows, 256)
+    row_block = lambda dtype: pltpu.VMEM((rows, HD), dtype)
+    outs = call(
+        functools.partial(attend_kernel, peers, block),
+        "attend",
+        [shape((3, token_count, HD), jnp.bfloat16)] * peers + [shape((8, stripe), jnp.float32)] * peers,
+        (stripe_of, *normed, *plain),
+        in_specs=[SMEM] + [VMEM] * (2 * peers),
+        scratch_shapes=[row_block(jnp.bfloat16)] * 4
+        + [row_block(jnp.float32)] * 3
+        + [pltpu.VMEM((rows, block), jnp.float32)] * 2,
+    )
+    grads, sums = outs[:peers], outs[peers:]
+    sums = [sums[0]] + [swap(sums[mask], "ctx", peers, mask) for mask in range(1, peers)]
+    grads = [grads[0]] + [swap(grads[mask], "ctx", peers, mask) for mask in range(1, peers)]
+    means = sum_over(functools.reduce(jnp.add, [part[:4] for part in sums]), "tp", tp_size)
+    whole = shape((token_count, local_width), jnp.bfloat16)
+    row = shape((1, local_width), jnp.float32)
+    grad_query, grad_key, grad_value, query_gain_grad, key_gain_grad = call(
+        functools.partial(finish_kernel, peers, width),
+        "finish",
+        [whole] * 3 + [row] * 2,
+        (squares, means, query_proj, key_proj, query_gain_row, key_gain_row, *grads, *sums),
+    )
+    return (grad_query, grad_key, grad_value, query_gain_grad[0], key_gain_grad[0])
 
 
 def row_positions(stripe_list, offset, count, stripe):
@@ -38,13 +273,14 @@
     return (probs.astype(jnp.bfloat16), grad_scores.astype(jnp.bfloat16))
 
 
-def finish_norm(inverse_norm, unit_rows, unit_grad, mean_terms):
-    return (inverse_norm * (unit_grad - unit_rows * (mean_terms / D)[:, None])).astype(jnp.bfloat16)
-
-
-def per_device(query_proj, key_proj, value_proj, query_gain, key_gain, stripe_of, grad_out):
+def finish_norm(inverse_norm, unit_rows, unit_grad, mean_rows):
+    return (inverse_norm * (unit_grad - unit_rows * mean_rows[:, None])).astype(jnp.bfloat16)
+
+
+def gathered_blocks(tp_size, query_proj, key_proj, value_proj, query_gain, key_gain, stripe_of, grad_out):
     token_count, local_width = query_proj.shape
     local_heads = local_width // HD
+    width = local_width * tp_size
     stripe = token_count // 2
     device = lax.axis_index("ctx")
     query_rows = query_proj.astype(jnp.float32)
@@ -52,8 +288,8 @@
     query_square, key_square = lax.psum(
         (jnp.sum(query_rows * query_rows, axis=1), jnp.sum(key_rows * key_rows, axis=1)), "tp"
     )
-    query_inverse = lax.rsqrt(query_square / D + EPSILON)[:, None]
-    key_inverse = lax.rsqrt(key_square / D + EPSILON)[:, None]
+    query_inverse = lax.rsqrt(query_square / width + EPSILON)[:, None]
+    key_inverse = lax.rsqrt(key_square / width + EPSILON)[:, None]
     query_unit = query_rows * query_inverse
     key_unit = key_rows * key_inverse
     query_normed = (query_unit * query_gain).astype(jnp.bfloat16)
@@ -181,8 +417,8 @@
         (jnp.sum(query_unit_grad * query_unit, axis=1), jnp.sum(key_unit_grad * key_unit, axis=1)),
         "tp",
     )
-    grad_query = finish_norm(query_inverse, query_unit, query_unit_grad, query_mean_terms)
-    grad_key = finish_norm(key_inverse, key_unit, key_unit_grad, key_mean_terms)
+    grad_query = finish_norm(query_inverse, query_unit, query_unit_grad, query_mean_terms / width)
+    grad_key = finish_norm(key_inverse, key_unit, key_unit_grad, key_mean_terms / width)
     grad_query_gain, grad_key_gain = lax.psum(
         (
             jnp.sum(query_normed_grad * query_unit, axis=0),
@@ -194,6 +430,14 @@
 
 
 def solution(mesh):
+    peers, tp_size = mesh.shape["ctx"], mesh.shape["tp"]
+
+    def per_device(query_proj, *others):
+        local_heads = query_proj.shape[1] // HD
+        whole = local_heads == peers and peers & (peers - 1) == 0 and tp_size & (tp_size - 1) == 0
+        plan = functools.partial(whole_heads, peers) if whole else gathered_blocks
+        return plan(tp_size, query_proj, *others)
+
     placed = (P("ctx", "tp"), P("ctx", "tp"), P("ctx", "tp"), P("tp"), P("tp"), P(), P("ctx", "tp"))
     return jax.shard_map(
         per_device,

time: 264 us -> 74.1 us (0.28)
  blocking collectives: 58 us -> 0 us
  matrix products: 51.9 us -> 0 us
  local copies, waits for them, and re-layouts: 45 us -> 1.68 us
  other arithmetic: 35.8 us -> 1.2 us
  starting transfers between devices: 0.16 us -> 23 us
  waiting for transfers between devices: 51.1 us -> 31 us
  Pallas kernels: 0 us -> 16.2 us
  between operations: 14.2 us -> 0.77 us
  loops' own time: 6.3 us -> 0 us
    dot_general x21 -> x0, matrix products: 51.9 us -> none  [the longest x3 12.1 us: query_advance(): jnp.einsum('htk,thd->khd', scores_rounded, query_block, preferred_element...]
    all_gather x4 -> x0, waiting for transfers between devices: 49.9 us -> none  [the longest x1 28.9 us: per_device(): lax.all_gather(value_proj, 'ctx', axis=0, tiled=True)]
    psum x3 -> x0, blocking collectives: 41.2 us -> none  [the longest x1 18.1 us: per_device(): lax.psum((jnp.sum(query_rows * query_rows, axis=1), jnp.sum(key_rows * ke...]
    ppermute x0 -> x18, waiting for transfers between devices: none -> 31 us  [swap(): lax.ppermute(array, axis, [(index, index ^ mask) for index in range(size)])]
    ppermute x0 -> x18, starting transfers between devices: none -> 23 us  [swap(): lax.ppermute(array, axis, [(index, index ^ mask) for index in range(size)])]
    dynamic_slice x15 -> x0, local copies, waits for them, and re-layouts: 18.5 us -> none  [the longest x12 16.3 us: per_device(): lax.scan(forward_advance, (start_best, zero_rows, zero_rows), (key_blocks...]
    all_gather x2 -> x0, blocking collectives: 16.8 us -> none  [the longest x1 8.78 us: per_device(): lax.all_gather(log_total, 'ctx', axis=1, tiled=True)]
    pallas_call x0 -> x4, Pallas kernels: none -> 16.2 us  [call(): pl.pallas_call(kernel, name=name, out_shape=out_shape, in_specs=in_specs...]
  transfers between devices with their start and end apart: 4 -> 18, of which waited for: 2 -> 9; matrix products, arithmetic and copies ran while one was open for 27% -> 2% of each run, Pallas kernels for 0% -> 3%
where the time goes in v1:
time: 74.1 us; the launch traced here: 73.8 us
  waiting for transfers between devices  31 us (42%)
  starting transfers between devices  23 us (31%)
  Pallas kernels  16.2 us (22%)
  local copies, waits for them, and re-layouts  1.68 us (2%)
  other arithmetic  1.2 us (2%)
  between operations  0.77 us (1%)
    ppermute x18, waiting for transfers between devices, swap(): lax.ppermute(array, axis, [(index, index ^ mask) for index in range(size)])  31 us
    ppermute x18, starting transfers between devices, swap(): lax.ppermute(array, axis, [(index, index ^ mask) for index in range(size)])  23 us
    pallas_call x4, Pallas kernels, call(): pl.pallas_call(kernel, name=name, out_shape=out_shape, in_specs=in_specs...  16.2 us
    unnamed x28, local copies, waits for them, and re-layouts  1.68 us
  transfers between devices with their start and end apart: 18, of which 9 were waited for; matrix products, arithmetic and copies ran while one was open for 2% of the time, Pallas kernels for 3%

profile of v1, /device:TPU:0, one launch (start us, length us, event | category | flops | bytes accessed | tf_op | source)
XLA Modules:
  0.0 73.8 jit_solution(3145280107348375272)
XLA Ops:
  0.6 2.4 %cut.1 = (bf16[2,384,128]{2,1,0:T(8,128)(2,1)}, bf16[2,384,128]{2,1,0:T(8,128)(2,1)}, bf16[2,384,128]{2,1,0:T(8,128)(2,1)}, bf16[2,384,128]{2,1,0:T(8,128)(2,1)}, f32[2,384]{1,0:T(2,128)}) custom-call(bf16[384,512]{1,0:T(8,128)(2,1)} %query_ref.5, bf16[384,512]{1,0:T(8,128)(2,1)} %key_ref.5, bf16[384,512]{1,0:T(8,128)(2,1)} %value_ref.1, ...), custom_call_target="tpu_custom_call" | custom-call | tf_op jit(solution)/shard_map/cut/pallas_call | solution.py:190
  3.0 3.0 %collective-permute-start.6 = (bf16[2,384,128]{2,1,0:T(8,128)(2,1)}, bf16[2,384,128]{2,1,0:T(8,128)(2,1)S(1)}, u32[]{:S(2)}, u32[]{:S(2)}) collective-permute-start(bf16[2,384,128]{2,1,0:T(8,128)(2,1)} %get-tuple-element.33), channel_id=1, source_target_pairs={{0,8},{8,0},{16,24},{24,16},{1,9},{9,1},{17,25},{25,17},{2,10},{10... | collective-permute-start | bytes 589832 | tf_op jit(solution)/shard_map/ppermute | solution.py:178
  6.0 1.2 %collective-permute-done = f32[2,384]{1,0:T(2,128)S(1)} collective-permute-done((f32[2,384]{1,0:T(2,128)S(1)}, f32[2,384]{1,0:T(2,128)S(1)}, u32[]{:S(2)}, u32[]{:S(2)}) %collective-permute-start) | collective-permute-done | bytes 3104 | tf_op jit(solution)/shard_map/ppermute | solution.py:178
  7.2 1.6 %collective-permute-start.1 = (f32[2,384]{1,0:T(2,128)S(1)}, f32[2,384]{1,0:T(2,128)S(1)}, u32[]{:S(2)}, u32[]{:S(2)}) collective-permute-start(f32[2,384]{1,0:T(2,128)S(1)} %add.27), channel_id=1, source_target_pairs={{0,2},{1,3},{2,0},{3,1},{4,6},{5,7},{6,4},{7,5},{8,10},{9,11},{10,... | collective-permute-start | bytes 9224 | tf_op jit(solution)/shard_map/ppermute | solution.py:178
  8.8 2.0 %collective-permute-done.1 = f32[2,384]{1,0:T(2,128)S(1)} collective-permute-done((f32[2,384]{1,0:T(2,128)S(1)}, f32[2,384]{1,0:T(2,128)S(1)}, u32[]{:S(2)}, u32[]{:S(2)}) %collective-permute-start.1) | collective-permute-done | bytes 3104 | tf_op jit(solution)/shard_map/ppermute | solution.py:178
  10.8 2.6 %collective-permute-start.2 = (f32[2,384]{1,0:T(2,128)S(1)}, f32[2,384]{1,0:T(2,128)S(1)}, u32[]{:S(2)}, u32[]{:S(2)}) collective-permute-start(f32[2,384]{1,0:T(2,128)S(1)} %add.28), channel_id=1, source_target_pairs={{0,4},{1,5},{2,6},{3,7},{4,0},{5,1},{6,2},{7,3},{8,12},{9,13},{10,... | collective-permute-start | bytes 9224 | tf_op jit(solution)/shard_map/ppermute | solution.py:178
  13.4 1.5 %collective-permute-start.7 = (bf16[2,384,128]{2,1,0:T(8,128)(2,1)}, bf16[2,384,128]{2,1,0:T(8,128)(2,1)S(1)}, u32[]{:S(2)}, u32[]{:S(2)}) collective-permute-start(bf16[2,384,128]{2,1,0:T(8,128)(2,1)} %get-tuple-element.34), channel_id=1, source_target_pairs={{0,16},{8,24},{16,0},{24,8},{1,17},{9,25},{17,1},{25,9},{2,18},{10... | collective-permute-start | bytes 589832 | tf_op jit(solution)/shard_map/ppermute | solution.py:178
  16.1 2.3 %normalize.1 = (bf16[2,384,128]{2,1,0:T(8,128)(2,1)}, bf16[2,384,128]{2,1,0:T(8,128)(2,1)}, bf16[2,384,128]{2,1,0:T(8,128)(2,1)}, bf16[2,384,128]{2,1,0:T(8,128)(2,1)}) custom-call(f32[2,384]{1,0:T(2,128)} %add.29.squares_ref, bf16[384,512]{1,0:T(8,128)(2,1)} %query_ref.5, bf16[384,512]{1,0:T(8,128)(2,1)} %key_ref.5, f32[1,512]{1,0:T(1,128)} %bitcast.4, ...), custom_call_target="tpu_custom_call" | custom-call | tf_op jit(solution)/shard_map/normalize/pallas_call | solution.py:190
  18.4 1.3 %collective-permute-start.3 = (bf16[2,384,128]{2,1,0:T(8,128)(2,1)}, bf16[2,384,128]{2,1,0:T(8,128)(2,1)S(1)}, u32[]{:S(2)}, u32[]{:S(2)}) collective-permute-start(bf16[2,384,128]{2,1,0:T(8,128)(2,1)} %get-tuple-element.29), channel_id=1, source_target_pairs={{0,8},{8,0},{16,24},{24,16},{1,9},{9,1},{17,25},{25,17},{2,10},{10... | collective-permute-start | bytes 589832 | tf_op jit(solution)/shard_map/ppermute | solution.py:178
  19.7 1.5 %collective-permute-start.4 = (bf16[2,384,128]{2,1,0:T(8,128)(2,1)}, bf16[2,384,128]{2,1,0:T(8,128)(2,1)S(1)}, u32[]{:S(2)}, u32[]{:S(2)}) collective-permute-start(bf16[2,384,128]{2,1,0:T(8,128)(2,1)} %get-tuple-element.30), channel_id=1, source_target_pairs={{0,16},{8,24},{16,0},{24,8},{1,17},{9,25},{17,1},{25,9},{2,18},{10... | collective-permute-start | bytes 589832 | tf_op jit(solution)/shard_map/ppermute | solution.py:178
  21.9 4.7 %collective-permute-done.7.refs_6_ = bf16[2,384,128]{2,1,0:T(8,128)(2,1)S(1)} collective-permute-done((bf16[2,384,128]{2,1,0:T(8,128)(2,1)}, bf16[2,384,128]{2,1,0:T(8,128)(2,1)S(1)}, u32[]{:S(2)}, u32[]{:S(2)}) %collective-permute-start.7) | collective-permute-done | bytes 196640 | tf_op jit(solution)/shard_map/ppermute | solution.py:178
  26.6 5.4 %collective-permute-done.4.refs_2_ = bf16[2,384,128]{2,1,0:T(8,128)(2,1)S(1)} collective-permute-done((bf16[2,384,128]{2,1,0:T(8,128)(2,1)}, bf16[2,384,128]{2,1,0:T(8,128)(2,1)S(1)}, u32[]{:S(2)}, u32[]{:S(2)}) %collective-permute-start.4) | collective-permute-done | bytes 196640 | tf_op jit(solution)/shard_map/ppermute | solution.py:178
  32.8 8.6 %attend.1 = (bf16[3,384,128]{2,1,0:T(8,128)(2,1)}, bf16[3,384,128]{2,1,0:T(8,128)(2,1)}, bf16[3,384,128]{2,1,0:T(8,128)(2,1)}, bf16[3,384,128]{2,1,0:T(8,128)(2,...) custom-call(s32[8]{0:T(128)} %stripe_ref.1, ...), custom_call_target="tpu_custom_call" | custom-call | tf_op jit(solution)/shard_map/attend/pallas_call | solution.py:190
  42.2 1.5 %collective-permute-start.16 = (bf16[3,384,128]{2,1,0:T(8,128)(2,1)}, bf16[3,384,128]{2,1,0:T(8,128)(2,1)S(1)}, u32[]{:S(2)}, u32[]{:S(2)}) collective-permute-start(bf16[3,384,128]{2,1,0:T(8,128)(2,1)} %get-tuple-element.42), channel_id=1, source_target_pairs={{0,16},{8,24},{16,0},{24,8},{1,17},{9,25},{17,1},{25,9},{2,18},{10... | collective-permute-start | bytes 884744 | tf_op jit(solution)/shard_map/ppermute | solution.py:178
  43.7 1.3 %collective-permute-start.17 = (bf16[3,384,128]{2,1,0:T(8,128)(2,1)}, bf16[3,384,128]{2,1,0:T(8,128)(2,1)S(1)}, u32[]{:S(2)}, u32[]{:S(2)}) collective-permute-start(bf16[3,384,128]{2,1,0:T(8,128)(2,1)} %get-tuple-element.43), channel_id=1, source_target_pairs={{0,24},{8,16},{16,8},{24,0},{1,25},{9,17},{17,9},{25,1},{2,26},{10... | collective-permute-start | bytes 884744 | tf_op jit(solution)/shard_map/ppermute | solution.py:178
  45.7 1.5 %collective-permute-start.10 = (f32[8,192]{1,0:T(8,128)}, f32[8,192]{1,0:T(8,128)S(1)}, u32[]{:S(2)}, u32[]{:S(2)}) collective-permute-start(f32[8,192]{1,0:T(8,128)} %get-tuple-element.38), channel_id=1, source_target_pairs={{0,16},{8,24},{16,0},{24,8},{1,17},{9,25},{17,1},{25,9},{2,18},{10... | collective-permute-start | bytes 18440 | tf_op jit(solution)/shard_map/ppermute | solution.py:178
  47.2 8.0 %collective-permute-done.9.refs_5_ = f32[8,192]{1,0:T(8,128)S(1)} collective-permute-done((f32[8,192]{1,0:T(8,128)}, f32[8,192]{1,0:T(8,128)S(1)}, u32[]{:S(2)}, u32[]{:S(2)}) %collective-permute-start.9) | collective-permute-done | bytes 6176 | tf_op jit(solution)/shard_map/ppermute | solution.py:178
  55.1 2.5 %collective-permute-start.11 = (f32[8,192]{1,0:T(8,128)}, f32[8,192]{1,0:T(8,128)S(1)}, u32[]{:S(2)}, u32[]{:S(2)}) collective-permute-start(f32[8,192]{1,0:T(8,128)} %get-tuple-element.39), channel_id=1, source_target_pairs={{0,24},{8,16},{16,8},{24,0},{1,25},{9,17},{17,9},{25,1},{2,26},{10... | collective-permute-start | bytes 18440 | tf_op jit(solution)/shard_map/ppermute | solution.py:178
  57.6 2.3 %collective-permute-done.11.refs_7_ = f32[8,192]{1,0:T(8,128)S(1)} collective-permute-done((f32[8,192]{1,0:T(8,128)}, f32[8,192]{1,0:T(8,128)S(1)}, u32[]{:S(2)}, u32[]{:S(2)}) %collective-permute-start.11) | collective-permute-done | bytes 6176 | tf_op jit(solution)/shard_map/ppermute | solution.py:178
  60.0 1.2 %collective-permute-done.12 = f32[4,192]{1,0:T(4,128)S(1)} collective-permute-done((f32[4,192]{1,0:T(4,128)S(1)}, f32[4,192]{1,0:T(4,128)S(1)}, u32[]{:S(2)}, u32[]{:S(2)}) %collective-permute-start.12) | collective-permute-done | bytes 3104 | tf_op jit(solution)/shard_map/ppermute | solution.py:178
  61.2 1.6 %collective-permute-start.13 = (f32[4,192]{1,0:T(4,128)S(1)}, f32[4,192]{1,0:T(4,128)S(1)}, u32[]{:S(2)}, u32[]{:S(2)}) collective-permute-start(f32[4,192]{1,0:T(4,128)S(1)} %add.33), channel_id=1, source_target_pairs={{0,2},{1,3},{2,0},{3,1},{4,6},{5,7},{6,4},{7,5},{8,10},{9,11},{10,... | collective-permute-start | bytes 9224 | tf_op jit(solution)/shard_map/ppermute | solution.py:178
  62.7 2.0 %collective-permute-done.13 = f32[4,192]{1,0:T(4,128)S(1)} collective-permute-done((f32[4,192]{1,0:T(4,128)S(1)}, f32[4,192]{1,0:T(4,128)S(1)}, u32[]{:S(2)}, u32[]{:S(2)}) %collective-permute-start.13) | collective-permute-done | bytes 3104 | tf_op jit(solution)/shard_map/ppermute | solution.py:178
  65.1 4.2 %collective-permute-done.14 = f32[4,192]{1,0:T(4,128)S(1)} collective-permute-done((f32[4,192]{1,0:T(4,128)S(1)}, f32[4,192]{1,0:T(4,128)S(1)}, u32[]{:S(2)}, u32[]{:S(2)}) %collective-permute-start.14) | collective-permute-done | bytes 3104 | tf_op jit(solution)/shard_map/ppermute | solution.py:178
  70.8 3.0 %finish.1 = (bf16[384,512]{1,0:T(8,128)(2,1)}, bf16[384,512]{1,0:T(8,128)(2,1)}, bf16[384,512]{1,0:T(8,128)(2,1)}, f32[1,512]{1,0:T(1,128)}, f32[1,512]{1,0:T(1,128)}) custom-call(f32[2,384]{1,0:T(2,128)} %add.29.squares_ref, f32[4,192]{1,0:T(4,128)} %add.35.means_ref, bf16[384,512]{1,0:T(8,128)(2,1)} %query_ref.5, bf16[384,512]{1,0:T(8,128)(2,1)} %key_ref.5, ...), custom_call_target="tpu_custom_call" | custom-call | tf_op jit(solution)/shard_map/finish/pallas_call | solution.py:190
  (51 shorter events, 6.0 us)
Async XLA Ops:
  3.0 18.2 %collective-permute-start.6 = (bf16[2,384,128]{2,1,0:T(8,128)(2,1)}, bf16[2,384,128]{2,1,0:T(8,128)(2,1)S(1)}, u32[]{:S(2)}, u32[]{:S(2)}) collective-permute-start(bf16[2,384,128]{2,1,0:T(8,128)(2,1)} %get-tuple-element.33), channel_id=1, source_target_pairs={{0,8},{8,0},{16,24},{24,16},{1,9},{9,1},{17,25},{25,17},{2,10},{10... | collective-permute-start | bytes 589832 | tf_op jit(solution)/shard_map/ppermute | solution.py:178
  6.0 1.2 %collective-permute-start = (f32[2,384]{1,0:T(2,128)S(1)}, f32[2,384]{1,0:T(2,128)S(1)}, u32[]{:S(2)}, u32[]{:S(2)}) collective-permute-start(f32[2,384]{1,0:T(2,128)S(1)} %copy-done.13), channel_id=1, source_target_pairs={{0,1},{1,0},{2,3},{3,2},{4,5},{5,4},{6,7},{7,6},{8,9},{9,8},{10,11... | collective-permute-start | bytes 9224 | tf_op jit(solution)/shard_map/ppermute | solution.py:178
  7.2 3.6 %collective-permute-start.1 = (f32[2,384]{1,0:T(2,128)S(1)}, f32[2,384]{1,0:T(2,128)S(1)}, u32[]{:S(2)}, u32[]{:S(2)}) collective-permute-start(f32[2,384]{1,0:T(2,128)S(1)} %add.27), channel_id=1, source_target_pairs={{0,2},{1,3},{2,0},{3,1},{4,6},{5,7},{6,4},{7,5},{8,10},{9,11},{10,... | collective-permute-start | bytes 9224 | tf_op jit(solution)/shard_map/ppermute | solution.py:178
  10.8 4.7 %collective-permute-start.2 = (f32[2,384]{1,0:T(2,128)S(1)}, f32[2,384]{1,0:T(2,128)S(1)}, u32[]{:S(2)}, u32[]{:S(2)}) collective-permute-start(f32[2,384]{1,0:T(2,128)S(1)} %add.28), channel_id=1, source_target_pairs={{0,4},{1,5},{2,6},{3,7},{4,0},{5,1},{6,2},{7,3},{8,12},{9,13},{10,... | collective-permute-start | bytes 9224 | tf_op jit(solution)/shard_map/ppermute | solution.py:178
  13.4 13.2 %collective-permute-start.7 = (bf16[2,384,128]{2,1,0:T(8,128)(2,1)}, bf16[2,384,128]{2,1,0:T(8,128)(2,1)S(1)}, u32[]{:S(2)}, u32[]{:S(2)}) collective-permute-start(bf16[2,384,128]{2,1,0:T(8,128)(2,1)} %get-tuple-element.34), channel_id=1, source_target_pairs={{0,16},{8,24},{16,0},{24,8},{1,17},{9,25},{17,1},{25,9},{2,18},{10... | collective-permute-start | bytes 589832 | tf_op jit(solution)/shard_map/ppermute | solution.py:178
  14.9 11.7 %collective-permute-start.8 = (bf16[2,384,128]{2,1,0:T(8,128)(2,1)}, bf16[2,384,128]{2,1,0:T(8,128)(2,1)S(1)}, u32[]{:S(2)}, u32[]{:S(2)}) collective-permute-start(bf16[2,384,128]{2,1,0:T(8,128)(2,1)} %get-tuple-element.35), channel_id=1, source_target_pairs={{0,24},{8,16},{16,8},{24,0},{1,25},{9,17},{17,9},{25,1},{2,26},{10... | collective-permute-start | bytes 589832 | tf_op jit(solution)/shard_map/ppermute | solution.py:178
  18.4 8.3 %collective-permute-start.3 = (bf16[2,384,128]{2,1,0:T(8,128)(2,1)}, bf16[2,384,128]{2,1,0:T(8,128)(2,1)S(1)}, u32[]{:S(2)}, u32[]{:S(2)}) collective-permute-start(bf16[2,384,128]{2,1,0:T(8,128)(2,1)} %get-tuple-element.29), channel_id=1, source_target_pairs={{0,8},{8,0},{16,24},{24,16},{1,9},{9,1},{17,25},{25,17},{2,10},{10... | collective-permute-start | bytes 589832 | tf_op jit(solution)/shard_map/ppermute | solution.py:178
  19.7 12.3 %collective-permute-start.4 = (bf16[2,384,128]{2,1,0:T(8,128)(2,1)}, bf16[2,384,128]{2,1,0:T(8,128)(2,1)S(1)}, u32[]{:S(2)}, u32[]{:S(2)}) collective-permute-start(bf16[2,384,128]{2,1,0:T(8,128)(2,1)} %get-tuple-element.30), channel_id=1, source_target_pairs={{0,16},{8,24},{16,0},{24,8},{1,17},{9,25},{17,1},{25,9},{2,18},{10... | collective-permute-start | bytes 589832 | tf_op jit(solution)/shard_map/ppermute | solution.py:178
  21.2 10.8 %copy-start.3 = (bf16[2,384,128]{2,1,0:T(8,128)(2,1)}, bf16[2,384,128]{2,1,0:T(8,128)(2,1)S(1)}, u32[]{:S(2)}) copy-start(bf16[2,384,128]{2,1,0:T(8,128)(2,1)S(1)} %collective-permute-done.6.refs_5_) | copy-start | bytes 589828
  21.2 10.8 %collective-permute-start.5 = (bf16[2,384,128]{2,1,0:T(8,128)(2,1)}, bf16[2,384,128]{2,1,0:T(8,128)(2,1)S(1)}, u32[]{:S(2)}, u32[]{:S(2)}) collective-permute-start(bf16[2,384,128]{2,1,0:T(8,128)(2,1)} %get-tuple-element.31), channel_id=1, source_target_pairs={{0,24},{8,16},{16,8},{24,0},{1,25},{9,17},{17,9},{25,1},{2,26},{10... | collective-permute-start | bytes 589832 | tf_op jit(solution)/shard_map/ppermute | solution.py:178
  26.6 5.5 %copy-start.4 = (bf16[2,384,128]{2,1,0:T(8,128)(2,1)}, bf16[2,384,128]{2,1,0:T(8,128)(2,1)S(1)}, u32[]{:S(2)}) copy-start(bf16[2,384,128]{2,1,0:T(8,128)(2,1)S(1)} %collective-permute-done.7.refs_6_) | copy-start | bytes 589828
  26.6 5.5 %copy-start.5 = (bf16[2,384,128]{2,1,0:T(8,128)(2,1)}, bf16[2,384,128]{2,1,0:T(8,128)(2,1)S(1)}, u32[]{:S(2)}) copy-start(bf16[2,384,128]{2,1,0:T(8,128)(2,1)S(1)} %collective-permute-done.8.refs_7_) | copy-start | bytes 589828
  26.6 5.5 %copy-start.6 = (bf16[2,384,128]{2,1,0:T(8,128)(2,1)}, bf16[2,384,128]{2,1,0:T(8,128)(2,1)S(1)}, u32[]{:S(2)}) copy-start(bf16[2,384,128]{2,1,0:T(8,128)(2,1)S(1)} %collective-permute-done.3.refs_1_) | copy-start | bytes 589828
  41.4 18.5 %copy-start.9 = (f32[8,192]{1,0:T(8,128)S(1)}, f32[8,192]{1,0:T(8,128)}, u32[]{:S(2)}) copy-start(f32[8,192]{1,0:T(8,128)} %get-tuple-element.36.refs_4_) | copy-start | bytes 18436
  41.4 28.5 %collective-permute-start.15 = (bf16[3,384,128]{2,1,0:T(8,128)(2,1)}, bf16[3,384,128]{2,1,0:T(8,128)(2,1)S(1)}, u32[]{:S(2)}, u32[]{:S(2)}) collective-permute-start(bf16[3,384,128]{2,1,0:T(8,128)(2,1)} %get-tuple-element.41), channel_id=1, source_target_pairs={{0,8},{8,0},{16,24},{24,16},{1,9},{9,1},{17,25},{25,17},{2,10},{10... | collective-permute-start | bytes 884744 | tf_op jit(solution)/shard_map/ppermute | solution.py:178
  42.2 27.7 %collective-permute-start.16 = (bf16[3,384,128]{2,1,0:T(8,128)(2,1)}, bf16[3,384,128]{2,1,0:T(8,128)(2,1)S(1)}, u32[]{:S(2)}, u32[]{:S(2)}) collective-permute-start(bf16[3,384,128]{2,1,0:T(8,128)(2,1)} %get-tuple-element.42), channel_id=1, source_target_pairs={{0,16},{8,24},{16,0},{24,8},{1,17},{9,25},{17,1},{25,9},{2,18},{10... | collective-permute-start | bytes 884744 | tf_op jit(solution)/shard_map/ppermute | solution.py:178
  43.7 26.2 %collective-permute-start.17 = (bf16[3,384,128]{2,1,0:T(8,128)(2,1)}, bf16[3,384,128]{2,1,0:T(8,128)(2,1)S(1)}, u32[]{:S(2)}, u32[]{:S(2)}) collective-permute-start(bf16[3,384,128]{2,1,0:T(8,128)(2,1)} %get-tuple-element.43), channel_id=1, source_target_pairs={{0,24},{8,16},{16,8},{24,0},{1,25},{9,17},{17,9},{25,1},{2,26},{10... | collective-permute-start | bytes 884744 | tf_op jit(solution)/shard_map/ppermute | solution.py:178
  45.0 10.2 %collective-permute-start.9 = (f32[8,192]{1,0:T(8,128)}, f32[8,192]{1,0:T(8,128)S(1)}, u32[]{:S(2)}, u32[]{:S(2)}) collective-permute-start(f32[8,192]{1,0:T(8,128)} %get-tuple-element.37), channel_id=1, source_target_pairs={{0,8},{8,0},{16,24},{24,16},{1,9},{9,1},{17,25},{25,17},{2,10},{10... | collective-permute-start | bytes 18440 | tf_op jit(solution)/shard_map/ppermute | solution.py:178
  45.7 12.0 %collective-permute-start.10 = (f32[8,192]{1,0:T(8,128)}, f32[8,192]{1,0:T(8,128)S(1)}, u32[]{:S(2)}, u32[]{:S(2)}) collective-permute-start(f32[8,192]{1,0:T(8,128)} %get-tuple-element.38), channel_id=1, source_target_pairs={{0,16},{8,24},{16,0},{24,8},{1,17},{9,25},{17,1},{25,9},{2,18},{10... | collective-permute-start | bytes 18440 | tf_op jit(solution)/shard_map/ppermute | solution.py:178
  55.1 4.8 %collective-permute-start.11 = (f32[8,192]{1,0:T(8,128)}, f32[8,192]{1,0:T(8,128)S(1)}, u32[]{:S(2)}, u32[]{:S(2)}) collective-permute-start(f32[8,192]{1,0:T(8,128)} %get-tuple-element.39), channel_id=1, source_target_pairs={{0,24},{8,16},{16,8},{24,0},{1,25},{9,17},{17,9},{25,1},{2,26},{10... | collective-permute-start | bytes 18440 | tf_op jit(solution)/shard_map/ppermute | solution.py:178
  59.9 10.0 %copy-start.12 = (f32[8,192]{1,0:T(8,128)}, f32[8,192]{1,0:T(8,128)S(1)}, u32[]{:S(2)}) copy-start(f32[8,192]{1,0:T(8,128)S(1)} %collective-permute-done.11.refs_7_) | copy-start | bytes 18436
  59.9 1.2 %collective-permute-start.12 = (f32[4,192]{1,0:T(4,128)S(1)}, f32[4,192]{1,0:T(4,128)S(1)}, u32[]{:S(2)}, u32[]{:S(2)}) collective-permute-start(f32[4,192]{1,0:T(4,128)S(1)} %slice_add_fusion), channel_id=1, source_target_pairs={{0,1},{1,0},{2,3},{3,2},{4,5},{5,4},{6,7},{7,6},{8,9},{9,8},{10,11... | collective-permute-start | bytes 9224 | tf_op jit(solution)/shard_map/ppermute | solution.py:178
  61.2 3.6 %collective-permute-start.13 = (f32[4,192]{1,0:T(4,128)S(1)}, f32[4,192]{1,0:T(4,128)S(1)}, u32[]{:S(2)}, u32[]{:S(2)}) collective-permute-start(f32[4,192]{1,0:T(4,128)S(1)} %add.33), channel_id=1, source_target_pairs={{0,2},{1,3},{2,0},{3,1},{4,6},{5,7},{6,4},{7,5},{8,10},{9,11},{10,... | collective-permute-start | bytes 9224 | tf_op jit(solution)/shard_map/ppermute | solution.py:178
  64.8 4.5 %collective-permute-start.14 = (f32[4,192]{1,0:T(4,128)S(1)}, f32[4,192]{1,0:T(4,128)S(1)}, u32[]{:S(2)}, u32[]{:S(2)}) collective-permute-start(f32[4,192]{1,0:T(4,128)S(1)} %add.34), channel_id=1, source_target_pairs={{0,4},{1,5},{2,6},{3,7},{4,0},{5,1},{6,2},{7,3},{8,12},{9,13},{10,... | collective-permute-start | bytes 9224 | tf_op jit(solution)/shard_map/ppermute | solution.py:178
  (8 other events, 13.9 us)

commit v2 on v0

--- a/solution.py
+++ b/solution.py
@@ -1,15 +1,523 @@
+import functools
 import math
 
 import jax
 import jax.numpy as jnp
 from jax import lax
+from jax.experimental import pallas as pl
+from jax.experimental.pallas import tpu as pltpu
 from jax.sharding import PartitionSpec as P
 
 HD = 128
-D = 4096
-
-
 EPSILON = 1e-06
+VMEM = pl.BlockSpec(memory_space=pltpu.VMEM)
+SMEM = pl.BlockSpec(memory_space=pltpu.SMEM)
+HBM = pl.BlockSpec(memory_space=pltpu.HBM)
+ANY = pl.BlockSpec(memory_space=pl.ANY)
+ROWS_BY_ROWS = (((1,), (1,)), ((), ()))
+COLUMNS_BY_COLUMNS = (((0,), (0,)), ((), ()))
+
+
+def head_columns(head):
+    return pl.ds(pl.multiple_of(head * HD, HD), HD)
+
+
+def down_rows(row_vector):
+    return jnp.broadcast_to(row_vector, (HD, row_vector.shape[1])).T
+
+
+def lane_sums(rows):
+    count = rows.shape[0]
+    sums = jnp.broadcast_to(jnp.sum(rows, axis=1, keepdims=True), rows.shape)
+    pieces = []
+    for start in range(0, count, HD):
+        size = min(HD, count - start)
+        shape = (size, HD)
+        mine = lax.broadcasted_iota(jnp.int32, shape, 0) == lax.broadcasted_iota(jnp.int32, shape, 1)
+        piece = jnp.sum(jnp.where(mine, sums[start : start + size], 0.0), axis=0, keepdims=True)
+        pieces.append(piece[:, :size])
+    return jnp.concatenate(pieces, axis=1)
+
+
+def cut_kernel(peers, *refs):
+    in_refs, gain_refs, stripe_ref, refs = refs[:4], refs[4:6], refs[6], refs[7:]
+    out_refs, (squares_ref, gains_ref, numbers_ref, sems) = refs[: 2 * peers], refs[2 * peers :]
+    device = lax.axis_index("ctx")
+    loads, small_loads = [], []
+    for side, ref in enumerate(gain_refs):
+        load = pltpu.make_async_copy(ref, gains_ref.at[side : side + 1], sems.at[4 * peers + side])
+        load.start()
+        small_loads.append(load)
+    load = pltpu.make_async_copy(stripe_ref, numbers_ref, sems.at[4 * peers + 2])
+    load.start()
+    small_loads.append(load)
+    for index, ref in enumerate(in_refs):
+        for mask in range(peers):
+            load = pltpu.make_async_copy(
+                ref.at[:, head_columns(device ^ mask)],
+                out_refs[index // 2 * peers + mask].at[index % 2],
+                sems.at[index * peers + mask],
+            )
+            load.start()
+            loads.append(load)
+    for side in range(2):
+        folded = None
+        for mask in range(peers):
+            loads[side * peers + mask].wait()
+            rows = out_refs[mask][side].astype(jnp.float32)
+            folded = rows * rows if folded is None else folded + rows * rows
+        squares_ref[side : side + 1, :] = jnp.sum(folded.T, axis=0, keepdims=True)
+    for load in loads[2 * peers :] + small_loads:
+        load.wait()
+
+
+def stripe_rows(numbers_ref, device, high, stripe):
+    first, second = numbers_ref[2 * device], numbers_ref[2 * device + 1]
+    number = jnp.maximum(first, second) if high else jnp.minimum(first, second)
+    slot = jnp.where(second == number, 1, 0)
+    place = pl.ds(pl.multiple_of(number * stripe, stripe), stripe)
+    return place, pl.ds(pl.multiple_of(slot * stripe, stripe), stripe), slot
+
+
+def high_rows(place, rows):
+    return pl.ds(pl.multiple_of(place.start - rows // 2, place.size), place.size)
+
+
+def normalize_kernel(peers, width, members, numbers_ref, gains_ref, *refs):
+    parts, raw_refs = refs[:members], refs[members : members + peers]
+    low_refs, high_refs = refs[members + peers : members + 2 * peers], refs[members + 2 * peers : members + 3 * peers]
+    total_ref, scale_ref = refs[members + 3 * peers :]
+    total = parts[0][...]
+    for ref in parts[1:]:
+        total = total + ref[...]
+    total_ref[...] = total
+    inverse = lax.rsqrt(total / width + EPSILON)
+    device = lax.axis_index("ctx")
+    stripe = total.shape[1] // 2
+    for side in range(2):
+        scale_ref[side] = down_rows(inverse[side : side + 1, :])
+        for out_refs, high in ((low_refs, False), (high_refs, True)):
+            _, local, _ = stripe_rows(numbers_ref, device, high, stripe)
+            for mask in range(peers):
+                gain = gains_ref[side : side + 1, head_columns(device ^ mask)]
+                unit = raw_refs[mask][side, local, :].astype(jnp.float32) * scale_ref[side, local, :]
+                out_refs[mask][side] = (unit * gain).astype(jnp.bfloat16)
+
+
+def tile_rows(index, other, block):
+    start = (index * (index + 1) // 2 + other) * block
+    return slice(start, start + block)
+
+
+def grad_probs_kernel(peers, block, numbers_ref, *refs):
+    plain_refs, (grad, tiles_ref, value) = refs[:peers], refs[peers:]
+    rows = grad.shape[0]
+    device = lax.axis_index("ctx")
+    for mask in range(peers):
+        for high in (False, True):
+            place, local, _ = stripe_rows(numbers_ref, device ^ mask, high, rows // (2 * peers))
+            value[place, :] = plain_refs[mask][0, local, :]
+            grad[place, :] = plain_refs[mask][1, local, :]
+    for index in range(rows // block):
+        grad_block = grad[index * block : (index + 1) * block, :]
+        for other in range(index + 1):
+            tiles_ref[tile_rows(index, other, block), :] = lax.dot_general(
+                value[other * block : (other + 1) * block, :],
+                grad_block,
+                ROWS_BY_ROWS,
+                preferred_element_type=jnp.float32,
+            )
+
+
+def column_part(tile, reduce):
+    return reduce(tile.reshape(tile.shape[0] // 8, 8, tile.shape[1]), axis=0)
+
+
+def in_turn(first, second):
+    steps = [((index + 0.5) / len(part), step) for part in (first, second) for index, step in enumerate(part)]
+    for _, step in sorted(steps, key=lambda entry: entry[0]):
+        step()
+
+
+def query_blocks(block, indices, query, key, grad, grad_probs, scores, probs, grad_scores, on_query, on_key):
+    base, chunk = indices[-1], block // 2
+    exponent_scale = HD ** (-0.5) * math.log2(math.e)
+    down = lax.broadcasted_iota(jnp.int32, (chunk, block), 0)
+    across = lax.broadcasted_iota(jnp.int32, (chunk, block), 1)
+    best, total, delta = {}, {}, {}
+
+    def rows_of(index):
+        return slice(index * block, (index + 1) * block)
+
+    def merge(table, index, part, join):
+        table[index] = join(table[index], part) if index in table else part
+
+    def score_steps(index):
+        held = scores.at[index % 2]
+
+        def step(start):
+            tile = lax.dot_general(
+                key[start : start + chunk, :],
+                query[rows_of(index - base), :],
+                ROWS_BY_ROWS,
+                preferred_element_type=jnp.float32,
+            )
+            if start >= index * block:
+                tile = jnp.where(down + (start - index * block) <= across, tile, -jnp.inf)
+            held[start : start + chunk, :] = tile
+            merge(best, index, column_part(tile, jnp.max), jnp.maximum)
+
+        return [functools.partial(step, start) for start in range(0, (index + 1) * block, chunk)]
+
+    def softmax_steps(index):
+        held = scores.at[index % 2]
+
+        def sums_step(start):
+            if start == 0:
+                best[index] = jnp.max(best[index], axis=0, keepdims=True)
+            there = slice(start, start + chunk)
+            tile = jnp.exp2((held[there, :] - best[index]) * exponent_scale)
+            held[there, :] = tile
+            merge(total, index, column_part(tile, jnp.sum), jnp.add)
+            first = tile_rows(index, 0, block).start + start
+            merge(delta, index, column_part(tile * grad_probs[first : first + chunk, :], jnp.sum), jnp.add)
+
+        def rounding_step(start):
+            if start == 0:
+                total[index] = 1.0 / jnp.sum(total[index], axis=0, keepdims=True)
+                delta[index] = jnp.sum(delta[index], axis=0, keepdims=True) * total[index]
+            there, columns = slice(start, start + chunk), rows_of(index - base)
+            tile = held[there, :] * total[index]
+            probs[there, columns] = tile.astype(jnp.bfloat16)
+            first = tile_rows(index, 0, block).start + start
+            tile = tile * (grad_probs[first : first + chunk, :] - delta[index])
+            grad_scores[there, columns] = tile.astype(jnp.bfloat16)
+
+        starts = range(0, (index + 1) * block, chunk)
+        return [functools.partial(step, start) for step in (sums_step, rounding_step) for start in starts]
+
+    def product_steps(index):
+        def query_step():
+            seen = slice(0, (index + 1) * block)
+            on_query(
+                rows_of(index - base),
+                lax.dot_general(
+                    grad_scores[seen, rows_of(index - base)],
+                    key[seen, :],
+                    COLUMNS_BY_COLUMNS,
+                    preferred_element_type=jnp.float32,
+                ),
+            )
+
+        def key_step(other):
+            columns = slice((max(index, other) - base) * block, query.shape[0])
+            products = [
+                jnp.dot(left[rows_of(other), columns], right[columns, :], preferred_element_type=jnp.float32)
+                for left, right in ((grad_scores, query), (probs, grad))
+            ]
+            on_key(rows_of(other), *products)
+
+        final = range(index, -1, -1) if index == base else [index]
+        return [query_step] + [functools.partial(key_step, other) for other in final]
+
+    for step in score_steps(indices[0]):
+        step()
+    products = []
+    for position, index in enumerate(indices):
+        following = score_steps(indices[position + 1]) if position + 1 < len(indices) else []
+        in_turn(softmax_steps(index), products + following)
+        products = product_steps(index)
+    for step in products:
+        step()
+
+
+def low_kernel(peers, block, numbers_ref, grad, grad_probs, *refs):
+    normed_refs, refs = refs[:peers], refs[peers:]
+    query, key, query_out, key_part, value_part, sums_ref, gain_ref, query_grad, scores, probs, grad_scores = refs
+    low = query.shape[0]
+    stripe = low // peers
+    device = lax.axis_index("ctx")
+    for mask in range(peers):
+        place, _, _ = stripe_rows(numbers_ref, device ^ mask, False, stripe)
+        query[place, :] = normed_refs[mask][0]
+        key[place, :] = normed_refs[mask][1]
+
+    def on_query(rows, product):
+        normed_grad = product * HD ** (-0.5)
+        query_out[rows, :] = normed_grad.astype(jnp.bfloat16)
+        query_grad[rows, :] = normed_grad * query[rows, :].astype(jnp.float32)
+
+    def on_key(rows, key_product, value_product):
+        key_part[rows, :] = key_product
+        value_part[rows, :] = value_product
+
+    indices = range(low // block - 1, -1, -1)
+    query_blocks(
+        block, indices, query, key, grad.at[:low], grad_probs, scores, probs, grad_scores, on_query, on_key
+    )
+    gain = None
+    for mask in range(peers):
+        place, _, _ = stripe_rows(numbers_ref, device ^ mask, False, stripe)
+        terms = query_grad[place, :]
+        sums_ref[mask : mask + 1, :] = lane_sums(terms)
+        part = jnp.sum(terms, axis=0, keepdims=True)
+        gain = part if gain is None else gain + part
+    gain_ref[...] = gain
+
+
+def high_kernel(peers, block, numbers_ref, grad, grad_probs, *refs):
+    normed_refs, refs = refs[:peers], refs[peers:]
+    _, low_key, low_query_grad, low_key_part, low_value_part, low_sums, low_gain = refs[:7]
+    grads_refs, refs = refs[7 : 7 + peers], refs[7 + peers :]
+    sums_ref, gain_sums_ref, query, key, query_grad, key_grad, value_grad, scores, probs, grad_scores = refs
+    rows = key.shape[0]
+    low = rows // 2
+    stripe = low // peers
+    device = lax.axis_index("ctx")
+    key[:low, :] = low_key[...]
+    for mask in range(peers):
+        place, _, _ = stripe_rows(numbers_ref, device ^ mask, True, stripe)
+        query[high_rows(place, rows), :] = normed_refs[mask][0]
+        key[place, :] = normed_refs[mask][1]
+
+    def on_query(there, product):
+        query_grad[there, :] = product * HD ** (-0.5)
+
+    def on_key(there, key_product, value_product):
+        if there.start < low:
+            key_product = key_product + low_key_part[there, :]
+            value_product = value_product + low_value_part[there, :]
+        key_grad[there, :] = key_product * HD ** (-0.5)
+        value_grad[there, :] = value_product.astype(jnp.bfloat16)
+
+    indices = range(rows // block - 1, low // block - 1, -1)
+    query_blocks(
+        block, indices, query, key, grad.at[low:], grad_probs, scores, probs, grad_scores, on_query, on_key
+    )
+    gains, sums = [low_gain[...], None], {}
+
+    def finished(side, terms):
+        part = jnp.sum(terms, axis=0, keepdims=True)
+        gains[side] = part if gains[side] is None else gains[side] + part
+        return lane_sums(terms)
+
+    for high in (True, False):
+        for mask in range(peers):
+            place, local, _ = stripe_rows(numbers_ref, device ^ mask, high, stripe)
+            normed_grad = key_grad[place, :]
+            grads_refs[mask][1, local, :] = normed_grad.astype(jnp.bfloat16)
+            sums[mask, 1, high] = finished(1, normed_grad * key[place, :].astype(jnp.float32))
+            grads_refs[mask][2, local, :] = value_grad[place, :]
+            if high:
+                upper = high_rows(place, rows)
+                normed_grad = query_grad[upper, :]
+                grads_refs[mask][0, local, :] = normed_grad.astype(jnp.bfloat16)
+                sums[mask, 0, high] = finished(0, normed_grad * query[upper, :].astype(jnp.float32))
+            else:
+                grads_refs[mask][0, local, :] = low_query_grad[place, :]
+                sums[mask, 0, high] = low_sums[mask : mask + 1, :]
+    for mask in range(peers):
+        _, _, slot = stripe_rows(numbers_ref, device ^ mask, True, stripe)
+        for side in range(2):
+            low_row, high_row = sums[mask, side, False], sums[mask, side, True]
+            row = jnp.where(
+                slot == 1,
+                jnp.concatenate([low_row, high_row], axis=1),
+                jnp.concatenate([high_row, low_row], axis=1),
+            )
+            sums_ref[2 * mask + side : 2 * mask + side + 1, :] = row
+    for side in range(2):
+        gain_sums_ref[side : side + 1, :] = gains[side]
+
+
+def totals_kernel(peers, members, gain_sums_ref, *refs):
+    out_refs = refs[members:]
+    total = refs[0][...]
+    for ref in refs[1:members]:
+        total = total + ref[...]
+    for mask in range(peers):
+        out_refs[mask][0:2, :] = total[2 * mask : 2 * mask + 2]
+        for side in range(2):
+            out_refs[mask][2 + side : 3 + side, :HD] = gain_sums_ref[side : side + 1, :]
+
+
+def finish_kernel(peers, width, squares_ref, gains_ref, *refs):
+    raw_refs, refs = refs[:peers], refs[peers:]
+    grads_refs, sums_refs = refs[:peers], refs[peers : 2 * peers]
+    out_refs, gain_out_refs = refs[2 * peers : 2 * peers + 3], refs[2 * peers + 3 : 2 * peers + 5]
+    outs, out_sems = refs[2 * peers + 5 :]
+    device = lax.axis_index("ctx")
+    stores = []
+
+    def store(side, mask):
+        columns = head_columns(device ^ mask)
+        source = grads_refs[mask].at[2] if side == 2 else outs.at[side, mask]
+        copy = pltpu.make_async_copy(
+            source, out_refs[side].at[:, columns], out_sems.at[side * peers + mask]
+        )
+        copy.start()
+        stores.append(copy)
+
+    for mask in range(peers):
+        store(2, mask)
+    sums = sums_refs[0][...]
+    for mask in range(1, peers):
+        sums = sums + sums_refs[mask][...]
+    means = sums[0:2] / width
+    inverse = lax.rsqrt(squares_ref[...] / width + EPSILON)
+    for side in range(2):
+        scale = down_rows(inverse[side : side + 1, :])
+        drop = scale * down_rows(means[side : side + 1, :])
+        for mask in range(peers):
+            columns = head_columns(device ^ mask)
+            gain = gains_ref[side : side + 1, columns]
+            unit_grad = grads_refs[mask][side].astype(jnp.float32) * gain
+            centered = unit_grad - raw_refs[mask][side].astype(jnp.float32) * drop
+            outs[side, mask] = (scale * centered).astype(jnp.bfloat16)
+            store(side, mask)
+            gain_out_refs[side][:, columns] = sums_refs[mask][2 + side : 3 + side, :HD] / gain
+    for copy in stores:
+        copy.wait()
+
+
+def swap(array, axis, size, mask):
+    return lax.ppermute(array, axis, [(index, index ^ mask) for index in range(size)])
+
+
+def tp_parts(array, size):
+    array = array + swap(array, "tp", size, 1)
+    return [array] + [swap(array, "tp", size, mask) for mask in range(2, size, 2)]
+
+
+def to_peers(arrays, peers):
+    return [arrays[0]] + [swap(arrays[mask], "ctx", peers, mask) for mask in range(1, peers)]
+
+
+def in_hbm(array):
+    return pltpu.with_memory_space_constraint(array, pltpu.HBM)
+
+
+def call(kernel, out_shape, operands, in_specs, out_specs, scratch_shapes, vmem_mib):
+    return pl.pallas_call(
+        kernel,
+        out_shape=out_shape,
+        in_specs=in_specs,
+        out_specs=out_specs,
+        scratch_shapes=scratch_shapes,
+        compiler_params=pltpu.CompilerParams(vmem_limit_bytes=vmem_mib << 20),
+    )(*operands)
+
+
+def whole_heads(peers, tp_size, query_proj, key_proj, value_proj, query_gain, key_gain, stripe_of, grad_out):
+    token_count, local_width = query_proj.shape
+    width = local_width * tp_size
+    rows = token_count * peers
+    members = tp_size // 2
+    block = math.gcd(rows // 2, 256)
+    count = rows // block
+    tiles = count * (count + 1) // 2
+    shape, semaphores = jax.ShapeDtypeStruct, pltpu.SemaphoreType.DMA
+    head = lambda parts: shape((parts, token_count, HD), jnp.bfloat16)
+    *blocks, squares, gains, numbers = call(
+        functools.partial(cut_kernel, peers),
+        [head(2)] * (2 * peers)
+        + [
+            shape((2, token_count), jnp.float32),
+            shape((2, local_width), jnp.float32),
+            shape(stripe_of.shape, jnp.int32),
+        ],
+        [
+            in_hbm(array)
+            for array in (query_proj, key_proj, value_proj, grad_out, query_gain[None], key_gain[None], stripe_of)
+        ],
+        [HBM] * 7,
+        [VMEM] * (2 * peers + 3),
+        [semaphores((4 * peers + 3,))],
+        8,
+    )
+    raw, plain = blocks[:peers], to_peers(blocks[peers:], peers)
+    half = shape((2, token_count // 2, HD), jnp.bfloat16)
+    *normed, squares = call(
+        functools.partial(normalize_kernel, peers, width, members),
+        [half] * (2 * peers) + [shape((2, token_count), jnp.float32)],
+        (numbers, gains, *tp_parts(squares, tp_size), *raw),
+        [SMEM] + [VMEM] * (1 + members + peers),
+        [VMEM] * (2 * peers + 1),
+        [pltpu.VMEM((2, token_count, HD), jnp.float32)],
+        8,
+    )
+    low_normed = to_peers(normed[:peers], peers)
+    high_normed = to_peers(normed[peers:], peers)
+    whole_head = shape((rows, HD), jnp.bfloat16)
+    grad, grad_probs = call(
+        functools.partial(grad_probs_kernel, peers, block),
+        [whole_head, shape((tiles * block, block), jnp.float32)],
+        (numbers, *plain),
+        [SMEM] + [VMEM] * peers,
+        [VMEM] * 2,
+        [pltpu.VMEM((rows, HD), jnp.bfloat16)],
+        8,
+    )
+    low = rows // 2
+    low_head = lambda dtype: shape((low, HD), dtype)
+    scratch = lambda keys, queries: [
+        pltpu.VMEM((2, keys, block), jnp.float32),
+        pltpu.VMEM((keys, queries), jnp.bfloat16),
+        pltpu.VMEM((keys, queries), jnp.bfloat16),
+    ]
+    low_results = call(
+        functools.partial(low_kernel, peers, block),
+        [low_head(jnp.bfloat16)] * 3
+        + [low_head(jnp.float32)] * 2
+        + [shape((peers, token_count // 2), jnp.float32), shape((1, HD), jnp.float32)],
+        (numbers, grad, grad_probs, *low_normed),
+        [SMEM] + [VMEM] * (2 + peers),
+        [VMEM] * 7,
+        [pltpu.VMEM((low, HD), jnp.float32)] + scratch(low, low),
+        16,
+    )
+    *grads, sums, gain_sums = call(
+        functools.partial(high_kernel, peers, block),
+        [head(3)] * peers + [shape((2 * peers, token_count), jnp.float32), shape((2, HD), jnp.float32)],
+        (numbers, grad, grad_probs, *high_normed, *low_results),
+        [SMEM] + [VMEM] * (2 + peers + 7),
+        [VMEM] * (peers + 2),
+        [
+            pltpu.VMEM((low, HD), jnp.bfloat16),
+            pltpu.VMEM((rows, HD), jnp.bfloat16),
+            pltpu.VMEM((low, HD), jnp.float32),
+            pltpu.VMEM((rows, HD), jnp.float32),
+            pltpu.VMEM((rows, HD), jnp.bfloat16),
+        ]
+        + scratch(rows, low),
+        24,
+    )
+    grads = to_peers(grads, peers)
+    totals = call(
+        functools.partial(totals_kernel, peers, members),
+        [shape((4, token_count), jnp.float32)] * peers,
+        (gain_sums, *tp_parts(sums, tp_size)),
+        [VMEM] * (1 + members),
+        [VMEM] * peers,
+        [],
+        8,
+    )
+    totals = to_peers(totals, peers)
+    whole_out = shape((token_count, local_width), jnp.bfloat16)
+    row = shape((1, local_width), jnp.float32)
+    grad_query, grad_key, grad_value, query_gain_grad, key_gain_grad = call(
+        functools.partial(finish_kernel, peers, width),
+        [whole_out] * 3 + [row] * 2,
+        (squares, gains, *raw, *grads, *totals),
+        [VMEM] * (2 + 3 * peers),
+        [ANY] * 3 + [VMEM] * 2,
+        [
+            pltpu.VMEM((2, peers, token_count, HD), jnp.bfloat16),
+            semaphores((3 * peers,)),
+        ],
+        8,
+    )
+    return (grad_query, grad_key, grad_value, query_gain_grad[0], key_gain_grad[0])
 
 
 def row_positions(stripe_list, offset, count, stripe):
@@ -38,13 +546,14 @@
     return (probs.astype(jnp.bfloat16), grad_scores.astype(jnp.bfloat16))
 
 
-def finish_norm(inverse_norm, unit_rows, unit_grad, mean_terms):
-    return (inverse_norm * (unit_grad - unit_rows * (mean_terms / D)[:, None])).astype(jnp.bfloat16)
-
-
-def per_device(query_proj, key_proj, value_proj, query_gain, key_gain, stripe_of, grad_out):
+def finish_norm(inverse_norm, unit_rows, unit_grad, mean_rows):
+    return (inverse_norm * (unit_grad - unit_rows * mean_rows[:, None])).astype(jnp.bfloat16)
+
+
+def gathered_blocks(tp_size, query_proj, key_proj, value_proj, query_gain, key_gain, stripe_of, grad_out):
     token_count, local_width = query_proj.shape
     local_heads = local_width // HD
+    width = local_width * tp_size
     stripe = token_count // 2
     device = lax.axis_index("ctx")
     query_rows = query_proj.astype(jnp.float32)
@@ -52,8 +561,8 @@
     query_square, key_square = lax.psum(
         (jnp.sum(query_rows * query_rows, axis=1), jnp.sum(key_rows * key_rows, axis=1)), "tp"
     )
-    query_inverse = lax.rsqrt(query_square / D + EPSILON)[:, None]
-    key_inverse = lax.rsqrt(key_square / D + EPSILON)[:, None]
+    query_inverse = lax.rsqrt(query_square / width + EPSILON)[:, None]
+    key_inverse = lax.rsqrt(key_square / width + EPSILON)[:, None]
     query_unit = query_rows * query_inverse
     key_unit = key_rows * key_inverse
     query_normed = (query_unit * query_gain).astype(jnp.bfloat16)
@@ -155,7 +664,7 @@
             scores, grad_probs = block_scores(
                 query_heads, grad_heads, query_places, key_block, value_block, key_places
             )
-            probs_rounded, scores_rounded = block_weights(scores, grad_probs, log_total, row_delta)
+            _, scores_rounded = block_weights(scores, grad_probs, log_total, row_delta)
             query_grad = query_grad + jnp.einsum(
                 "htk,khd->thd", scores_rounded, key_block, preferred_element_type=jnp.float32
             )
@@ -181,8 +690,8 @@
         (jnp.sum(query_unit_grad * query_unit, axis=1), jnp.sum(key_unit_grad * key_unit, axis=1)),
         "tp",
     )
-    grad_query = finish_norm(query_inverse, query_unit, query_unit_grad, query_mean_terms)
-    grad_key = finish_norm(key_inverse, key_unit, key_unit_grad, key_mean_terms)
+    grad_query = finish_norm(query_inverse, query_unit, query_unit_grad, query_mean_terms / width)
+    grad_key = finish_norm(key_inverse, key_unit, key_unit_grad, key_mean_terms / width)
     grad_query_gain, grad_key_gain = lax.psum(
         (
             jnp.sum(query_normed_grad * query_unit, axis=0),
@@ -194,6 +703,15 @@
 
 
 def solution(mesh):
+    peers, tp_size = mesh.shape["ctx"], mesh.shape["tp"]
+
+    def per_device(query_proj, *others):
+        local_heads = query_proj.shape[1] // HD
+        whole = local_heads == peers and peers & (peers - 1) == 0 and tp_size & (tp_size - 1) == 0
+        if not whole:
+            return gathered_blocks(tp_size, query_proj, *others)
+        return whole_heads(peers, tp_size, query_proj, *others)
+
     placed = (P("ctx", "tp"), P("ctx", "tp"), P("ctx", "tp"), P("tp"), P("tp"), P(), P("ctx", "tp"))
     return jax.shard_map(
         per_device,

time: 264 us -> 62 us (0.23)
  blocking collectives: 58 us -> 0 us
  matrix products: 51.9 us -> 0 us
  local copies, waits for them, and re-layouts: 45 us -> 0 us
  other arithmetic: 35.8 us -> 0.01 us
  waiting for transfers between devices: 51.1 us -> 18.6 us
  starting transfers between devices: 0.16 us -> 29.8 us
  between operations: 14.2 us -> 0.73 us
  Pallas kernels: 0 us -> 12.7 us
  loops' own time: 6.3 us -> 0 us
    dot_general x21 -> x0, matrix products: 51.9 us -> none  [the longest x3 12.1 us: query_advance(): jnp.einsum('htk,thd->khd', scores_rounded, query_block, preferred_element...]
    all_gather x4 -> x0, waiting for transfers between devices: 49.9 us -> none  [the longest x1 28.9 us: per_device(): lax.all_gather(value_proj, 'ctx', axis=0, tiled=True)]
    psum x3 -> x0, blocking collectives: 41.2 us -> none  [the longest x1 18.1 us: per_device(): lax.psum((jnp.sum(query_rows * query_rows, axis=1), jnp.sum(key_rows * ke...]
    ppermute x0 -> x23, starting transfers between devices: none -> 29.8 us  [swap(): lax.ppermute(array, axis, [(index, index ^ mask) for index in range(size)])]
    ppermute x0 -> x23, waiting for transfers between devices: none -> 18.6 us  [swap(): lax.ppermute(array, axis, [(index, index ^ mask) for index in range(size)])]
    dynamic_slice x15 -> x0, local copies, waits for them, and re-layouts: 18.5 us -> none  [the longest x12 16.3 us: per_device(): lax.scan(forward_advance, (start_best, zero_rows, zero_rows), (key_blocks...]
    all_gather x2 -> x0, blocking collectives: 16.8 us -> none  [the longest x1 8.78 us: per_device(): lax.all_gather(log_total, 'ctx', axis=1, tiled=True)]
    pallas_call x0 -> x7, Pallas kernels: none -> 12.7 us  [call(): pl.pallas_call(kernel, out_shape=out_shape, in_specs=in_specs, out_specs=...]
  transfers between devices with their start and end apart: 4 -> 23, of which waited for: 2 -> 11; matrix products, arithmetic and copies ran while one was open for 27% -> 0% of each run, Pallas kernels for 0% -> 7%
where the time goes in v2:
time: 62 us; the launch traced here: 61.9 us
  starting transfers between devices  29.8 us (48%)
  waiting for transfers between devices  18.6 us (30%)
  Pallas kernels  12.7 us (20%)
  between operations  0.73 us (1%)
    ppermute x23, starting transfers between devices, swap(): lax.ppermute(array, axis, [(index, index ^ mask) for index in range(size)])  29.8 us
    ppermute x23, waiting for transfers between devices, swap(): lax.ppermute(array, axis, [(index, index ^ mask) for index in range(size)])  18.6 us
    pallas_call x7, Pallas kernels, call(): pl.pallas_call(kernel, out_shape=out_shape, in_specs=in_specs, out_specs=...  12.7 us
  transfers between devices with their start and end apart: 23, of which 11 were waited for; matrix products, arithmetic and copies ran while one was open for 0% of the time, Pallas kernels for 7%

profile of v2, /device:TPU:0, one launch (start us, length us, event | category | flops | bytes accessed | tf_op | source)
XLA Modules:
  0.0 61.9 jit_solution(5798426574862633837)
XLA Ops:
  0.6 1.7 %shard_map.110 = (bf16[2,384,128]{2,1,0:T(8,128)(2,1)S(1)}, bf16[2,384,128]{2,1,0:T(8,128)(2,1)S(1)}, bf16[2,384,128]{2,1,0:T(8,128)(2,1)S(1)}, bf16[2,384,128]{...) custom-call(bf16[384,512]{1,0:T(8,128)(2,1)} %refs_0_.1, ...), custom_call_target="tpu_custom_call" | custom-call | tf_op jit(solution)/shard_map/pallas_call | solution.py:401
  2.4 3.0 %collective-permute-start.4 = (bf16[2,384,128]{2,1,0:T(8,128)(2,1)S(1)}, bf16[2,384,128]{2,1,0:T(8,128)(2,1)S(1)}, u32[]{:S(2)}, u32[]{:S(2)}) collective-permute-start(bf16[2,384,128]{2,1,0:T(8,128)(2,1)S(1)} %get-tuple-element.58), channel_id=1, source_target_pairs={{0,8},{8,0},{16,24},{24,16},{1,9},{9,1},{17,25},{25,17},{2,10},{10... | collective-permute-start | bytes 589832 | tf_op jit(solution)/shard_map/ppermute | solution.py:384
  5.4 1.5 %collective-permute-start.5 = (bf16[2,384,128]{2,1,0:T(8,128)(2,1)S(1)}, bf16[2,384,128]{2,1,0:T(8,128)(2,1)S(1)}, u32[]{:S(2)}, u32[]{:S(2)}) collective-permute-start(bf16[2,384,128]{2,1,0:T(8,128)(2,1)S(1)} %get-tuple-element.59), channel_id=1, source_target_pairs={{0,16},{8,24},{16,0},{24,8},{1,17},{9,25},{17,1},{25,9},{2,18},{10... | collective-permute-start | bytes 589832 | tf_op jit(solution)/shard_map/ppermute | solution.py:384
  8.1 4.1 %collective-permute-start.3 = (f32[2,384]{1,0:T(2,128)S(1)}, f32[2,384]{1,0:T(2,128)S(1)}, u32[]{:S(2)}, u32[]{:S(2)}) collective-permute-start(f32[2,384]{1,0:T(2,128)S(1)} %add.6.refs_0_), channel_id=1, source_target_pairs={{0,6},{1,7},{2,4},{3,5},{4,2},{5,3},{6,0},{7,1},{8,14},{9,15},{10,... | collective-permute-start | bytes 9224 | tf_op jit(solution)/shard_map/ppermute | solution.py:384
  12.2 1.6 %collective-permute-done.3.refs_3_ = f32[2,384]{1,0:T(2,128)S(1)} collective-permute-done((f32[2,384]{1,0:T(2,128)S(1)}, f32[2,384]{1,0:T(2,128)S(1)}, u32[]{:S(2)}, u32[]{:S(2)}) %collective-permute-start.3) | collective-permute-done | bytes 3104 | tf_op jit(solution)/shard_map/ppermute | solution.py:384
  13.7 2.9 %collective-permute-done.2.refs_2_ = f32[2,384]{1,0:T(2,128)S(1)} collective-permute-done((f32[2,384]{1,0:T(2,128)S(1)}, f32[2,384]{1,0:T(2,128)S(1)}, u32[]{:S(2)}, u32[]{:S(2)}) %collective-permute-start.2) | collective-permute-done | bytes 3104 | tf_op jit(solution)/shard_map/ppermute | solution.py:384
  18.2 1.8 %collective-permute-start.10 = (bf16[2,192,128]{2,1,0:T(8,128)(2,1)S(1)}, bf16[2,192,128]{2,1,0:T(8,128)(2,1)S(1)}, u32[]{:S(2)}, u32[]{:S(2)}) collective-permute-start(bf16[2,192,128]{2,1,0:T(8,128)(2,1)S(1)} %get-tuple-element.68), channel_id=1, source_target_pairs={{0,8},{8,0},{16,24},{24,16},{1,9},{9,1},{17,25},{25,17},{2,10},{10... | collective-permute-start | bytes 294920 | tf_op jit(solution)/shard_map/ppermute | solution.py:384
  20.0 1.5 %collective-permute-start.11 = (bf16[2,192,128]{2,1,0:T(8,128)(2,1)S(1)}, bf16[2,192,128]{2,1,0:T(8,128)(2,1)S(1)}, u32[]{:S(2)}, u32[]{:S(2)}) collective-permute-start(bf16[2,192,128]{2,1,0:T(8,128)(2,1)S(1)} %get-tuple-element.69), channel_id=1, source_target_pairs={{0,16},{8,24},{16,0},{24,8},{1,17},{9,25},{17,1},{25,9},{2,18},{10... | collective-permute-start | bytes 294920 | tf_op jit(solution)/shard_map/ppermute | solution.py:384
  21.5 1.4 %collective-permute-done.10.refs_1_ = bf16[2,192,128]{2,1,0:T(8,128)(2,1)S(1)} collective-permute-done((bf16[2,192,128]{2,1,0:T(8,128)(2,1)S(1)}, bf16[2,192,128]{2,1,0:T(8,128)(2,1)S(1)}, u32[]{:S(2)}, u32[]{:S(2)}) %collective-permute-start.10) | collective-permute-done | bytes 98336 | tf_op jit(solution)/shard_map/ppermute | solution.py:384
  22.9 3.0 %collective-permute-start.12 = (bf16[2,192,128]{2,1,0:T(8,128)(2,1)S(1)}, bf16[2,192,128]{2,1,0:T(8,128)(2,1)S(1)}, u32[]{:S(2)}, u32[]{:S(2)}) collective-permute-start(bf16[2,192,128]{2,1,0:T(8,128)(2,1)S(1)} %get-tuple-element.70), channel_id=1, source_target_pairs={{0,24},{8,16},{16,8},{24,0},{1,25},{9,17},{17,9},{25,1},{2,26},{10... | collective-permute-start | bytes 294920 | tf_op jit(solution)/shard_map/ppermute | solution.py:384
  26.5 2.9 %collective-permute-start.9 = (bf16[2,192,128]{2,1,0:T(8,128)(2,1)S(1)}, bf16[2,192,128]{2,1,0:T(8,128)(2,1)S(1)}, u32[]{:S(2)}, u32[]{:S(2)}) collective-permute-start(bf16[2,192,128]{2,1,0:T(8,128)(2,1)S(1)} %get-tuple-element.66), channel_id=1, source_target_pairs={{0,24},{8,16},{16,8},{24,0},{1,25},{9,17},{17,9},{25,1},{2,26},{10... | collective-permute-start | bytes 294920 | tf_op jit(solution)/shard_map/ppermute | solution.py:384
  29.4 1.5 %shard_map.112 = (bf16[1536,128]{1,0:T(8,128)(2,1)S(1)}, f32[5376,256]{1,0:T(8,128)S(1)}) custom-call(s32[8]{0:T(128)S(1)} %get-tuple-element.49.numbers_ref, bf16[2,384,128]{2,1,0:T(8,128)(2,1)S(1)} %get-tuple-element.57.refs_0_, bf16[2,384,128]{2,1,0:T(8,128)(2,1)S(1)} %collective-permute-done.4.refs_1_, ...), custom_call_target="tpu_custom_call" | custom-call | tf_op jit(solution)/shard_map/pallas_call | solution.py:401
  31.0 2.2 %shard_map.113 = (bf16[768,128]{1,0:T(8,128)(2,1)S(1)}, bf16[768,128]{1,0:T(8,128)(2,1)S(1)}, bf16[768,128]{1,0:T(8,128)(2,1)S(1)}, f32[768,128]{1,0:T(8,128)S(1...) custom-call(s32[8]{0:T(128)S(1)} %get-tuple-element.49.numbers_ref, ...), custom_call_target="tpu_custom_call" | custom-call | tf_op jit(solution)/shard_map/pallas_call | solution.py:401
  33.2 4.6 %shard_map.114 = (bf16[3,384,128]{2,1,0:T(8,128)(2,1)S(1)}, bf16[3,384,128]{2,1,0:T(8,128)(2,1)S(1)}, bf16[3,384,128]{2,1,0:T(8,128)(2,1)S(1)}, bf16[3,384,128]{...) custom-call(s32[8]{0:T(128)S(1)} %get-tuple-element.49.numbers_ref, ...), custom_call_target="tpu_custom_call" | custom-call | tf_op jit(solution)/shard_map/pallas_call | solution.py:401
  38.3 1.8 %collective-permute-start.14 = (bf16[3,384,128]{2,1,0:T(8,128)(2,1)S(1)}, bf16[3,384,128]{2,1,0:T(8,128)(2,1)S(1)}, u32[]{:S(2)}, u32[]{:S(2)}) collective-permute-start(bf16[3,384,128]{2,1,0:T(8,128)(2,1)S(1)} %get-tuple-element.80), channel_id=1, source_target_pairs={{0,16},{8,24},{16,0},{24,8},{1,17},{9,25},{17,1},{25,9},{2,18},{10... | collective-permute-start | bytes 884744 | tf_op jit(solution)/shard_map/ppermute | solution.py:384
  40.1 1.2 %collective-permute-start.15 = (bf16[3,384,128]{2,1,0:T(8,128)(2,1)S(1)}, bf16[3,384,128]{2,1,0:T(8,128)(2,1)S(1)}, u32[]{:S(2)}, u32[]{:S(2)}) collective-permute-start(bf16[3,384,128]{2,1,0:T(8,128)(2,1)S(1)} %get-tuple-element.81), channel_id=1, source_target_pairs={{0,24},{8,16},{16,8},{24,0},{1,25},{9,17},{17,9},{25,1},{2,26},{10... | collective-permute-start | bytes 884744 | tf_op jit(solution)/shard_map/ppermute | solution.py:384
  42.5 3.7 %collective-permute-start.19 = (f32[8,384]{1,0:T(8,128)S(1)}, f32[8,384]{1,0:T(8,128)S(1)}, u32[]{:S(2)}, u32[]{:S(2)}) collective-permute-start(f32[8,384]{1,0:T(8,128)S(1)} %add.7.refs_0_), channel_id=1, source_target_pairs={{0,6},{1,7},{2,4},{3,5},{4,2},{5,3},{6,0},{7,1},{8,14},{9,15},{10,... | collective-permute-start | bytes 36872 | tf_op jit(solution)/shard_map/ppermute | solution.py:384
  46.1 1.9 %collective-permute-done.19.refs_3_ = f32[8,384]{1,0:T(8,128)S(1)} collective-permute-done((f32[8,384]{1,0:T(8,128)S(1)}, f32[8,384]{1,0:T(8,128)S(1)}, u32[]{:S(2)}, u32[]{:S(2)}) %collective-permute-start.19) | collective-permute-done | bytes 12320 | tf_op jit(solution)/shard_map/ppermute | solution.py:384
  48.0 2.7 %collective-permute-done.18.refs_2_ = f32[8,384]{1,0:T(8,128)S(1)} collective-permute-done((f32[8,384]{1,0:T(8,128)S(1)}, f32[8,384]{1,0:T(8,128)S(1)}, u32[]{:S(2)}, u32[]{:S(2)}) %collective-permute-start.18) | collective-permute-done | bytes 12320 | tf_op jit(solution)/shard_map/ppermute | solution.py:384
  52.4 1.8 %collective-permute-start.21 = (f32[4,384]{1,0:T(4,128)S(1)}, f32[4,384]{1,0:T(4,128)S(1)}, u32[]{:S(2)}, u32[]{:S(2)}) collective-permute-start(f32[4,384]{1,0:T(4,128)S(1)} %get-tuple-element.86), channel_id=1, source_target_pairs={{0,16},{8,24},{16,0},{24,8},{1,17},{9,25},{17,1},{25,9},{2,18},{10... | collective-permute-start | bytes 18440 | tf_op jit(solution)/shard_map/ppermute | solution.py:384
  54.1 1.3 %collective-permute-done.20.refs_9_ = f32[4,384]{1,0:T(4,128)S(1)} collective-permute-done((f32[4,384]{1,0:T(4,128)S(1)}, f32[4,384]{1,0:T(4,128)S(1)}, u32[]{:S(2)}, u32[]{:S(2)}) %collective-permute-start.20) | collective-permute-done | bytes 6176 | tf_op jit(solution)/shard_map/ppermute | solution.py:384
  55.4 1.7 %collective-permute-start.22 = (f32[4,384]{1,0:T(4,128)S(1)}, f32[4,384]{1,0:T(4,128)S(1)}, u32[]{:S(2)}, u32[]{:S(2)}) collective-permute-start(f32[4,384]{1,0:T(4,128)S(1)} %get-tuple-element.87), channel_id=1, source_target_pairs={{0,24},{8,16},{16,8},{24,0},{1,25},{9,17},{17,9},{25,1},{2,26},{10... | collective-permute-start | bytes 18440 | tf_op jit(solution)/shard_map/ppermute | solution.py:384
  57.2 2.8 %collective-permute-done.22.refs_11_ = f32[4,384]{1,0:T(4,128)S(1)} collective-permute-done((f32[4,384]{1,0:T(4,128)S(1)}, f32[4,384]{1,0:T(4,128)S(1)}, u32[]{:S(2)}, u32[]{:S(2)}) %collective-permute-start.22) | collective-permute-done | bytes 6176 | tf_op jit(solution)/shard_map/ppermute | solution.py:384
  60.0 1.9 %shard_map.116 = (bf16[384,512]{1,0:T(8,128)(2,1)}, bf16[384,512]{1,0:T(8,128)(2,1)}, bf16[384,512]{1,0:T(8,128)(2,1)}, f32[1,512]{1,0:T(1,128)}, f32[1,512]{1,0:T(1,128)}) custom-call(f32[2,384]{1,0:T(2,128)S(1)} %get-tuple-element.56.squares_ref, f32[2,512]{1,0:T(2,128)S(1)} %get-tuple-element.50.gains_ref, ...), custom_call_target="tpu_custom_call" | custom-call | tf_op jit(solution)/shard_map/pallas_call | solution.py:401
  (31 shorter events, 6.7 us)
Async XLA Ops:
  2.4 23.6 %collective-permute-start.4 = (bf16[2,384,128]{2,1,0:T(8,128)(2,1)S(1)}, bf16[2,384,128]{2,1,0:T(8,128)(2,1)S(1)}, u32[]{:S(2)}, u32[]{:S(2)}) collective-permute-start(bf16[2,384,128]{2,1,0:T(8,128)(2,1)S(1)} %get-tuple-element.58), channel_id=1, source_target_pairs={{0,8},{8,0},{16,24},{24,16},{1,9},{9,1},{17,25},{25,17},{2,10},{10... | collective-permute-start | bytes 589832 | tf_op jit(solution)/shard_map/ppermute | solution.py:384
  5.4 21.1 %collective-permute-start.5 = (bf16[2,384,128]{2,1,0:T(8,128)(2,1)S(1)}, bf16[2,384,128]{2,1,0:T(8,128)(2,1)S(1)}, u32[]{:S(2)}, u32[]{:S(2)}) collective-permute-start(bf16[2,384,128]{2,1,0:T(8,128)(2,1)S(1)} %get-tuple-element.59), channel_id=1, source_target_pairs={{0,16},{8,24},{16,0},{24,8},{1,17},{9,25},{17,1},{25,9},{2,18},{10... | collective-permute-start | bytes 589832 | tf_op jit(solution)/shard_map/ppermute | solution.py:384
  6.9 19.6 %collective-permute-start.6 = (bf16[2,384,128]{2,1,0:T(8,128)(2,1)S(1)}, bf16[2,384,128]{2,1,0:T(8,128)(2,1)S(1)}, u32[]{:S(2)}, u32[]{:S(2)}) collective-permute-start(bf16[2,384,128]{2,1,0:T(8,128)(2,1)S(1)} %get-tuple-element.60), channel_id=1, source_target_pairs={{0,24},{8,16},{16,8},{24,0},{1,25},{9,17},{17,9},{25,1},{2,26},{10... | collective-permute-start | bytes 589832 | tf_op jit(solution)/shard_map/ppermute | solution.py:384
  6.9 1.2 %collective-permute-start = (f32[2,384]{1,0:T(2,128)S(1)}, f32[2,384]{1,0:T(2,128)S(1)}, u32[]{:S(2)}, u32[]{:S(2)}) collective-permute-start(f32[2,384]{1,0:T(2,128)S(1)} %get-tuple-element.51), channel_id=1, source_target_pairs={{0,1},{1,0},{2,3},{3,2},{4,5},{5,4},{6,7},{7,6},{8,9},{9,8},{10,11... | collective-permute-start | bytes 9224 | tf_op jit(solution)/shard_map/ppermute | solution.py:384
  8.1 5.6 %collective-permute-start.3 = (f32[2,384]{1,0:T(2,128)S(1)}, f32[2,384]{1,0:T(2,128)S(1)}, u32[]{:S(2)}, u32[]{:S(2)}) collective-permute-start(f32[2,384]{1,0:T(2,128)S(1)} %add.6.refs_0_), channel_id=1, source_target_pairs={{0,6},{1,7},{2,4},{3,5},{4,2},{5,3},{6,0},{7,1},{8,14},{9,15},{10,... | collective-permute-start | bytes 9224 | tf_op jit(solution)/shard_map/ppermute | solution.py:384
  12.2 4.5 %collective-permute-start.2 = (f32[2,384]{1,0:T(2,128)S(1)}, f32[2,384]{1,0:T(2,128)S(1)}, u32[]{:S(2)}, u32[]{:S(2)}) collective-permute-start(f32[2,384]{1,0:T(2,128)S(1)} %add.6.refs_0_), channel_id=1, source_target_pairs={{0,4},{1,5},{2,6},{3,7},{4,0},{5,1},{6,2},{7,3},{8,12},{9,13},{10,... | collective-permute-start | bytes 9224 | tf_op jit(solution)/shard_map/ppermute | solution.py:384
  13.7 3.6 %collective-permute-start.1 = (f32[2,384]{1,0:T(2,128)S(1)}, f32[2,384]{1,0:T(2,128)S(1)}, u32[]{:S(2)}, u32[]{:S(2)}) collective-permute-start(f32[2,384]{1,0:T(2,128)S(1)} %add.6.refs_0_), channel_id=1, source_target_pairs={{0,2},{1,3},{2,0},{3,1},{4,6},{5,7},{6,4},{7,5},{8,10},{9,11},{10,... | collective-permute-start | bytes 9224 | tf_op jit(solution)/shard_map/ppermute | solution.py:384
  18.2 4.7 %collective-permute-start.10 = (bf16[2,192,128]{2,1,0:T(8,128)(2,1)S(1)}, bf16[2,192,128]{2,1,0:T(8,128)(2,1)S(1)}, u32[]{:S(2)}, u32[]{:S(2)}) collective-permute-start(bf16[2,192,128]{2,1,0:T(8,128)(2,1)S(1)} %get-tuple-element.68), channel_id=1, source_target_pairs={{0,8},{8,0},{16,24},{24,16},{1,9},{9,1},{17,25},{25,17},{2,10},{10... | collective-permute-start | bytes 294920 | tf_op jit(solution)/shard_map/ppermute | solution.py:384
  20.0 11.0 %collective-permute-start.11 = (bf16[2,192,128]{2,1,0:T(8,128)(2,1)S(1)}, bf16[2,192,128]{2,1,0:T(8,128)(2,1)S(1)}, u32[]{:S(2)}, u32[]{:S(2)}) collective-permute-start(bf16[2,192,128]{2,1,0:T(8,128)(2,1)S(1)} %get-tuple-element.69), channel_id=1, source_target_pairs={{0,16},{8,24},{16,0},{24,8},{1,17},{9,25},{17,1},{25,9},{2,18},{10... | collective-permute-start | bytes 294920 | tf_op jit(solution)/shard_map/ppermute | solution.py:384
  22.9 8.1 %collective-permute-start.12 = (bf16[2,192,128]{2,1,0:T(8,128)(2,1)S(1)}, bf16[2,192,128]{2,1,0:T(8,128)(2,1)S(1)}, u32[]{:S(2)}, u32[]{:S(2)}) collective-permute-start(bf16[2,192,128]{2,1,0:T(8,128)(2,1)S(1)} %get-tuple-element.70), channel_id=1, source_target_pairs={{0,24},{8,16},{16,8},{24,0},{1,25},{9,17},{17,9},{25,1},{2,26},{10... | collective-permute-start | bytes 294920 | tf_op jit(solution)/shard_map/ppermute | solution.py:384
  25.9 7.2 %collective-permute-start.7 = (bf16[2,192,128]{2,1,0:T(8,128)(2,1)S(1)}, bf16[2,192,128]{2,1,0:T(8,128)(2,1)S(1)}, u32[]{:S(2)}, u32[]{:S(2)}) collective-permute-start(bf16[2,192,128]{2,1,0:T(8,128)(2,1)S(1)} %get-tuple-element.64), channel_id=1, source_target_pairs={{0,8},{8,0},{16,24},{24,16},{1,9},{9,1},{17,25},{25,17},{2,10},{10... | collective-permute-start | bytes 294920 | tf_op jit(solution)/shard_map/ppermute | solution.py:384
  26.5 6.7 %collective-permute-start.8 = (bf16[2,192,128]{2,1,0:T(8,128)(2,1)S(1)}, bf16[2,192,128]{2,1,0:T(8,128)(2,1)S(1)}, u32[]{:S(2)}, u32[]{:S(2)}) collective-permute-start(bf16[2,192,128]{2,1,0:T(8,128)(2,1)S(1)} %get-tuple-element.65), channel_id=1, source_target_pairs={{0,16},{8,24},{16,0},{24,8},{1,17},{9,25},{17,1},{25,9},{2,18},{10... | collective-permute-start | bytes 294920 | tf_op jit(solution)/shard_map/ppermute | solution.py:384
  26.5 6.7 %collective-permute-start.9 = (bf16[2,192,128]{2,1,0:T(8,128)(2,1)S(1)}, bf16[2,192,128]{2,1,0:T(8,128)(2,1)S(1)}, u32[]{:S(2)}, u32[]{:S(2)}) collective-permute-start(bf16[2,192,128]{2,1,0:T(8,128)(2,1)S(1)} %get-tuple-element.66), channel_id=1, source_target_pairs={{0,24},{8,16},{16,8},{24,0},{1,25},{9,17},{17,9},{25,1},{2,26},{10... | collective-permute-start | bytes 294920 | tf_op jit(solution)/shard_map/ppermute | solution.py:384
  37.8 22.2 %collective-permute-start.13 = (bf16[3,384,128]{2,1,0:T(8,128)(2,1)S(1)}, bf16[3,384,128]{2,1,0:T(8,128)(2,1)S(1)}, u32[]{:S(2)}, u32[]{:S(2)}) collective-permute-start(bf16[3,384,128]{2,1,0:T(8,128)(2,1)S(1)} %get-tuple-element.79), channel_id=1, source_target_pairs={{0,8},{8,0},{16,24},{24,16},{1,9},{9,1},{17,25},{25,17},{2,10},{10... | collective-permute-start | bytes 884744 | tf_op jit(solution)/shard_map/ppermute | solution.py:384
  38.3 21.6 %collective-permute-start.14 = (bf16[3,384,128]{2,1,0:T(8,128)(2,1)S(1)}, bf16[3,384,128]{2,1,0:T(8,128)(2,1)S(1)}, u32[]{:S(2)}, u32[]{:S(2)}) collective-permute-start(bf16[3,384,128]{2,1,0:T(8,128)(2,1)S(1)} %get-tuple-element.80), channel_id=1, source_target_pairs={{0,16},{8,24},{16,0},{24,8},{1,17},{9,25},{17,1},{25,9},{2,18},{10... | collective-permute-start | bytes 884744 | tf_op jit(solution)/shard_map/ppermute | solution.py:384
  40.1 19.9 %collective-permute-start.15 = (bf16[3,384,128]{2,1,0:T(8,128)(2,1)S(1)}, bf16[3,384,128]{2,1,0:T(8,128)(2,1)S(1)}, u32[]{:S(2)}, u32[]{:S(2)}) collective-permute-start(bf16[3,384,128]{2,1,0:T(8,128)(2,1)S(1)} %get-tuple-element.81), channel_id=1, source_target_pairs={{0,24},{8,16},{16,8},{24,0},{1,25},{9,17},{17,9},{25,1},{2,26},{10... | collective-permute-start | bytes 884744 | tf_op jit(solution)/shard_map/ppermute | solution.py:384
  41.3 1.2 %collective-permute-start.16 = (f32[8,384]{1,0:T(8,128)S(1)}, f32[8,384]{1,0:T(8,128)S(1)}, u32[]{:S(2)}, u32[]{:S(2)}) collective-permute-start(f32[8,384]{1,0:T(8,128)S(1)} %get-tuple-element.83), channel_id=1, source_target_pairs={{0,1},{1,0},{2,3},{3,2},{4,5},{5,4},{6,7},{7,6},{8,9},{9,8},{10,11... | collective-permute-start | bytes 36872 | tf_op jit(solution)/shard_map/ppermute | solution.py:384
  42.5 5.6 %collective-permute-start.19 = (f32[8,384]{1,0:T(8,128)S(1)}, f32[8,384]{1,0:T(8,128)S(1)}, u32[]{:S(2)}, u32[]{:S(2)}) collective-permute-start(f32[8,384]{1,0:T(8,128)S(1)} %add.7.refs_0_), channel_id=1, source_target_pairs={{0,6},{1,7},{2,4},{3,5},{4,2},{5,3},{6,0},{7,1},{8,14},{9,15},{10,... | collective-permute-start | bytes 36872 | tf_op jit(solution)/shard_map/ppermute | solution.py:384
  46.1 4.6 %collective-permute-start.18 = (f32[8,384]{1,0:T(8,128)S(1)}, f32[8,384]{1,0:T(8,128)S(1)}, u32[]{:S(2)}, u32[]{:S(2)}) collective-permute-start(f32[8,384]{1,0:T(8,128)S(1)} %add.7.refs_0_), channel_id=1, source_target_pairs={{0,4},{1,5},{2,6},{3,7},{4,0},{5,1},{6,2},{7,3},{8,12},{9,13},{10,... | collective-permute-start | bytes 36872 | tf_op jit(solution)/shard_map/ppermute | solution.py:384
  48.0 3.7 %collective-permute-start.17 = (f32[8,384]{1,0:T(8,128)S(1)}, f32[8,384]{1,0:T(8,128)S(1)}, u32[]{:S(2)}, u32[]{:S(2)}) collective-permute-start(f32[8,384]{1,0:T(8,128)S(1)} %add.7.refs_0_), channel_id=1, source_target_pairs={{0,2},{1,3},{2,0},{3,1},{4,6},{5,7},{6,4},{7,5},{8,10},{9,11},{10,... | collective-permute-start | bytes 36872 | tf_op jit(solution)/shard_map/ppermute | solution.py:384
  51.8 3.7 %collective-permute-start.20 = (f32[4,384]{1,0:T(4,128)S(1)}, f32[4,384]{1,0:T(4,128)S(1)}, u32[]{:S(2)}, u32[]{:S(2)}) collective-permute-start(f32[4,384]{1,0:T(4,128)S(1)} %get-tuple-element.85), channel_id=1, source_target_pairs={{0,8},{8,0},{16,24},{24,16},{1,9},{9,1},{17,25},{25,17},{2,10},{10... | collective-permute-start | bytes 18440 | tf_op jit(solution)/shard_map/ppermute | solution.py:384
  52.4 4.8 %collective-permute-start.21 = (f32[4,384]{1,0:T(4,128)S(1)}, f32[4,384]{1,0:T(4,128)S(1)}, u32[]{:S(2)}, u32[]{:S(2)}) collective-permute-start(f32[4,384]{1,0:T(4,128)S(1)} %get-tuple-element.86), channel_id=1, source_target_pairs={{0,16},{8,24},{16,0},{24,8},{1,17},{9,25},{17,1},{25,9},{2,18},{10... | collective-permute-start | bytes 18440 | tf_op jit(solution)/shard_map/ppermute | solution.py:384
  55.4 4.5 %collective-permute-start.22 = (f32[4,384]{1,0:T(4,128)S(1)}, f32[4,384]{1,0:T(4,128)S(1)}, u32[]{:S(2)}, u32[]{:S(2)}) collective-permute-start(f32[4,384]{1,0:T(4,128)S(1)} %get-tuple-element.87), channel_id=1, source_target_pairs={{0,24},{8,16},{16,8},{24,0},{1,25},{9,17},{17,9},{25,1},{2,26},{10... | collective-permute-start | bytes 18440 | tf_op jit(solution)/shard_map/ppermute | solution.py:384

commit v3 on v2

--- a/solution.py
+++ b/solution.py
@@ -139,8 +139,10 @@
         step()
 
 
-def query_blocks(block, indices, query, key, grad, grad_probs, scores, probs, grad_scores, on_query, on_key):
-    base, chunk = indices[-1], block // 2
+def query_blocks(
+    block, indices, query, key, grad, grad_probs, scores, probs, grad_scores, on_query, on_key, late_steps=()
+):
+    base, chunk, fine = indices[-1], block // 2, block // 4
     exponent_scale = HD ** (-0.5) * math.log2(math.e)
     down = lax.broadcasted_iota(jnp.int32, (chunk, block), 0)
     across = lax.broadcasted_iota(jnp.int32, (chunk, block), 1)
@@ -175,25 +177,25 @@
         def sums_step(start):
             if start == 0:
                 best[index] = jnp.max(best[index], axis=0, keepdims=True)
-            there = slice(start, start + chunk)
+            there = slice(start, start + fine)
             tile = jnp.exp2((held[there, :] - best[index]) * exponent_scale)
             held[there, :] = tile
             merge(total, index, column_part(tile, jnp.sum), jnp.add)
             first = tile_rows(index, 0, block).start + start
-            merge(delta, index, column_part(tile * grad_probs[first : first + chunk, :], jnp.sum), jnp.add)
+            merge(delta, index, column_part(tile * grad_probs[first : first + fine, :], jnp.sum), jnp.add)
 
         def rounding_step(start):
             if start == 0:
                 total[index] = 1.0 / jnp.sum(total[index], axis=0, keepdims=True)
                 delta[index] = jnp.sum(delta[index], axis=0, keepdims=True) * total[index]
-            there, columns = slice(start, start + chunk), rows_of(index - base)
+            there, columns = slice(start, start + fine), rows_of(index - base)
             tile = held[there, :] * total[index]
             probs[there, columns] = tile.astype(jnp.bfloat16)
             first = tile_rows(index, 0, block).start + start
-            tile = tile * (grad_probs[first : first + chunk, :] - delta[index])
+            tile = tile * (grad_probs[first : first + fine, :] - delta[index])
             grad_scores[there, columns] = tile.astype(jnp.bfloat16)
 
-        starts = range(0, (index + 1) * block, chunk)
+        starts = range(0, (index + 1) * block, fine)
         return [functools.partial(step, start) for step in (sums_step, rounding_step) for start in starts]
 
     def product_steps(index):
@@ -227,8 +229,9 @@
         following = score_steps(indices[position + 1]) if position + 1 < len(indices) else []
         in_turn(softmax_steps(index), products + following)
         products = product_steps(index)
-    for step in products:
+    for step in products[:2]:
         step()
+    in_turn(products[2:], late_steps)
 
 
 def low_kernel(peers, block, numbers_ref, grad, grad_probs, *refs):
@@ -290,10 +293,6 @@
         key_grad[there, :] = key_product * HD ** (-0.5)
         value_grad[there, :] = value_product.astype(jnp.bfloat16)
 
-    indices = range(rows // block - 1, low // block - 1, -1)
-    query_blocks(
-        block, indices, query, key, grad.at[low:], grad_probs, scores, probs, grad_scores, on_query, on_key
-    )
     gains, sums = [low_gain[...], None], {}
 
     def finished(side, terms):
@@ -301,21 +300,38 @@
         gains[side] = part if gains[side] is None else gains[side] + part
         return lane_sums(terms)
 
-    for high in (True, False):
-        for mask in range(peers):
-            place, local, _ = stripe_rows(numbers_ref, device ^ mask, high, stripe)
-            normed_grad = key_grad[place, :]
-            grads_refs[mask][1, local, :] = normed_grad.astype(jnp.bfloat16)
-            sums[mask, 1, high] = finished(1, normed_grad * key[place, :].astype(jnp.float32))
-            grads_refs[mask][2, local, :] = value_grad[place, :]
-            if high:
-                upper = high_rows(place, rows)
-                normed_grad = query_grad[upper, :]
-                grads_refs[mask][0, local, :] = normed_grad.astype(jnp.bfloat16)
-                sums[mask, 0, high] = finished(0, normed_grad * query[upper, :].astype(jnp.float32))
-            else:
-                grads_refs[mask][0, local, :] = low_query_grad[place, :]
-                sums[mask, 0, high] = low_sums[mask : mask + 1, :]
+    def result_step(mask, high):
+        place, local, _ = stripe_rows(numbers_ref, device ^ mask, high, stripe)
+        normed_grad = key_grad[place, :]
+        grads_refs[mask][1, local, :] = normed_grad.astype(jnp.bfloat16)
+        sums[mask, 1, high] = finished(1, normed_grad * key[place, :].astype(jnp.float32))
+        grads_refs[mask][2, local, :] = value_grad[place, :]
+        if high:
+            upper = high_rows(place, rows)
+            normed_grad = query_grad[upper, :]
+            grads_refs[mask][0, local, :] = normed_grad.astype(jnp.bfloat16)
+            sums[mask, 0, high] = finished(0, normed_grad * query[upper, :].astype(jnp.float32))
+        else:
+            grads_refs[mask][0, local, :] = low_query_grad[place, :]
+            sums[mask, 0, high] = low_sums[mask : mask + 1, :]
+
+    indices = range(rows // block - 1, low // block - 1, -1)
+    query_blocks(
+        block,
+        indices,
+        query,
+        key,
+        grad.at[low:],
+        grad_probs,
+        scores,
+        probs,
+        grad_scores,
+        on_query,
+        on_key,
+        [functools.partial(result_step, mask, True) for mask in range(peers)],
+    )
+    for mask in range(peers):
+        result_step(mask, False)
     for mask in range(peers):
         _, _, slot = stripe_rows(numbers_ref, device ^ mask, True, stripe)
         for side in range(2):

time: 62 us -> 61.9 us (level)
  no operation moved by 1% of the time
where the time goes in v3:
time: 61.9 us; the launch traced here: 61.7 us
  starting transfers between devices  29.8 us (48%)
  waiting for transfers between devices  18.6 us (30%)
  Pallas kernels  12.6 us (20%)
  between operations  0.73 us (1%)
    ppermute x23, starting transfers between devices, swap(): lax.ppermute(array, axis, [(index, index ^ mask) for index in range(size)])  29.8 us
    ppermute x23, waiting for transfers between devices, swap(): lax.ppermute(array, axis, [(index, index ^ mask) for index in range(size)])  18.6 us
    pallas_call x7, Pallas kernels, call(): pl.pallas_call(kernel, out_shape=out_shape, in_specs=in_specs, out_specs=...  12.6 us
  transfers between devices with their start and end apart: 23, of which 11 were waited for; matrix products, arithmetic and copies ran while one was open for 0% of the time, Pallas kernels for 7%

profile of v3, /device:TPU:0, one launch (start us, length us, event | category | flops | bytes accessed | tf_op | source)
XLA Modules:
  0.0 61.7 jit_solution(8143244699685471033)
XLA Ops:
  0.6 1.7 %shard_map.110 = (bf16[2,384,128]{2,1,0:T(8,128)(2,1)S(1)}, bf16[2,384,128]{2,1,0:T(8,128)(2,1)S(1)}, bf16[2,384,128]{2,1,0:T(8,128)(2,1)S(1)}, bf16[2,384,128]{...) custom-call(bf16[384,512]{1,0:T(8,128)(2,1)} %refs_0_.1, ...), custom_call_target="tpu_custom_call" | custom-call | tf_op jit(solution)/shard_map/pallas_call | solution.py:417
  2.4 3.0 %collective-permute-start.4 = (bf16[2,384,128]{2,1,0:T(8,128)(2,1)S(1)}, bf16[2,384,128]{2,1,0:T(8,128)(2,1)S(1)}, u32[]{:S(2)}, u32[]{:S(2)}) collective-permute-start(bf16[2,384,128]{2,1,0:T(8,128)(2,1)S(1)} %get-tuple-element.58), channel_id=1, source_target_pairs={{0,8},{8,0},{16,24},{24,16},{1,9},{9,1},{17,25},{25,17},{2,10},{10... | collective-permute-start | bytes 589832 | tf_op jit(solution)/shard_map/ppermute | solution.py:400
  5.4 1.5 %collective-permute-start.5 = (bf16[2,384,128]{2,1,0:T(8,128)(2,1)S(1)}, bf16[2,384,128]{2,1,0:T(8,128)(2,1)S(1)}, u32[]{:S(2)}, u32[]{:S(2)}) collective-permute-start(bf16[2,384,128]{2,1,0:T(8,128)(2,1)S(1)} %get-tuple-element.59), channel_id=1, source_target_pairs={{0,16},{8,24},{16,0},{24,8},{1,17},{9,25},{17,1},{25,9},{2,18},{10... | collective-permute-start | bytes 589832 | tf_op jit(solution)/shard_map/ppermute | solution.py:400
  8.1 4.1 %collective-permute-start.3 = (f32[2,384]{1,0:T(2,128)S(1)}, f32[2,384]{1,0:T(2,128)S(1)}, u32[]{:S(2)}, u32[]{:S(2)}) collective-permute-start(f32[2,384]{1,0:T(2,128)S(1)} %add.6.refs_0_), channel_id=1, source_target_pairs={{0,6},{1,7},{2,4},{3,5},{4,2},{5,3},{6,0},{7,1},{8,14},{9,15},{10,... | collective-permute-start | bytes 9224 | tf_op jit(solution)/shard_map/ppermute | solution.py:400
  12.2 1.6 %collective-permute-done.3.refs_3_ = f32[2,384]{1,0:T(2,128)S(1)} collective-permute-done((f32[2,384]{1,0:T(2,128)S(1)}, f32[2,384]{1,0:T(2,128)S(1)}, u32[]{:S(2)}, u32[]{:S(2)}) %collective-permute-start.3) | collective-permute-done | bytes 3104 | tf_op jit(solution)/shard_map/ppermute | solution.py:400
  13.7 2.9 %collective-permute-done.2.refs_2_ = f32[2,384]{1,0:T(2,128)S(1)} collective-permute-done((f32[2,384]{1,0:T(2,128)S(1)}, f32[2,384]{1,0:T(2,128)S(1)}, u32[]{:S(2)}, u32[]{:S(2)}) %collective-permute-start.2) | collective-permute-done | bytes 3104 | tf_op jit(solution)/shard_map/ppermute | solution.py:400
  18.2 1.8 %collective-permute-start.10 = (bf16[2,192,128]{2,1,0:T(8,128)(2,1)S(1)}, bf16[2,192,128]{2,1,0:T(8,128)(2,1)S(1)}, u32[]{:S(2)}, u32[]{:S(2)}) collective-permute-start(bf16[2,192,128]{2,1,0:T(8,128)(2,1)S(1)} %get-tuple-element.68), channel_id=1, source_target_pairs={{0,8},{8,0},{16,24},{24,16},{1,9},{9,1},{17,25},{25,17},{2,10},{10... | collective-permute-start | bytes 294920 | tf_op jit(solution)/shard_map/ppermute | solution.py:400
  20.0 1.5 %collective-permute-start.11 = (bf16[2,192,128]{2,1,0:T(8,128)(2,1)S(1)}, bf16[2,192,128]{2,1,0:T(8,128)(2,1)S(1)}, u32[]{:S(2)}, u32[]{:S(2)}) collective-permute-start(bf16[2,192,128]{2,1,0:T(8,128)(2,1)S(1)} %get-tuple-element.69), channel_id=1, source_target_pairs={{0,16},{8,24},{16,0},{24,8},{1,17},{9,25},{17,1},{25,9},{2,18},{10... | collective-permute-start | bytes 294920 | tf_op jit(solution)/shard_map/ppermute | solution.py:400
  21.5 1.4 %collective-permute-done.10.refs_1_ = bf16[2,192,128]{2,1,0:T(8,128)(2,1)S(1)} collective-permute-done((bf16[2,192,128]{2,1,0:T(8,128)(2,1)S(1)}, bf16[2,192,128]{2,1,0:T(8,128)(2,1)S(1)}, u32[]{:S(2)}, u32[]{:S(2)}) %collective-permute-start.10) | collective-permute-done | bytes 98336 | tf_op jit(solution)/shard_map/ppermute | solution.py:400
  22.9 3.0 %collective-permute-start.12 = (bf16[2,192,128]{2,1,0:T(8,128)(2,1)S(1)}, bf16[2,192,128]{2,1,0:T(8,128)(2,1)S(1)}, u32[]{:S(2)}, u32[]{:S(2)}) collective-permute-start(bf16[2,192,128]{2,1,0:T(8,128)(2,1)S(1)} %get-tuple-element.70), channel_id=1, source_target_pairs={{0,24},{8,16},{16,8},{24,0},{1,25},{9,17},{17,9},{25,1},{2,26},{10... | collective-permute-start | bytes 294920 | tf_op jit(solution)/shard_map/ppermute | solution.py:400
  26.5 2.9 %collective-permute-start.9 = (bf16[2,192,128]{2,1,0:T(8,128)(2,1)S(1)}, bf16[2,192,128]{2,1,0:T(8,128)(2,1)S(1)}, u32[]{:S(2)}, u32[]{:S(2)}) collective-permute-start(bf16[2,192,128]{2,1,0:T(8,128)(2,1)S(1)} %get-tuple-element.66), channel_id=1, source_target_pairs={{0,24},{8,16},{16,8},{24,0},{1,25},{9,17},{17,9},{25,1},{2,26},{10... | collective-permute-start | bytes 294920 | tf_op jit(solution)/shard_map/ppermute | solution.py:400
  29.4 1.5 %shard_map.112 = (bf16[1536,128]{1,0:T(8,128)(2,1)S(1)}, f32[5376,256]{1,0:T(8,128)S(1)}) custom-call(s32[8]{0:T(128)S(1)} %get-tuple-element.49.numbers_ref, bf16[2,384,128]{2,1,0:T(8,128)(2,1)S(1)} %get-tuple-element.57.refs_0_, bf16[2,384,128]{2,1,0:T(8,128)(2,1)S(1)} %collective-permute-done.4.refs_1_, ...), custom_call_target="tpu_custom_call" | custom-call | tf_op jit(solution)/shard_map/pallas_call | solution.py:417
  31.0 2.2 %shard_map.113 = (bf16[768,128]{1,0:T(8,128)(2,1)S(1)}, bf16[768,128]{1,0:T(8,128)(2,1)S(1)}, bf16[768,128]{1,0:T(8,128)(2,1)S(1)}, f32[768,128]{1,0:T(8,128)S(1...) custom-call(s32[8]{0:T(128)S(1)} %get-tuple-element.49.numbers_ref, ...), custom_call_target="tpu_custom_call" | custom-call | tf_op jit(solution)/shard_map/pallas_call | solution.py:417
  33.2 4.5 %shard_map.114 = (bf16[3,384,128]{2,1,0:T(8,128)(2,1)S(1)}, bf16[3,384,128]{2,1,0:T(8,128)(2,1)S(1)}, bf16[3,384,128]{2,1,0:T(8,128)(2,1)S(1)}, bf16[3,384,128]{...) custom-call(s32[8]{0:T(128)S(1)} %get-tuple-element.49.numbers_ref, ...), custom_call_target="tpu_custom_call" | custom-call | tf_op jit(solution)/shard_map/pallas_call | solution.py:417
  38.2 1.8 %collective-permute-start.14 = (bf16[3,384,128]{2,1,0:T(8,128)(2,1)S(1)}, bf16[3,384,128]{2,1,0:T(8,128)(2,1)S(1)}, u32[]{:S(2)}, u32[]{:S(2)}) collective-permute-start(bf16[3,384,128]{2,1,0:T(8,128)(2,1)S(1)} %get-tuple-element.80), channel_id=1, source_target_pairs={{0,16},{8,24},{16,0},{24,8},{1,17},{9,25},{17,1},{25,9},{2,18},{10... | collective-permute-start | bytes 884744 | tf_op jit(solution)/shard_map/ppermute | solution.py:400
  41.2 1.2 %collective-permute-done.16 = f32[8,384]{1,0:T(8,128)S(1)} collective-permute-done((f32[8,384]{1,0:T(8,128)S(1)}, f32[8,384]{1,0:T(8,128)S(1)}, u32[]{:S(2)}, u32[]{:S(2)}) %collective-permute-start.16) | collective-permute-done | bytes 12320 | tf_op jit(solution)/shard_map/ppermute | solution.py:400
  42.4 3.7 %collective-permute-start.19 = (f32[8,384]{1,0:T(8,128)S(1)}, f32[8,384]{1,0:T(8,128)S(1)}, u32[]{:S(2)}, u32[]{:S(2)}) collective-permute-start(f32[8,384]{1,0:T(8,128)S(1)} %add.7.refs_0_), channel_id=1, source_target_pairs={{0,6},{1,7},{2,4},{3,5},{4,2},{5,3},{6,0},{7,1},{8,14},{9,15},{10,... | collective-permute-start | bytes 36872 | tf_op jit(solution)/shard_map/ppermute | solution.py:400
  46.0 1.9 %collective-permute-done.19.refs_3_ = f32[8,384]{1,0:T(8,128)S(1)} collective-permute-done((f32[8,384]{1,0:T(8,128)S(1)}, f32[8,384]{1,0:T(8,128)S(1)}, u32[]{:S(2)}, u32[]{:S(2)}) %collective-permute-start.19) | collective-permute-done | bytes 12320 | tf_op jit(solution)/shard_map/ppermute | solution.py:400
  47.9 2.7 %collective-permute-done.18.refs_2_ = f32[8,384]{1,0:T(8,128)S(1)} collective-permute-done((f32[8,384]{1,0:T(8,128)S(1)}, f32[8,384]{1,0:T(8,128)S(1)}, u32[]{:S(2)}, u32[]{:S(2)}) %collective-permute-start.18) | collective-permute-done | bytes 12320 | tf_op jit(solution)/shard_map/ppermute | solution.py:400
  52.2 1.8 %collective-permute-start.21 = (f32[4,384]{1,0:T(4,128)S(1)}, f32[4,384]{1,0:T(4,128)S(1)}, u32[]{:S(2)}, u32[]{:S(2)}) collective-permute-start(f32[4,384]{1,0:T(4,128)S(1)} %get-tuple-element.86), channel_id=1, source_target_pairs={{0,16},{8,24},{16,0},{24,8},{1,17},{9,25},{17,1},{25,9},{2,18},{10... | collective-permute-start | bytes 18440 | tf_op jit(solution)/shard_map/ppermute | solution.py:400
  54.0 1.3 %collective-permute-done.20.refs_9_ = f32[4,384]{1,0:T(4,128)S(1)} collective-permute-done((f32[4,384]{1,0:T(4,128)S(1)}, f32[4,384]{1,0:T(4,128)S(1)}, u32[]{:S(2)}, u32[]{:S(2)}) %collective-permute-start.20) | collective-permute-done | bytes 6176 | tf_op jit(solution)/shard_map/ppermute | solution.py:400
  55.3 1.8 %collective-permute-start.22 = (f32[4,384]{1,0:T(4,128)S(1)}, f32[4,384]{1,0:T(4,128)S(1)}, u32[]{:S(2)}, u32[]{:S(2)}) collective-permute-start(f32[4,384]{1,0:T(4,128)S(1)} %get-tuple-element.87), channel_id=1, source_target_pairs={{0,24},{8,16},{16,8},{24,0},{1,25},{9,17},{17,9},{25,1},{2,26},{10... | collective-permute-start | bytes 18440 | tf_op jit(solution)/shard_map/ppermute | solution.py:400
  57.1 2.8 %collective-permute-done.22.refs_11_ = f32[4,384]{1,0:T(4,128)S(1)} collective-permute-done((f32[4,384]{1,0:T(4,128)S(1)}, f32[4,384]{1,0:T(4,128)S(1)}, u32[]{:S(2)}, u32[]{:S(2)}) %collective-permute-start.22) | collective-permute-done | bytes 6176 | tf_op jit(solution)/shard_map/ppermute | solution.py:400
  59.9 1.9 %shard_map.116 = (bf16[384,512]{1,0:T(8,128)(2,1)}, bf16[384,512]{1,0:T(8,128)(2,1)}, bf16[384,512]{1,0:T(8,128)(2,1)}, f32[1,512]{1,0:T(1,128)}, f32[1,512]{1,0:T(1,128)}) custom-call(f32[2,384]{1,0:T(2,128)S(1)} %get-tuple-element.56.squares_ref, f32[2,512]{1,0:T(2,128)S(1)} %get-tuple-element.50.gains_ref, ...), custom_call_target="tpu_custom_call" | custom-call | tf_op jit(solution)/shard_map/pallas_call | solution.py:417
  (31 shorter events, 6.7 us)
Async XLA Ops:
  2.4 23.6 %collective-permute-start.4 = (bf16[2,384,128]{2,1,0:T(8,128)(2,1)S(1)}, bf16[2,384,128]{2,1,0:T(8,128)(2,1)S(1)}, u32[]{:S(2)}, u32[]{:S(2)}) collective-permute-start(bf16[2,384,128]{2,1,0:T(8,128)(2,1)S(1)} %get-tuple-element.58), channel_id=1, source_target_pairs={{0,8},{8,0},{16,24},{24,16},{1,9},{9,1},{17,25},{25,17},{2,10},{10... | collective-permute-start | bytes 589832 | tf_op jit(solution)/shard_map/ppermute | solution.py:400
  5.4 21.1 %collective-permute-start.5 = (bf16[2,384,128]{2,1,0:T(8,128)(2,1)S(1)}, bf16[2,384,128]{2,1,0:T(8,128)(2,1)S(1)}, u32[]{:S(2)}, u32[]{:S(2)}) collective-permute-start(bf16[2,384,128]{2,1,0:T(8,128)(2,1)S(1)} %get-tuple-element.59), channel_id=1, source_target_pairs={{0,16},{8,24},{16,0},{24,8},{1,17},{9,25},{17,1},{25,9},{2,18},{10... | collective-permute-start | bytes 589832 | tf_op jit(solution)/shard_map/ppermute | solution.py:400
  6.9 19.6 %collective-permute-start.6 = (bf16[2,384,128]{2,1,0:T(8,128)(2,1)S(1)}, bf16[2,384,128]{2,1,0:T(8,128)(2,1)S(1)}, u32[]{:S(2)}, u32[]{:S(2)}) collective-permute-start(bf16[2,384,128]{2,1,0:T(8,128)(2,1)S(1)} %get-tuple-element.60), channel_id=1, source_target_pairs={{0,24},{8,16},{16,8},{24,0},{1,25},{9,17},{17,9},{25,1},{2,26},{10... | collective-permute-start | bytes 589832 | tf_op jit(solution)/shard_map/ppermute | solution.py:400
  6.9 1.2 %collective-permute-start = (f32[2,384]{1,0:T(2,128)S(1)}, f32[2,384]{1,0:T(2,128)S(1)}, u32[]{:S(2)}, u32[]{:S(2)}) collective-permute-start(f32[2,384]{1,0:T(2,128)S(1)} %get-tuple-element.51), channel_id=1, source_target_pairs={{0,1},{1,0},{2,3},{3,2},{4,5},{5,4},{6,7},{7,6},{8,9},{9,8},{10,11... | collective-permute-start | bytes 9224 | tf_op jit(solution)/shard_map/ppermute | solution.py:400
  8.1 5.6 %collective-permute-start.3 = (f32[2,384]{1,0:T(2,128)S(1)}, f32[2,384]{1,0:T(2,128)S(1)}, u32[]{:S(2)}, u32[]{:S(2)}) collective-permute-start(f32[2,384]{1,0:T(2,128)S(1)} %add.6.refs_0_), channel_id=1, source_target_pairs={{0,6},{1,7},{2,4},{3,5},{4,2},{5,3},{6,0},{7,1},{8,14},{9,15},{10,... | collective-permute-start | bytes 9224 | tf_op jit(solution)/shard_map/ppermute | solution.py:400
  12.2 4.5 %collective-permute-start.2 = (f32[2,384]{1,0:T(2,128)S(1)}, f32[2,384]{1,0:T(2,128)S(1)}, u32[]{:S(2)}, u32[]{:S(2)}) collective-permute-start(f32[2,384]{1,0:T(2,128)S(1)} %add.6.refs_0_), channel_id=1, source_target_pairs={{0,4},{1,5},{2,6},{3,7},{4,0},{5,1},{6,2},{7,3},{8,12},{9,13},{10,... | collective-permute-start | bytes 9224 | tf_op jit(solution)/shard_map/ppermute | solution.py:400
  13.7 3.6 %collective-permute-start.1 = (f32[2,384]{1,0:T(2,128)S(1)}, f32[2,384]{1,0:T(2,128)S(1)}, u32[]{:S(2)}, u32[]{:S(2)}) collective-permute-start(f32[2,384]{1,0:T(2,128)S(1)} %add.6.refs_0_), channel_id=1, source_target_pairs={{0,2},{1,3},{2,0},{3,1},{4,6},{5,7},{6,4},{7,5},{8,10},{9,11},{10,... | collective-permute-start | bytes 9224 | tf_op jit(solution)/shard_map/ppermute | solution.py:400
  18.2 4.7 %collective-permute-start.10 = (bf16[2,192,128]{2,1,0:T(8,128)(2,1)S(1)}, bf16[2,192,128]{2,1,0:T(8,128)(2,1)S(1)}, u32[]{:S(2)}, u32[]{:S(2)}) collective-permute-start(bf16[2,192,128]{2,1,0:T(8,128)(2,1)S(1)} %get-tuple-element.68), channel_id=1, source_target_pairs={{0,8},{8,0},{16,24},{24,16},{1,9},{9,1},{17,25},{25,17},{2,10},{10... | collective-permute-start | bytes 294920 | tf_op jit(solution)/shard_map/ppermute | solution.py:400
  20.0 11.0 %collective-permute-start.11 = (bf16[2,192,128]{2,1,0:T(8,128)(2,1)S(1)}, bf16[2,192,128]{2,1,0:T(8,128)(2,1)S(1)}, u32[]{:S(2)}, u32[]{:S(2)}) collective-permute-start(bf16[2,192,128]{2,1,0:T(8,128)(2,1)S(1)} %get-tuple-element.69), channel_id=1, source_target_pairs={{0,16},{8,24},{16,0},{24,8},{1,17},{9,25},{17,1},{25,9},{2,18},{10... | collective-permute-start | bytes 294920 | tf_op jit(solution)/shard_map/ppermute | solution.py:400
  22.9 8.1 %collective-permute-start.12 = (bf16[2,192,128]{2,1,0:T(8,128)(2,1)S(1)}, bf16[2,192,128]{2,1,0:T(8,128)(2,1)S(1)}, u32[]{:S(2)}, u32[]{:S(2)}) collective-permute-start(bf16[2,192,128]{2,1,0:T(8,128)(2,1)S(1)} %get-tuple-element.70), channel_id=1, source_target_pairs={{0,24},{8,16},{16,8},{24,0},{1,25},{9,17},{17,9},{25,1},{2,26},{10... | collective-permute-start | bytes 294920 | tf_op jit(solution)/shard_map/ppermute | solution.py:400
  25.9 7.2 %collective-permute-start.7 = (bf16[2,192,128]{2,1,0:T(8,128)(2,1)S(1)}, bf16[2,192,128]{2,1,0:T(8,128)(2,1)S(1)}, u32[]{:S(2)}, u32[]{:S(2)}) collective-permute-start(bf16[2,192,128]{2,1,0:T(8,128)(2,1)S(1)} %get-tuple-element.64), channel_id=1, source_target_pairs={{0,8},{8,0},{16,24},{24,16},{1,9},{9,1},{17,25},{25,17},{2,10},{10... | collective-permute-start | bytes 294920 | tf_op jit(solution)/shard_map/ppermute | solution.py:400
  26.5 6.7 %collective-permute-start.8 = (bf16[2,192,128]{2,1,0:T(8,128)(2,1)S(1)}, bf16[2,192,128]{2,1,0:T(8,128)(2,1)S(1)}, u32[]{:S(2)}, u32[]{:S(2)}) collective-permute-start(bf16[2,192,128]{2,1,0:T(8,128)(2,1)S(1)} %get-tuple-element.65), channel_id=1, source_target_pairs={{0,16},{8,24},{16,0},{24,8},{1,17},{9,25},{17,1},{25,9},{2,18},{10... | collective-permute-start | bytes 294920 | tf_op jit(solution)/shard_map/ppermute | solution.py:400
  26.5 6.7 %collective-permute-start.9 = (bf16[2,192,128]{2,1,0:T(8,128)(2,1)S(1)}, bf16[2,192,128]{2,1,0:T(8,128)(2,1)S(1)}, u32[]{:S(2)}, u32[]{:S(2)}) collective-permute-start(bf16[2,192,128]{2,1,0:T(8,128)(2,1)S(1)} %get-tuple-element.66), channel_id=1, source_target_pairs={{0,24},{8,16},{16,8},{24,0},{1,25},{9,17},{17,9},{25,1},{2,26},{10... | collective-permute-start | bytes 294920 | tf_op jit(solution)/shard_map/ppermute | solution.py:400
  37.6 22.2 %collective-permute-start.13 = (bf16[3,384,128]{2,1,0:T(8,128)(2,1)S(1)}, bf16[3,384,128]{2,1,0:T(8,128)(2,1)S(1)}, u32[]{:S(2)}, u32[]{:S(2)}) collective-permute-start(bf16[3,384,128]{2,1,0:T(8,128)(2,1)S(1)} %get-tuple-element.79), channel_id=1, source_target_pairs={{0,8},{8,0},{16,24},{24,16},{1,9},{9,1},{17,25},{25,17},{2,10},{10... | collective-permute-start | bytes 884744 | tf_op jit(solution)/shard_map/ppermute | solution.py:400
  38.2 21.6 %collective-permute-start.14 = (bf16[3,384,128]{2,1,0:T(8,128)(2,1)S(1)}, bf16[3,384,128]{2,1,0:T(8,128)(2,1)S(1)}, u32[]{:S(2)}, u32[]{:S(2)}) collective-permute-start(bf16[3,384,128]{2,1,0:T(8,128)(2,1)S(1)} %get-tuple-element.80), channel_id=1, source_target_pairs={{0,16},{8,24},{16,0},{24,8},{1,17},{9,25},{17,1},{25,9},{2,18},{10... | collective-permute-start | bytes 884744 | tf_op jit(solution)/shard_map/ppermute | solution.py:400
  40.0 19.8 %collective-permute-start.15 = (bf16[3,384,128]{2,1,0:T(8,128)(2,1)S(1)}, bf16[3,384,128]{2,1,0:T(8,128)(2,1)S(1)}, u32[]{:S(2)}, u32[]{:S(2)}) collective-permute-start(bf16[3,384,128]{2,1,0:T(8,128)(2,1)S(1)} %get-tuple-element.81), channel_id=1, source_target_pairs={{0,24},{8,16},{16,8},{24,0},{1,25},{9,17},{17,9},{25,1},{2,26},{10... | collective-permute-start | bytes 884744 | tf_op jit(solution)/shard_map/ppermute | solution.py:400
  41.2 1.2 %collective-permute-start.16 = (f32[8,384]{1,0:T(8,128)S(1)}, f32[8,384]{1,0:T(8,128)S(1)}, u32[]{:S(2)}, u32[]{:S(2)}) collective-permute-start(f32[8,384]{1,0:T(8,128)S(1)} %get-tuple-element.83), channel_id=1, source_target_pairs={{0,1},{1,0},{2,3},{3,2},{4,5},{5,4},{6,7},{7,6},{8,9},{9,8},{10,11... | collective-permute-start | bytes 36872 | tf_op jit(solution)/shard_map/ppermute | solution.py:400
  42.4 5.6 %collective-permute-start.19 = (f32[8,384]{1,0:T(8,128)S(1)}, f32[8,384]{1,0:T(8,128)S(1)}, u32[]{:S(2)}, u32[]{:S(2)}) collective-permute-start(f32[8,384]{1,0:T(8,128)S(1)} %add.7.refs_0_), channel_id=1, source_target_pairs={{0,6},{1,7},{2,4},{3,5},{4,2},{5,3},{6,0},{7,1},{8,14},{9,15},{10,... | collective-permute-start | bytes 36872 | tf_op jit(solution)/shard_map/ppermute | solution.py:400
  46.0 4.6 %collective-permute-start.18 = (f32[8,384]{1,0:T(8,128)S(1)}, f32[8,384]{1,0:T(8,128)S(1)}, u32[]{:S(2)}, u32[]{:S(2)}) collective-permute-start(f32[8,384]{1,0:T(8,128)S(1)} %add.7.refs_0_), channel_id=1, source_target_pairs={{0,4},{1,5},{2,6},{3,7},{4,0},{5,1},{6,2},{7,3},{8,12},{9,13},{10,... | collective-permute-start | bytes 36872 | tf_op jit(solution)/shard_map/ppermute | solution.py:400
  47.9 3.7 %collective-permute-start.17 = (f32[8,384]{1,0:T(8,128)S(1)}, f32[8,384]{1,0:T(8,128)S(1)}, u32[]{:S(2)}, u32[]{:S(2)}) collective-permute-start(f32[8,384]{1,0:T(8,128)S(1)} %add.7.refs_0_), channel_id=1, source_target_pairs={{0,2},{1,3},{2,0},{3,1},{4,6},{5,7},{6,4},{7,5},{8,10},{9,11},{10,... | collective-permute-start | bytes 36872 | tf_op jit(solution)/shard_map/ppermute | solution.py:400
  51.6 3.7 %collective-permute-start.20 = (f32[4,384]{1,0:T(4,128)S(1)}, f32[4,384]{1,0:T(4,128)S(1)}, u32[]{:S(2)}, u32[]{:S(2)}) collective-permute-start(f32[4,384]{1,0:T(4,128)S(1)} %get-tuple-element.85), channel_id=1, source_target_pairs={{0,8},{8,0},{16,24},{24,16},{1,9},{9,1},{17,25},{25,17},{2,10},{10... | collective-permute-start | bytes 18440 | tf_op jit(solution)/shard_map/ppermute | solution.py:400
  52.2 4.9 %collective-permute-start.21 = (f32[4,384]{1,0:T(4,128)S(1)}, f32[4,384]{1,0:T(4,128)S(1)}, u32[]{:S(2)}, u32[]{:S(2)}) collective-permute-start(f32[4,384]{1,0:T(4,128)S(1)} %get-tuple-element.86), channel_id=1, source_target_pairs={{0,16},{8,24},{16,0},{24,8},{1,17},{9,25},{17,1},{25,9},{2,18},{10... | collective-permute-start | bytes 18440 | tf_op jit(solution)/shard_map/ppermute | solution.py:400
  55.3 4.5 %collective-permute-start.22 = (f32[4,384]{1,0:T(4,128)S(1)}, f32[4,384]{1,0:T(4,128)S(1)}, u32[]{:S(2)}, u32[]{:S(2)}) collective-permute-start(f32[4,384]{1,0:T(4,128)S(1)} %get-tuple-element.87), channel_id=1, source_target_pairs={{0,24},{8,16},{16,8},{24,0},{1,25},{9,17},{17,9},{25,1},{2,26},{10... | collective-permute-start | bytes 18440 | tf_op jit(solution)/shard_map/ppermute | solution.py:400

commit v4 on v3

--- a/solution.py
+++ b/solution.py
@@ -11,7 +11,6 @@
 HD = 128
 EPSILON = 1e-06
 VMEM = pl.BlockSpec(memory_space=pltpu.VMEM)
-SMEM = pl.BlockSpec(memory_space=pltpu.SMEM)
 HBM = pl.BlockSpec(memory_space=pltpu.HBM)
 ANY = pl.BlockSpec(memory_space=pl.ANY)
 ROWS_BY_ROWS = (((1,), (1,)), ((), ()))
@@ -72,7 +71,11 @@
 
 
 def stripe_rows(numbers_ref, device, high, stripe):
-    first, second = numbers_ref[2 * device], numbers_ref[2 * device + 1]
+    numbers = numbers_ref[...].astype(jnp.float32)
+    lanes = lax.broadcasted_iota(jnp.int32, numbers.shape, 1)
+    first, second = (
+        jnp.sum(jnp.where(lanes == 2 * device + slot, numbers, 0.0)).astype(jnp.int32) for slot in range(2)
+    )
     number = jnp.maximum(first, second) if high else jnp.minimum(first, second)
     slot = jnp.where(second == number, 1, 0)
     place = pl.ds(pl.multiple_of(number * stripe, stripe), stripe)
@@ -405,6 +408,14 @@
     return [array] + [swap(array, "tp", size, mask) for mask in range(2, size, 2)]
 
 
+def tp_halves(array, size):
+    mask = 1
+    while mask < size // 2:
+        array = array + swap(array, "tp", size, mask)
+        mask *= 2
+    return [array, swap(array, "tp", size, mask)]
+
+
 def to_peers(arrays, peers):
     return [arrays[0]] + [swap(arrays[mask], "ctx", peers, mask) for mask in range(1, peers)]
 
@@ -440,11 +451,11 @@
         + [
             shape((2, token_count), jnp.float32),
             shape((2, local_width), jnp.float32),
-            shape(stripe_of.shape, jnp.int32),
+            shape((1, stripe_of.shape[0]), jnp.int32),
         ],
         [
             in_hbm(array)
-            for array in (query_proj, key_proj, value_proj, grad_out, query_gain[None], key_gain[None], stripe_of)
+            for array in (query_proj, key_proj, value_proj, grad_out, query_gain[None], key_gain[None], stripe_of[None])
         ],
         [HBM] * 7,
         [VMEM] * (2 * peers + 3),
@@ -457,7 +468,7 @@
         functools.partial(normalize_kernel, peers, width, members),
         [half] * (2 * peers) + [shape((2, token_count), jnp.float32)],
         (numbers, gains, *tp_parts(squares, tp_size), *raw),
-        [SMEM] + [VMEM] * (1 + members + peers),
+        [VMEM] + [VMEM] * (1 + members + peers),
         [VMEM] * (2 * peers + 1),
         [pltpu.VMEM((2, token_count, HD), jnp.float32)],
         8,
@@ -469,7 +480,7 @@
         functools.partial(grad_probs_kernel, peers, block),
         [whole_head, shape((tiles * block, block), jnp.float32)],
         (numbers, *plain),
-        [SMEM] + [VMEM] * peers,
+        [VMEM] + [VMEM] * peers,
         [VMEM] * 2,
         [pltpu.VMEM((rows, HD), jnp.bfloat16)],
         8,
@@ -487,7 +498,7 @@
         + [low_head(jnp.float32)] * 2
         + [shape((peers, token_count // 2), jnp.float32), shape((1, HD), jnp.float32)],
         (numbers, grad, grad_probs, *low_normed),
-        [SMEM] + [VMEM] * (2 + peers),
+        [VMEM] + [VMEM] * (2 + peers),
         [VMEM] * 7,
         [pltpu.VMEM((low, HD), jnp.float32)] + scratch(low, low),
         16,
@@ -496,7 +507,7 @@
         functools.partial(high_kernel, peers, block),
         [head(3)] * peers + [shape((2 * peers, token_count), jnp.float32), shape((2, HD), jnp.float32)],
         (numbers, grad, grad_probs, *high_normed, *low_results),
-        [SMEM] + [VMEM] * (2 + peers + 7),
+        [VMEM] + [VMEM] * (2 + peers + 7),
         [VMEM] * (peers + 2),
         [
             pltpu.VMEM((low, HD), jnp.bfloat16),
@@ -510,10 +521,10 @@
     )
     grads = to_peers(grads, peers)
     totals = call(
-        functools.partial(totals_kernel, peers, members),
+        functools.partial(totals_kernel, peers, 2),
         [shape((4, token_count), jnp.float32)] * peers,
-        (gain_sums, *tp_parts(sums, tp_size)),
-        [VMEM] * (1 + members),
+        (gain_sums, *tp_halves(sums, tp_size)),
+        [VMEM] * 3,
         [VMEM] * peers,
         [],
         8,

time: 61.9 us -> 59 us (0.953)
  Pallas kernels: 12.6 us -> 10.8 us
  waiting for transfers between devices: 18.6 us -> 17.3 us
    pallas_call x7, Pallas kernels: 12.6 us -> 10.8 us  [call(): pl.pallas_call(kernel, out_shape=out_shape, in_specs=in_specs, out_specs=...]
    ppermute x23 -> x22, waiting for transfers between devices: 18.6 us -> 17.3 us  [swap(): lax.ppermute(array, axis, [(index, index ^ mask) for index in range(size)])]
    ppermute x23 -> x22, starting transfers between devices: 29.8 us -> 30.1 us  [swap(): lax.ppermute(array, axis, [(index, index ^ mask) for index in range(size)])]
  transfers between devices with their start and end apart: 23 -> 22, of which waited for: 11 -> 10; matrix products, arithmetic and copies ran while one was open for 0% -> 0% of each run, Pallas kernels for 7% -> 5%
where the time goes in v4:
time: 59 us; the launch traced here: 58.9 us
  starting transfers between devices  30.1 us (51%)
  waiting for transfers between devices  17.3 us (29%)
  Pallas kernels  10.8 us (18%)
  between operations  0.72 us (1%)
    ppermute x22, starting transfers between devices, swap(): lax.ppermute(array, axis, [(index, index ^ mask) for index in range(size)])  30.1 us
    ppermute x22, waiting for transfers between devices, swap(): lax.ppermute(array, axis, [(index, index ^ mask) for index in range(size)])  17.3 us
    pallas_call x7, Pallas kernels, call(): pl.pallas_call(kernel, out_shape=out_shape, in_specs=in_specs, out_specs=...  10.8 us
  transfers between devices with their start and end apart: 22, of which 10 were waited for; matrix products, arithmetic and copies ran while one was open for 0% of the time, Pallas kernels for 5%

profile of v4, /device:TPU:0, one launch (start us, length us, event | category | flops | bytes accessed | tf_op | source)
XLA Modules:
  0.0 58.9 jit_solution(17542477807887811574)
XLA Ops:
  0.6 1.7 %shard_map.110 = (bf16[2,384,128]{2,1,0:T(8,128)(2,1)S(1)}, bf16[2,384,128]{2,1,0:T(8,128)(2,1)S(1)}, bf16[2,384,128]{2,1,0:T(8,128)(2,1)S(1)}, bf16[2,384,128]{...) custom-call(bf16[384,512]{1,0:T(8,128)(2,1)} %refs_0_.1, ...), custom_call_target="tpu_custom_call" | custom-call | tf_op jit(solution)/shard_map/pallas_call | solution.py:428
  2.4 3.0 %collective-permute-start.4 = (bf16[2,384,128]{2,1,0:T(8,128)(2,1)S(1)}, bf16[2,384,128]{2,1,0:T(8,128)(2,1)S(1)}, u32[]{:S(2)}, u32[]{:S(2)}) collective-permute-start(bf16[2,384,128]{2,1,0:T(8,128)(2,1)S(1)} %get-tuple-element.58), channel_id=1, source_target_pairs={{0,8},{8,0},{16,24},{24,16},{1,9},{9,1},{17,25},{25,17},{2,10},{10... | collective-permute-start | bytes 589832 | tf_op jit(solution)/shard_map/ppermute | solution.py:403
  5.4 1.5 %collective-permute-start.5 = (bf16[2,384,128]{2,1,0:T(8,128)(2,1)S(1)}, bf16[2,384,128]{2,1,0:T(8,128)(2,1)S(1)}, u32[]{:S(2)}, u32[]{:S(2)}) collective-permute-start(bf16[2,384,128]{2,1,0:T(8,128)(2,1)S(1)} %get-tuple-element.59), channel_id=1, source_target_pairs={{0,16},{8,24},{16,0},{24,8},{1,17},{9,25},{17,1},{25,9},{2,18},{10... | collective-permute-start | bytes 589832 | tf_op jit(solution)/shard_map/ppermute | solution.py:403
  8.1 4.1 %collective-permute-start.3 = (f32[2,384]{1,0:T(2,128)S(1)}, f32[2,384]{1,0:T(2,128)S(1)}, u32[]{:S(2)}, u32[]{:S(2)}) collective-permute-start(f32[2,384]{1,0:T(2,128)S(1)} %add.9.refs_0_), channel_id=1, source_target_pairs={{0,6},{1,7},{2,4},{3,5},{4,2},{5,3},{6,0},{7,1},{8,14},{9,15},{10,... | collective-permute-start | bytes 9224 | tf_op jit(solution)/shard_map/ppermute | solution.py:403
  12.2 1.6 %collective-permute-done.3.refs_3_ = f32[2,384]{1,0:T(2,128)S(1)} collective-permute-done((f32[2,384]{1,0:T(2,128)S(1)}, f32[2,384]{1,0:T(2,128)S(1)}, u32[]{:S(2)}, u32[]{:S(2)}) %collective-permute-start.3) | collective-permute-done | bytes 3104 | tf_op jit(solution)/shard_map/ppermute | solution.py:403
  13.7 2.9 %collective-permute-done.2.refs_2_ = f32[2,384]{1,0:T(2,128)S(1)} collective-permute-done((f32[2,384]{1,0:T(2,128)S(1)}, f32[2,384]{1,0:T(2,128)S(1)}, u32[]{:S(2)}, u32[]{:S(2)}) %collective-permute-start.2) | collective-permute-done | bytes 3104 | tf_op jit(solution)/shard_map/ppermute | solution.py:403
  17.7 1.8 %collective-permute-start.10 = (bf16[2,192,128]{2,1,0:T(8,128)(2,1)S(1)}, bf16[2,192,128]{2,1,0:T(8,128)(2,1)S(1)}, u32[]{:S(2)}, u32[]{:S(2)}) collective-permute-start(bf16[2,192,128]{2,1,0:T(8,128)(2,1)S(1)} %get-tuple-element.68), channel_id=1, source_target_pairs={{0,8},{8,0},{16,24},{24,16},{1,9},{9,1},{17,25},{25,17},{2,10},{10... | collective-permute-start | bytes 294920 | tf_op jit(solution)/shard_map/ppermute | solution.py:403
  19.5 1.5 %collective-permute-start.11 = (bf16[2,192,128]{2,1,0:T(8,128)(2,1)S(1)}, bf16[2,192,128]{2,1,0:T(8,128)(2,1)S(1)}, u32[]{:S(2)}, u32[]{:S(2)}) collective-permute-start(bf16[2,192,128]{2,1,0:T(8,128)(2,1)S(1)} %get-tuple-element.69), channel_id=1, source_target_pairs={{0,16},{8,24},{16,0},{24,8},{1,17},{9,25},{17,1},{25,9},{2,18},{10... | collective-permute-start | bytes 294920 | tf_op jit(solution)/shard_map/ppermute | solution.py:403
  21.0 1.4 %collective-permute-done.10.refs_1_ = bf16[2,192,128]{2,1,0:T(8,128)(2,1)S(1)} collective-permute-done((bf16[2,192,128]{2,1,0:T(8,128)(2,1)S(1)}, bf16[2,192,128]{2,1,0:T(8,128)(2,1)S(1)}, u32[]{:S(2)}, u32[]{:S(2)}) %collective-permute-start.10) | collective-permute-done | bytes 98336 | tf_op jit(solution)/shard_map/ppermute | solution.py:403
  22.4 3.0 %collective-permute-start.12 = (bf16[2,192,128]{2,1,0:T(8,128)(2,1)S(1)}, bf16[2,192,128]{2,1,0:T(8,128)(2,1)S(1)}, u32[]{:S(2)}, u32[]{:S(2)}) collective-permute-start(bf16[2,192,128]{2,1,0:T(8,128)(2,1)S(1)} %get-tuple-element.70), channel_id=1, source_target_pairs={{0,24},{8,16},{16,8},{24,0},{1,25},{9,17},{17,9},{25,1},{2,26},{10... | collective-permute-start | bytes 294920 | tf_op jit(solution)/shard_map/ppermute | solution.py:403
  26.0 2.9 %collective-permute-start.9 = (bf16[2,192,128]{2,1,0:T(8,128)(2,1)S(1)}, bf16[2,192,128]{2,1,0:T(8,128)(2,1)S(1)}, u32[]{:S(2)}, u32[]{:S(2)}) collective-permute-start(bf16[2,192,128]{2,1,0:T(8,128)(2,1)S(1)} %get-tuple-element.66), channel_id=1, source_target_pairs={{0,24},{8,16},{16,8},{24,0},{1,25},{9,17},{17,9},{25,1},{2,26},{10... | collective-permute-start | bytes 294920 | tf_op jit(solution)/shard_map/ppermute | solution.py:403
  30.0 1.7 %shard_map.113 = (bf16[768,128]{1,0:T(8,128)(2,1)S(1)}, bf16[768,128]{1,0:T(8,128)(2,1)S(1)}, bf16[768,128]{1,0:T(8,128)(2,1)S(1)}, f32[768,128]{1,0:T(8,128)S(1...) custom-call(s32[1,8]{1,0:T(1,128)S(1)} %get-tuple-element.49.numbers_ref, ...), custom_call_target="tpu_custom_call" | custom-call | tf_op jit(solution)/shard_map/pallas_call | solution.py:428
  31.8 4.0 %shard_map.114 = (bf16[3,384,128]{2,1,0:T(8,128)(2,1)S(1)}, bf16[3,384,128]{2,1,0:T(8,128)(2,1)S(1)}, bf16[3,384,128]{2,1,0:T(8,128)(2,1)S(1)}, bf16[3,384,128]{...) custom-call(s32[1,8]{1,0:T(1,128)S(1)} %get-tuple-element.49.numbers_ref, ...), custom_call_target="tpu_custom_call" | custom-call | tf_op jit(solution)/shard_map/pallas_call | solution.py:428
  35.8 1.4 %collective-permute-start.13 = (bf16[3,384,128]{2,1,0:T(8,128)(2,1)S(1)}, bf16[3,384,128]{2,1,0:T(8,128)(2,1)S(1)}, u32[]{:S(2)}, u32[]{:S(2)}) collective-permute-start(bf16[3,384,128]{2,1,0:T(8,128)(2,1)S(1)} %get-tuple-element.79), channel_id=1, source_target_pairs={{0,8},{8,0},{16,24},{24,16},{1,9},{9,1},{17,25},{25,17},{2,10},{10... | collective-permute-start | bytes 884744 | tf_op jit(solution)/shard_map/ppermute | solution.py:403
  37.2 1.9 %collective-permute-start.14 = (bf16[3,384,128]{2,1,0:T(8,128)(2,1)S(1)}, bf16[3,384,128]{2,1,0:T(8,128)(2,1)S(1)}, u32[]{:S(2)}, u32[]{:S(2)}) collective-permute-start(bf16[3,384,128]{2,1,0:T(8,128)(2,1)S(1)} %get-tuple-element.80), channel_id=1, source_target_pairs={{0,16},{8,24},{16,0},{24,8},{1,17},{9,25},{17,1},{25,9},{2,18},{10... | collective-permute-start | bytes 884744 | tf_op jit(solution)/shard_map/ppermute | solution.py:403
  39.3 1.2 %collective-permute-done.16 = f32[8,384]{1,0:T(8,128)S(1)} collective-permute-done((f32[8,384]{1,0:T(8,128)S(1)}, f32[8,384]{1,0:T(8,128)S(1)}, u32[]{:S(2)}, u32[]{:S(2)}) %collective-permute-start.16) | collective-permute-done | bytes 12320 | tf_op jit(solution)/shard_map/ppermute | solution.py:403
  40.5 3.7 %collective-permute-done.17 = f32[8,384]{1,0:T(8,128)S(1)} collective-permute-done((f32[8,384]{1,0:T(8,128)S(1)}, f32[8,384]{1,0:T(8,128)S(1)}, u32[]{:S(2)}, u32[]{:S(2)}) %collective-permute-start.17) | collective-permute-done | bytes 12320 | tf_op jit(solution)/shard_map/ppermute | solution.py:403
  44.2 2.2 %collective-permute-start.18 = (f32[8,384]{1,0:T(8,128)S(1)}, f32[8,384]{1,0:T(8,128)S(1)}, u32[]{:S(2)}, u32[]{:S(2)}) collective-permute-start(f32[8,384]{1,0:T(8,128)S(1)} %add.11.refs_0_), channel_id=1, source_target_pairs={{0,4},{1,5},{2,6},{3,7},{4,0},{5,1},{6,2},{7,3},{8,12},{9,13},{10,... | collective-permute-start | bytes 36872 | tf_op jit(solution)/shard_map/ppermute | solution.py:403
  46.4 2.4 %collective-permute-done.18.refs_1_ = f32[8,384]{1,0:T(8,128)S(1)} collective-permute-done((f32[8,384]{1,0:T(8,128)S(1)}, f32[8,384]{1,0:T(8,128)S(1)}, u32[]{:S(2)}, u32[]{:S(2)}) %collective-permute-start.18) | collective-permute-done | bytes 12320 | tf_op jit(solution)/shard_map/ppermute | solution.py:403
  48.8 1.3 %collective-permute-start.19 = (f32[4,384]{1,0:T(4,128)S(1)}, f32[4,384]{1,0:T(4,128)S(1)}, u32[]{:S(2)}, u32[]{:S(2)}) collective-permute-start(f32[4,384]{1,0:T(4,128)S(1)} %get-tuple-element.85), channel_id=1, source_target_pairs={{0,8},{8,0},{16,24},{24,16},{1,9},{9,1},{17,25},{25,17},{2,10},{10... | collective-permute-start | bytes 18440 | tf_op jit(solution)/shard_map/ppermute | solution.py:403
  50.1 1.9 %collective-permute-start.20 = (f32[4,384]{1,0:T(4,128)S(1)}, f32[4,384]{1,0:T(4,128)S(1)}, u32[]{:S(2)}, u32[]{:S(2)}) collective-permute-start(f32[4,384]{1,0:T(4,128)S(1)} %get-tuple-element.86), channel_id=1, source_target_pairs={{0,16},{8,24},{16,0},{24,8},{1,17},{9,25},{17,1},{25,9},{2,18},{10... | collective-permute-start | bytes 18440 | tf_op jit(solution)/shard_map/ppermute | solution.py:403
  52.4 2.7 %collective-permute-start.21 = (f32[4,384]{1,0:T(4,128)S(1)}, f32[4,384]{1,0:T(4,128)S(1)}, u32[]{:S(2)}, u32[]{:S(2)}) collective-permute-start(f32[4,384]{1,0:T(4,128)S(1)} %get-tuple-element.87), channel_id=1, source_target_pairs={{0,24},{8,16},{16,8},{24,0},{1,25},{9,17},{17,9},{25,1},{2,26},{10... | collective-permute-start | bytes 18440 | tf_op jit(solution)/shard_map/ppermute | solution.py:403
  55.1 1.9 %collective-permute-done.21.refs_11_ = f32[4,384]{1,0:T(4,128)S(1)} collective-permute-done((f32[4,384]{1,0:T(4,128)S(1)}, f32[4,384]{1,0:T(4,128)S(1)}, u32[]{:S(2)}, u32[]{:S(2)}) %collective-permute-start.21) | collective-permute-done | bytes 6176 | tf_op jit(solution)/shard_map/ppermute | solution.py:403
  57.0 1.9 %shard_map.116 = (bf16[384,512]{1,0:T(8,128)(2,1)}, bf16[384,512]{1,0:T(8,128)(2,1)}, bf16[384,512]{1,0:T(8,128)(2,1)}, f32[1,512]{1,0:T(1,128)}, f32[1,512]{1,0:T(1,128)}) custom-call(f32[2,384]{1,0:T(2,128)S(1)} %get-tuple-element.56.squares_ref, f32[2,512]{1,0:T(2,128)S(1)} %get-tuple-element.50.gains_ref, ...), custom_call_target="tpu_custom_call" | custom-call | tf_op jit(solution)/shard_map/pallas_call | solution.py:428
  (30 shorter events, 4.6 us)
Async XLA Ops:
  2.4 23.1 %collective-permute-start.4 = (bf16[2,384,128]{2,1,0:T(8,128)(2,1)S(1)}, bf16[2,384,128]{2,1,0:T(8,128)(2,1)S(1)}, u32[]{:S(2)}, u32[]{:S(2)}) collective-permute-start(bf16[2,384,128]{2,1,0:T(8,128)(2,1)S(1)} %get-tuple-element.58), channel_id=1, source_target_pairs={{0,8},{8,0},{16,24},{24,16},{1,9},{9,1},{17,25},{25,17},{2,10},{10... | collective-permute-start | bytes 589832 | tf_op jit(solution)/shard_map/ppermute | solution.py:403
  5.4 20.6 %collective-permute-start.5 = (bf16[2,384,128]{2,1,0:T(8,128)(2,1)S(1)}, bf16[2,384,128]{2,1,0:T(8,128)(2,1)S(1)}, u32[]{:S(2)}, u32[]{:S(2)}) collective-permute-start(bf16[2,384,128]{2,1,0:T(8,128)(2,1)S(1)} %get-tuple-element.59), channel_id=1, source_target_pairs={{0,16},{8,24},{16,0},{24,8},{1,17},{9,25},{17,1},{25,9},{2,18},{10... | collective-permute-start | bytes 589832 | tf_op jit(solution)/shard_map/ppermute | solution.py:403
  6.9 19.1 %collective-permute-start.6 = (bf16[2,384,128]{2,1,0:T(8,128)(2,1)S(1)}, bf16[2,384,128]{2,1,0:T(8,128)(2,1)S(1)}, u32[]{:S(2)}, u32[]{:S(2)}) collective-permute-start(bf16[2,384,128]{2,1,0:T(8,128)(2,1)S(1)} %get-tuple-element.60), channel_id=1, source_target_pairs={{0,24},{8,16},{16,8},{24,0},{1,25},{9,17},{17,9},{25,1},{2,26},{10... | collective-permute-start | bytes 589832 | tf_op jit(solution)/shard_map/ppermute | solution.py:403
  6.9 1.2 %collective-permute-start = (f32[2,384]{1,0:T(2,128)S(1)}, f32[2,384]{1,0:T(2,128)S(1)}, u32[]{:S(2)}, u32[]{:S(2)}) collective-permute-start(f32[2,384]{1,0:T(2,128)S(1)} %get-tuple-element.51), channel_id=1, source_target_pairs={{0,1},{1,0},{2,3},{3,2},{4,5},{5,4},{6,7},{7,6},{8,9},{9,8},{10,11... | collective-permute-start | bytes 9224 | tf_op jit(solution)/shard_map/ppermute | solution.py:403
  8.1 5.6 %collective-permute-start.3 = (f32[2,384]{1,0:T(2,128)S(1)}, f32[2,384]{1,0:T(2,128)S(1)}, u32[]{:S(2)}, u32[]{:S(2)}) collective-permute-start(f32[2,384]{1,0:T(2,128)S(1)} %add.9.refs_0_), channel_id=1, source_target_pairs={{0,6},{1,7},{2,4},{3,5},{4,2},{5,3},{6,0},{7,1},{8,14},{9,15},{10,... | collective-permute-start | bytes 9224 | tf_op jit(solution)/shard_map/ppermute | solution.py:403
  12.2 4.5 %collective-permute-start.2 = (f32[2,384]{1,0:T(2,128)S(1)}, f32[2,384]{1,0:T(2,128)S(1)}, u32[]{:S(2)}, u32[]{:S(2)}) collective-permute-start(f32[2,384]{1,0:T(2,128)S(1)} %add.9.refs_0_), channel_id=1, source_target_pairs={{0,4},{1,5},{2,6},{3,7},{4,0},{5,1},{6,2},{7,3},{8,12},{9,13},{10,... | collective-permute-start | bytes 9224 | tf_op jit(solution)/shard_map/ppermute | solution.py:403
  13.7 3.6 %collective-permute-start.1 = (f32[2,384]{1,0:T(2,128)S(1)}, f32[2,384]{1,0:T(2,128)S(1)}, u32[]{:S(2)}, u32[]{:S(2)}) collective-permute-start(f32[2,384]{1,0:T(2,128)S(1)} %add.9.refs_0_), channel_id=1, source_target_pairs={{0,2},{1,3},{2,0},{3,1},{4,6},{5,7},{6,4},{7,5},{8,10},{9,11},{10,... | collective-permute-start | bytes 9224 | tf_op jit(solution)/shard_map/ppermute | solution.py:403
  17.7 4.7 %collective-permute-start.10 = (bf16[2,192,128]{2,1,0:T(8,128)(2,1)S(1)}, bf16[2,192,128]{2,1,0:T(8,128)(2,1)S(1)}, u32[]{:S(2)}, u32[]{:S(2)}) collective-permute-start(bf16[2,192,128]{2,1,0:T(8,128)(2,1)S(1)} %get-tuple-element.68), channel_id=1, source_target_pairs={{0,8},{8,0},{16,24},{24,16},{1,9},{9,1},{17,25},{25,17},{2,10},{10... | collective-permute-start | bytes 294920 | tf_op jit(solution)/shard_map/ppermute | solution.py:403
  19.5 10.5 %collective-permute-start.11 = (bf16[2,192,128]{2,1,0:T(8,128)(2,1)S(1)}, bf16[2,192,128]{2,1,0:T(8,128)(2,1)S(1)}, u32[]{:S(2)}, u32[]{:S(2)}) collective-permute-start(bf16[2,192,128]{2,1,0:T(8,128)(2,1)S(1)} %get-tuple-element.69), channel_id=1, source_target_pairs={{0,16},{8,24},{16,0},{24,8},{1,17},{9,25},{17,1},{25,9},{2,18},{10... | collective-permute-start | bytes 294920 | tf_op jit(solution)/shard_map/ppermute | solution.py:403
  22.4 7.6 %collective-permute-start.12 = (bf16[2,192,128]{2,1,0:T(8,128)(2,1)S(1)}, bf16[2,192,128]{2,1,0:T(8,128)(2,1)S(1)}, u32[]{:S(2)}, u32[]{:S(2)}) collective-permute-start(bf16[2,192,128]{2,1,0:T(8,128)(2,1)S(1)} %get-tuple-element.70), channel_id=1, source_target_pairs={{0,24},{8,16},{16,8},{24,0},{1,25},{9,17},{17,9},{25,1},{2,26},{10... | collective-permute-start | bytes 294920 | tf_op jit(solution)/shard_map/ppermute | solution.py:403
  25.4 6.3 %collective-permute-start.7 = (bf16[2,192,128]{2,1,0:T(8,128)(2,1)S(1)}, bf16[2,192,128]{2,1,0:T(8,128)(2,1)S(1)}, u32[]{:S(2)}, u32[]{:S(2)}) collective-permute-start(bf16[2,192,128]{2,1,0:T(8,128)(2,1)S(1)} %get-tuple-element.64), channel_id=1, source_target_pairs={{0,8},{8,0},{16,24},{24,16},{1,9},{9,1},{17,25},{25,17},{2,10},{10... | collective-permute-start | bytes 294920 | tf_op jit(solution)/shard_map/ppermute | solution.py:403
  26.0 5.8 %collective-permute-start.8 = (bf16[2,192,128]{2,1,0:T(8,128)(2,1)S(1)}, bf16[2,192,128]{2,1,0:T(8,128)(2,1)S(1)}, u32[]{:S(2)}, u32[]{:S(2)}) collective-permute-start(bf16[2,192,128]{2,1,0:T(8,128)(2,1)S(1)} %get-tuple-element.65), channel_id=1, source_target_pairs={{0,16},{8,24},{16,0},{24,8},{1,17},{9,25},{17,1},{25,9},{2,18},{10... | collective-permute-start | bytes 294920 | tf_op jit(solution)/shard_map/ppermute | solution.py:403
  26.0 5.8 %collective-permute-start.9 = (bf16[2,192,128]{2,1,0:T(8,128)(2,1)S(1)}, bf16[2,192,128]{2,1,0:T(8,128)(2,1)S(1)}, u32[]{:S(2)}, u32[]{:S(2)}) collective-permute-start(bf16[2,192,128]{2,1,0:T(8,128)(2,1)S(1)} %get-tuple-element.66), channel_id=1, source_target_pairs={{0,24},{8,16},{16,8},{24,0},{1,25},{9,17},{17,9},{25,1},{2,26},{10... | collective-permute-start | bytes 294920 | tf_op jit(solution)/shard_map/ppermute | solution.py:403
  35.8 21.2 %collective-permute-start.13 = (bf16[3,384,128]{2,1,0:T(8,128)(2,1)S(1)}, bf16[3,384,128]{2,1,0:T(8,128)(2,1)S(1)}, u32[]{:S(2)}, u32[]{:S(2)}) collective-permute-start(bf16[3,384,128]{2,1,0:T(8,128)(2,1)S(1)} %get-tuple-element.79), channel_id=1, source_target_pairs={{0,8},{8,0},{16,24},{24,16},{1,9},{9,1},{17,25},{25,17},{2,10},{10... | collective-permute-start | bytes 884744 | tf_op jit(solution)/shard_map/ppermute | solution.py:403
  37.2 19.8 %collective-permute-start.14 = (bf16[3,384,128]{2,1,0:T(8,128)(2,1)S(1)}, bf16[3,384,128]{2,1,0:T(8,128)(2,1)S(1)}, u32[]{:S(2)}, u32[]{:S(2)}) collective-permute-start(bf16[3,384,128]{2,1,0:T(8,128)(2,1)S(1)} %get-tuple-element.80), channel_id=1, source_target_pairs={{0,16},{8,24},{16,0},{24,8},{1,17},{9,25},{17,1},{25,9},{2,18},{10... | collective-permute-start | bytes 884744 | tf_op jit(solution)/shard_map/ppermute | solution.py:403
  39.1 17.9 %collective-permute-start.15 = (bf16[3,384,128]{2,1,0:T(8,128)(2,1)S(1)}, bf16[3,384,128]{2,1,0:T(8,128)(2,1)S(1)}, u32[]{:S(2)}, u32[]{:S(2)}) collective-permute-start(bf16[3,384,128]{2,1,0:T(8,128)(2,1)S(1)} %get-tuple-element.81), channel_id=1, source_target_pairs={{0,24},{8,16},{16,8},{24,0},{1,25},{9,17},{17,9},{25,1},{2,26},{10... | collective-permute-start | bytes 884744 | tf_op jit(solution)/shard_map/ppermute | solution.py:403
  39.3 1.2 %collective-permute-start.16 = (f32[8,384]{1,0:T(8,128)S(1)}, f32[8,384]{1,0:T(8,128)S(1)}, u32[]{:S(2)}, u32[]{:S(2)}) collective-permute-start(f32[8,384]{1,0:T(8,128)S(1)} %get-tuple-element.83), channel_id=1, source_target_pairs={{0,1},{1,0},{2,3},{3,2},{4,5},{5,4},{6,7},{7,6},{8,9},{9,8},{10,11... | collective-permute-start | bytes 36872 | tf_op jit(solution)/shard_map/ppermute | solution.py:403
  40.5 3.7 %collective-permute-start.17 = (f32[8,384]{1,0:T(8,128)S(1)}, f32[8,384]{1,0:T(8,128)S(1)}, u32[]{:S(2)}, u32[]{:S(2)}) collective-permute-start(f32[8,384]{1,0:T(8,128)S(1)} %add.10), channel_id=1, source_target_pairs={{0,2},{1,3},{2,0},{3,1},{4,6},{5,7},{6,4},{7,5},{8,10},{9,11},{10,... | collective-permute-start | bytes 36872 | tf_op jit(solution)/shard_map/ppermute | solution.py:403
  44.2 4.6 %collective-permute-start.18 = (f32[8,384]{1,0:T(8,128)S(1)}, f32[8,384]{1,0:T(8,128)S(1)}, u32[]{:S(2)}, u32[]{:S(2)}) collective-permute-start(f32[8,384]{1,0:T(8,128)S(1)} %add.11.refs_0_), channel_id=1, source_target_pairs={{0,4},{1,5},{2,6},{3,7},{4,0},{5,1},{6,2},{7,3},{8,12},{9,13},{10,... | collective-permute-start | bytes 36872 | tf_op jit(solution)/shard_map/ppermute | solution.py:403
  48.8 3.6 %collective-permute-start.19 = (f32[4,384]{1,0:T(4,128)S(1)}, f32[4,384]{1,0:T(4,128)S(1)}, u32[]{:S(2)}, u32[]{:S(2)}) collective-permute-start(f32[4,384]{1,0:T(4,128)S(1)} %get-tuple-element.85), channel_id=1, source_target_pairs={{0,8},{8,0},{16,24},{24,16},{1,9},{9,1},{17,25},{25,17},{2,10},{10... | collective-permute-start | bytes 18440 | tf_op jit(solution)/shard_map/ppermute | solution.py:403
  50.1 5.0 %collective-permute-start.20 = (f32[4,384]{1,0:T(4,128)S(1)}, f32[4,384]{1,0:T(4,128)S(1)}, u32[]{:S(2)}, u32[]{:S(2)}) collective-permute-start(f32[4,384]{1,0:T(4,128)S(1)} %get-tuple-element.86), channel_id=1, source_target_pairs={{0,16},{8,24},{16,0},{24,8},{1,17},{9,25},{17,1},{25,9},{2,18},{10... | collective-permute-start | bytes 18440 | tf_op jit(solution)/shard_map/ppermute | solution.py:403
  52.4 4.5 %collective-permute-start.21 = (f32[4,384]{1,0:T(4,128)S(1)}, f32[4,384]{1,0:T(4,128)S(1)}, u32[]{:S(2)}, u32[]{:S(2)}) collective-permute-start(f32[4,384]{1,0:T(4,128)S(1)} %get-tuple-element.87), channel_id=1, source_target_pairs={{0,24},{8,16},{16,8},{24,0},{1,25},{9,17},{17,9},{25,1},{2,26},{10... | collective-permute-start | bytes 18440 | tf_op jit(solution)/shard_map/ppermute | solution.py:403

commit v5 on v4

--- a/solution.py
+++ b/solution.py
@@ -89,11 +89,10 @@
 def normalize_kernel(peers, width, members, numbers_ref, gains_ref, *refs):
     parts, raw_refs = refs[:members], refs[members : members + peers]
     low_refs, high_refs = refs[members + peers : members + 2 * peers], refs[members + 2 * peers : members + 3 * peers]
-    total_ref, scale_ref = refs[members + 3 * peers :]
+    scale_ref = refs[members + 3 * peers]
     total = parts[0][...]
     for ref in parts[1:]:
         total = total + ref[...]
-    total_ref[...] = total
     inverse = lax.rsqrt(total / width + EPSILON)
     device = lax.axis_index("ctx")
     stripe = total.shape[1] // 2
@@ -360,7 +359,7 @@
             out_refs[mask][2 + side : 3 + side, :HD] = gain_sums_ref[side : side + 1, :]
 
 
-def finish_kernel(peers, width, squares_ref, gains_ref, *refs):
+def finish_kernel(peers, width, scales_ref, gains_ref, *refs):
     raw_refs, refs = refs[:peers], refs[peers:]
     grads_refs, sums_refs = refs[:peers], refs[peers : 2 * peers]
     out_refs, gain_out_refs = refs[2 * peers : 2 * peers + 3], refs[2 * peers + 3 : 2 * peers + 5]
@@ -383,9 +382,8 @@
     for mask in range(1, peers):
         sums = sums + sums_refs[mask][...]
     means = sums[0:2] / width
-    inverse = lax.rsqrt(squares_ref[...] / width + EPSILON)
     for side in range(2):
-        scale = down_rows(inverse[side : side + 1, :])
+        scale = scales_ref[side]
         drop = scale * down_rows(means[side : side + 1, :])
         for mask in range(peers):
             columns = head_columns(device ^ mask)
@@ -464,13 +462,13 @@
     )
     raw, plain = blocks[:peers], to_peers(blocks[peers:], peers)
     half = shape((2, token_count // 2, HD), jnp.bfloat16)
-    *normed, squares = call(
+    *normed, scales = call(
         functools.partial(normalize_kernel, peers, width, members),
-        [half] * (2 * peers) + [shape((2, token_count), jnp.float32)],
+        [half] * (2 * peers) + [shape((2, token_count, HD), jnp.float32)],
         (numbers, gains, *tp_parts(squares, tp_size), *raw),
         [VMEM] + [VMEM] * (1 + members + peers),
         [VMEM] * (2 * peers + 1),
-        [pltpu.VMEM((2, token_count, HD), jnp.float32)],
+        [],
         8,
     )
     low_normed = to_peers(normed[:peers], peers)
@@ -535,7 +533,7 @@
     grad_query, grad_key, grad_value, query_gain_grad, key_gain_grad = call(
         functools.partial(finish_kernel, peers, width),
         [whole_out] * 3 + [row] * 2,
-        (squares, gains, *raw, *grads, *totals),
+        (scales, gains, *raw, *grads, *totals),
         [VMEM] * (2 + 3 * peers),
         [ANY] * 3 + [VMEM] * 2,
         [

time: 59 us -> 59 us (level)
  no operation moved by 1% of the time
where the time goes in v5:
time: 59 us; the launch traced here: 58.8 us
  starting transfers between devices  30 us (51%)
  waiting for transfers between devices  17.3 us (29%)
  Pallas kernels  10.8 us (18%)
  between operations  0.72 us (1%)
    ppermute x22, starting transfers between devices, swap(): lax.ppermute(array, axis, [(index, index ^ mask) for index in range(size)])  30 us
    ppermute x22, waiting for transfers between devices, swap(): lax.ppermute(array, axis, [(index, index ^ mask) for index in range(size)])  17.3 us
    pallas_call x7, Pallas kernels, call(): pl.pallas_call(kernel, out_shape=out_shape, in_specs=in_specs, out_specs=...  10.8 us
  transfers between devices with their start and end apart: 22, of which 10 were waited for; matrix products, arithmetic and copies ran while one was open for 0% of the time, Pallas kernels for 5%

profile of v5, /device:TPU:0, one launch (start us, length us, event | category | flops | bytes accessed | tf_op | source)
XLA Modules:
  0.0 58.8 jit_solution(15133966723936909739)
XLA Ops:
  0.6 1.7 %shard_map.110 = (bf16[2,384,128]{2,1,0:T(8,128)(2,1)S(1)}, bf16[2,384,128]{2,1,0:T(8,128)(2,1)S(1)}, bf16[2,384,128]{2,1,0:T(8,128)(2,1)S(1)}, bf16[2,384,128]{...) custom-call(bf16[384,512]{1,0:T(8,128)(2,1)} %refs_0_.1, ...), custom_call_target="tpu_custom_call" | custom-call | tf_op jit(solution)/shard_map/pallas_call | solution.py:426
  2.4 3.0 %collective-permute-start.4 = (bf16[2,384,128]{2,1,0:T(8,128)(2,1)S(1)}, bf16[2,384,128]{2,1,0:T(8,128)(2,1)S(1)}, u32[]{:S(2)}, u32[]{:S(2)}) collective-permute-start(bf16[2,384,128]{2,1,0:T(8,128)(2,1)S(1)} %get-tuple-element.58), channel_id=1, source_target_pairs={{0,8},{8,0},{16,24},{24,16},{1,9},{9,1},{17,25},{25,17},{2,10},{10... | collective-permute-start | bytes 589832 | tf_op jit(solution)/shard_map/ppermute | solution.py:401
  5.4 1.5 %collective-permute-start.5 = (bf16[2,384,128]{2,1,0:T(8,128)(2,1)S(1)}, bf16[2,384,128]{2,1,0:T(8,128)(2,1)S(1)}, u32[]{:S(2)}, u32[]{:S(2)}) collective-permute-start(bf16[2,384,128]{2,1,0:T(8,128)(2,1)S(1)} %get-tuple-element.59), channel_id=1, source_target_pairs={{0,16},{8,24},{16,0},{24,8},{1,17},{9,25},{17,1},{25,9},{2,18},{10... | collective-permute-start | bytes 589832 | tf_op jit(solution)/shard_map/ppermute | solution.py:401
  8.1 4.1 %collective-permute-start.3 = (f32[2,384]{1,0:T(2,128)S(1)}, f32[2,384]{1,0:T(2,128)S(1)}, u32[]{:S(2)}, u32[]{:S(2)}) collective-permute-start(f32[2,384]{1,0:T(2,128)S(1)} %add.9.refs_0_), channel_id=1, source_target_pairs={{0,6},{1,7},{2,4},{3,5},{4,2},{5,3},{6,0},{7,1},{8,14},{9,15},{10,... | collective-permute-start | bytes 9224 | tf_op jit(solution)/shard_map/ppermute | solution.py:401
  12.2 1.6 %collective-permute-done.3.refs_3_ = f32[2,384]{1,0:T(2,128)S(1)} collective-permute-done((f32[2,384]{1,0:T(2,128)S(1)}, f32[2,384]{1,0:T(2,128)S(1)}, u32[]{:S(2)}, u32[]{:S(2)}) %collective-permute-start.3) | collective-permute-done | bytes 3104 | tf_op jit(solution)/shard_map/ppermute | solution.py:401
  13.7 2.9 %collective-permute-done.2.refs_2_ = f32[2,384]{1,0:T(2,128)S(1)} collective-permute-done((f32[2,384]{1,0:T(2,128)S(1)}, f32[2,384]{1,0:T(2,128)S(1)}, u32[]{:S(2)}, u32[]{:S(2)}) %collective-permute-start.2) | collective-permute-done | bytes 3104 | tf_op jit(solution)/shard_map/ppermute | solution.py:401
  17.7 1.8 %collective-permute-start.10 = (bf16[2,192,128]{2,1,0:T(8,128)(2,1)S(1)}, bf16[2,192,128]{2,1,0:T(8,128)(2,1)S(1)}, u32[]{:S(2)}, u32[]{:S(2)}) collective-permute-start(bf16[2,192,128]{2,1,0:T(8,128)(2,1)S(1)} %get-tuple-element.68), channel_id=1, source_target_pairs={{0,8},{8,0},{16,24},{24,16},{1,9},{9,1},{17,25},{25,17},{2,10},{10... | collective-permute-start | bytes 294920 | tf_op jit(solution)/shard_map/ppermute | solution.py:401
  19.5 1.5 %collective-permute-start.11 = (bf16[2,192,128]{2,1,0:T(8,128)(2,1)S(1)}, bf16[2,192,128]{2,1,0:T(8,128)(2,1)S(1)}, u32[]{:S(2)}, u32[]{:S(2)}) collective-permute-start(bf16[2,192,128]{2,1,0:T(8,128)(2,1)S(1)} %get-tuple-element.69), channel_id=1, source_target_pairs={{0,16},{8,24},{16,0},{24,8},{1,17},{9,25},{17,1},{25,9},{2,18},{10... | collective-permute-start | bytes 294920 | tf_op jit(solution)/shard_map/ppermute | solution.py:401
  21.0 1.4 %collective-permute-done.10.refs_1_ = bf16[2,192,128]{2,1,0:T(8,128)(2,1)S(1)} collective-permute-done((bf16[2,192,128]{2,1,0:T(8,128)(2,1)S(1)}, bf16[2,192,128]{2,1,0:T(8,128)(2,1)S(1)}, u32[]{:S(2)}, u32[]{:S(2)}) %collective-permute-start.10) | collective-permute-done | bytes 98336 | tf_op jit(solution)/shard_map/ppermute | solution.py:401
  22.4 3.0 %collective-permute-start.12 = (bf16[2,192,128]{2,1,0:T(8,128)(2,1)S(1)}, bf16[2,192,128]{2,1,0:T(8,128)(2,1)S(1)}, u32[]{:S(2)}, u32[]{:S(2)}) collective-permute-start(bf16[2,192,128]{2,1,0:T(8,128)(2,1)S(1)} %get-tuple-element.70), channel_id=1, source_target_pairs={{0,24},{8,16},{16,8},{24,0},{1,25},{9,17},{17,9},{25,1},{2,26},{10... | collective-permute-start | bytes 294920 | tf_op jit(solution)/shard_map/ppermute | solution.py:401
  26.0 2.9 %collective-permute-start.9 = (bf16[2,192,128]{2,1,0:T(8,128)(2,1)S(1)}, bf16[2,192,128]{2,1,0:T(8,128)(2,1)S(1)}, u32[]{:S(2)}, u32[]{:S(2)}) collective-permute-start(bf16[2,192,128]{2,1,0:T(8,128)(2,1)S(1)} %get-tuple-element.66), channel_id=1, source_target_pairs={{0,24},{8,16},{16,8},{24,0},{1,25},{9,17},{17,9},{25,1},{2,26},{10... | collective-permute-start | bytes 294920 | tf_op jit(solution)/shard_map/ppermute | solution.py:401
  30.0 1.8 %shard_map.113 = (bf16[768,128]{1,0:T(8,128)(2,1)S(1)}, bf16[768,128]{1,0:T(8,128)(2,1)S(1)}, bf16[768,128]{1,0:T(8,128)(2,1)S(1)}, f32[768,128]{1,0:T(8,128)S(1...) custom-call(s32[1,8]{1,0:T(1,128)S(1)} %get-tuple-element.49.numbers_ref, ...), custom_call_target="tpu_custom_call" | custom-call | tf_op jit(solution)/shard_map/pallas_call | solution.py:426
  31.8 4.0 %shard_map.114 = (bf16[3,384,128]{2,1,0:T(8,128)(2,1)S(1)}, bf16[3,384,128]{2,1,0:T(8,128)(2,1)S(1)}, bf16[3,384,128]{2,1,0:T(8,128)(2,1)S(1)}, bf16[3,384,128]{...) custom-call(s32[1,8]{1,0:T(1,128)S(1)} %get-tuple-element.49.numbers_ref, ...), custom_call_target="tpu_custom_call" | custom-call | tf_op jit(solution)/shard_map/pallas_call | solution.py:426
  35.8 1.4 %collective-permute-start.13 = (bf16[3,384,128]{2,1,0:T(8,128)(2,1)S(1)}, bf16[3,384,128]{2,1,0:T(8,128)(2,1)S(1)}, u32[]{:S(2)}, u32[]{:S(2)}) collective-permute-start(bf16[3,384,128]{2,1,0:T(8,128)(2,1)S(1)} %get-tuple-element.79), channel_id=1, source_target_pairs={{0,8},{8,0},{16,24},{24,16},{1,9},{9,1},{17,25},{25,17},{2,10},{10... | collective-permute-start | bytes 884744 | tf_op jit(solution)/shard_map/ppermute | solution.py:401
  37.2 1.9 %collective-permute-start.14 = (bf16[3,384,128]{2,1,0:T(8,128)(2,1)S(1)}, bf16[3,384,128]{2,1,0:T(8,128)(2,1)S(1)}, u32[]{:S(2)}, u32[]{:S(2)}) collective-permute-start(bf16[3,384,128]{2,1,0:T(8,128)(2,1)S(1)} %get-tuple-element.80), channel_id=1, source_target_pairs={{0,16},{8,24},{16,0},{24,8},{1,17},{9,25},{17,1},{25,9},{2,18},{10... | collective-permute-start | bytes 884744 | tf_op jit(solution)/shard_map/ppermute | solution.py:401
  39.3 1.2 %collective-permute-done.16 = f32[8,384]{1,0:T(8,128)S(1)} collective-permute-done((f32[8,384]{1,0:T(8,128)S(1)}, f32[8,384]{1,0:T(8,128)S(1)}, u32[]{:S(2)}, u32[]{:S(2)}) %collective-permute-start.16) | collective-permute-done | bytes 12320 | tf_op jit(solution)/shard_map/ppermute | solution.py:401
  40.5 3.7 %collective-permute-done.17 = f32[8,384]{1,0:T(8,128)S(1)} collective-permute-done((f32[8,384]{1,0:T(8,128)S(1)}, f32[8,384]{1,0:T(8,128)S(1)}, u32[]{:S(2)}, u32[]{:S(2)}) %collective-permute-start.17) | collective-permute-done | bytes 12320 | tf_op jit(solution)/shard_map/ppermute | solution.py:401
  44.2 2.2 %collective-permute-start.18 = (f32[8,384]{1,0:T(8,128)S(1)}, f32[8,384]{1,0:T(8,128)S(1)}, u32[]{:S(2)}, u32[]{:S(2)}) collective-permute-start(f32[8,384]{1,0:T(8,128)S(1)} %add.11.refs_0_), channel_id=1, source_target_pairs={{0,4},{1,5},{2,6},{3,7},{4,0},{5,1},{6,2},{7,3},{8,12},{9,13},{10,... | collective-permute-start | bytes 36872 | tf_op jit(solution)/shard_map/ppermute | solution.py:401
  46.4 2.4 %collective-permute-done.18.refs_1_ = f32[8,384]{1,0:T(8,128)S(1)} collective-permute-done((f32[8,384]{1,0:T(8,128)S(1)}, f32[8,384]{1,0:T(8,128)S(1)}, u32[]{:S(2)}, u32[]{:S(2)}) %collective-permute-start.18) | collective-permute-done | bytes 12320 | tf_op jit(solution)/shard_map/ppermute | solution.py:401
  48.8 1.3 %collective-permute-start.19 = (f32[4,384]{1,0:T(4,128)S(1)}, f32[4,384]{1,0:T(4,128)S(1)}, u32[]{:S(2)}, u32[]{:S(2)}) collective-permute-start(f32[4,384]{1,0:T(4,128)S(1)} %get-tuple-element.85), channel_id=1, source_target_pairs={{0,8},{8,0},{16,24},{24,16},{1,9},{9,1},{17,25},{25,17},{2,10},{10... | collective-permute-start | bytes 18440 | tf_op jit(solution)/shard_map/ppermute | solution.py:401
  50.2 1.9 %collective-permute-start.20 = (f32[4,384]{1,0:T(4,128)S(1)}, f32[4,384]{1,0:T(4,128)S(1)}, u32[]{:S(2)}, u32[]{:S(2)}) collective-permute-start(f32[4,384]{1,0:T(4,128)S(1)} %get-tuple-element.86), channel_id=1, source_target_pairs={{0,16},{8,24},{16,0},{24,8},{1,17},{9,25},{17,1},{25,9},{2,18},{10... | collective-permute-start | bytes 18440 | tf_op jit(solution)/shard_map/ppermute | solution.py:401
  52.5 2.6 %collective-permute-start.21 = (f32[4,384]{1,0:T(4,128)S(1)}, f32[4,384]{1,0:T(4,128)S(1)}, u32[]{:S(2)}, u32[]{:S(2)}) collective-permute-start(f32[4,384]{1,0:T(4,128)S(1)} %get-tuple-element.87), channel_id=1, source_target_pairs={{0,24},{8,16},{16,8},{24,0},{1,25},{9,17},{17,9},{25,1},{2,26},{10... | collective-permute-start | bytes 18440 | tf_op jit(solution)/shard_map/ppermute | solution.py:401
  55.1 1.9 %collective-permute-done.21.refs_11_ = f32[4,384]{1,0:T(4,128)S(1)} collective-permute-done((f32[4,384]{1,0:T(4,128)S(1)}, f32[4,384]{1,0:T(4,128)S(1)}, u32[]{:S(2)}, u32[]{:S(2)}) %collective-permute-start.21) | collective-permute-done | bytes 6176 | tf_op jit(solution)/shard_map/ppermute | solution.py:401
  57.0 1.8 %shard_map.116 = (bf16[384,512]{1,0:T(8,128)(2,1)}, bf16[384,512]{1,0:T(8,128)(2,1)}, bf16[384,512]{1,0:T(8,128)(2,1)}, f32[1,512]{1,0:T(1,128)}, f32[1,512]{1,0:T(1,128)}) custom-call(f32[2,384,128]{2,1,0:T(8,128)S(1)} %get-tuple-element.56.scales_ref, f32[2,512]{1,0:T(2,128)S(1)} %get-tuple-element.50.gains_ref, ...), custom_call_target="tpu_custom_call" | custom-call | tf_op jit(solution)/shard_map/pallas_call | solution.py:426
  (30 shorter events, 4.6 us)
Async XLA Ops:
  2.4 23.1 %collective-permute-start.4 = (bf16[2,384,128]{2,1,0:T(8,128)(2,1)S(1)}, bf16[2,384,128]{2,1,0:T(8,128)(2,1)S(1)}, u32[]{:S(2)}, u32[]{:S(2)}) collective-permute-start(bf16[2,384,128]{2,1,0:T(8,128)(2,1)S(1)} %get-tuple-element.58), channel_id=1, source_target_pairs={{0,8},{8,0},{16,24},{24,16},{1,9},{9,1},{17,25},{25,17},{2,10},{10... | collective-permute-start | bytes 589832 | tf_op jit(solution)/shard_map/ppermute | solution.py:401
  5.4 20.6 %collective-permute-start.5 = (bf16[2,384,128]{2,1,0:T(8,128)(2,1)S(1)}, bf16[2,384,128]{2,1,0:T(8,128)(2,1)S(1)}, u32[]{:S(2)}, u32[]{:S(2)}) collective-permute-start(bf16[2,384,128]{2,1,0:T(8,128)(2,1)S(1)} %get-tuple-element.59), channel_id=1, source_target_pairs={{0,16},{8,24},{16,0},{24,8},{1,17},{9,25},{17,1},{25,9},{2,18},{10... | collective-permute-start | bytes 589832 | tf_op jit(solution)/shard_map/ppermute | solution.py:401
  6.9 19.1 %collective-permute-start.6 = (bf16[2,384,128]{2,1,0:T(8,128)(2,1)S(1)}, bf16[2,384,128]{2,1,0:T(8,128)(2,1)S(1)}, u32[]{:S(2)}, u32[]{:S(2)}) collective-permute-start(bf16[2,384,128]{2,1,0:T(8,128)(2,1)S(1)} %get-tuple-element.60), channel_id=1, source_target_pairs={{0,24},{8,16},{16,8},{24,0},{1,25},{9,17},{17,9},{25,1},{2,26},{10... | collective-permute-start | bytes 589832 | tf_op jit(solution)/shard_map/ppermute | solution.py:401
  6.9 1.2 %collective-permute-start = (f32[2,384]{1,0:T(2,128)S(1)}, f32[2,384]{1,0:T(2,128)S(1)}, u32[]{:S(2)}, u32[]{:S(2)}) collective-permute-start(f32[2,384]{1,0:T(2,128)S(1)} %get-tuple-element.51), channel_id=1, source_target_pairs={{0,1},{1,0},{2,3},{3,2},{4,5},{5,4},{6,7},{7,6},{8,9},{9,8},{10,11... | collective-permute-start | bytes 9224 | tf_op jit(solution)/shard_map/ppermute | solution.py:401
  8.1 5.6 %collective-permute-start.3 = (f32[2,384]{1,0:T(2,128)S(1)}, f32[2,384]{1,0:T(2,128)S(1)}, u32[]{:S(2)}, u32[]{:S(2)}) collective-permute-start(f32[2,384]{1,0:T(2,128)S(1)} %add.9.refs_0_), channel_id=1, source_target_pairs={{0,6},{1,7},{2,4},{3,5},{4,2},{5,3},{6,0},{7,1},{8,14},{9,15},{10,... | collective-permute-start | bytes 9224 | tf_op jit(solution)/shard_map/ppermute | solution.py:401
  12.2 4.5 %collective-permute-start.2 = (f32[2,384]{1,0:T(2,128)S(1)}, f32[2,384]{1,0:T(2,128)S(1)}, u32[]{:S(2)}, u32[]{:S(2)}) collective-permute-start(f32[2,384]{1,0:T(2,128)S(1)} %add.9.refs_0_), channel_id=1, source_target_pairs={{0,4},{1,5},{2,6},{3,7},{4,0},{5,1},{6,2},{7,3},{8,12},{9,13},{10,... | collective-permute-start | bytes 9224 | tf_op jit(solution)/shard_map/ppermute | solution.py:401
  13.7 3.6 %collective-permute-start.1 = (f32[2,384]{1,0:T(2,128)S(1)}, f32[2,384]{1,0:T(2,128)S(1)}, u32[]{:S(2)}, u32[]{:S(2)}) collective-permute-start(f32[2,384]{1,0:T(2,128)S(1)} %add.9.refs_0_), channel_id=1, source_target_pairs={{0,2},{1,3},{2,0},{3,1},{4,6},{5,7},{6,4},{7,5},{8,10},{9,11},{10,... | collective-permute-start | bytes 9224 | tf_op jit(solution)/shard_map/ppermute | solution.py:401
  17.7 4.7 %collective-permute-start.10 = (bf16[2,192,128]{2,1,0:T(8,128)(2,1)S(1)}, bf16[2,192,128]{2,1,0:T(8,128)(2,1)S(1)}, u32[]{:S(2)}, u32[]{:S(2)}) collective-permute-start(bf16[2,192,128]{2,1,0:T(8,128)(2,1)S(1)} %get-tuple-element.68), channel_id=1, source_target_pairs={{0,8},{8,0},{16,24},{24,16},{1,9},{9,1},{17,25},{25,17},{2,10},{10... | collective-permute-start | bytes 294920 | tf_op jit(solution)/shard_map/ppermute | solution.py:401
  19.5 10.5 %collective-permute-start.11 = (bf16[2,192,128]{2,1,0:T(8,128)(2,1)S(1)}, bf16[2,192,128]{2,1,0:T(8,128)(2,1)S(1)}, u32[]{:S(2)}, u32[]{:S(2)}) collective-permute-start(bf16[2,192,128]{2,1,0:T(8,128)(2,1)S(1)} %get-tuple-element.69), channel_id=1, source_target_pairs={{0,16},{8,24},{16,0},{24,8},{1,17},{9,25},{17,1},{25,9},{2,18},{10... | collective-permute-start | bytes 294920 | tf_op jit(solution)/shard_map/ppermute | solution.py:401
  22.4 7.6 %collective-permute-start.12 = (bf16[2,192,128]{2,1,0:T(8,128)(2,1)S(1)}, bf16[2,192,128]{2,1,0:T(8,128)(2,1)S(1)}, u32[]{:S(2)}, u32[]{:S(2)}) collective-permute-start(bf16[2,192,128]{2,1,0:T(8,128)(2,1)S(1)} %get-tuple-element.70), channel_id=1, source_target_pairs={{0,24},{8,16},{16,8},{24,0},{1,25},{9,17},{17,9},{25,1},{2,26},{10... | collective-permute-start | bytes 294920 | tf_op jit(solution)/shard_map/ppermute | solution.py:401
  25.4 6.3 %collective-permute-start.7 = (bf16[2,192,128]{2,1,0:T(8,128)(2,1)S(1)}, bf16[2,192,128]{2,1,0:T(8,128)(2,1)S(1)}, u32[]{:S(2)}, u32[]{:S(2)}) collective-permute-start(bf16[2,192,128]{2,1,0:T(8,128)(2,1)S(1)} %get-tuple-element.64), channel_id=1, source_target_pairs={{0,8},{8,0},{16,24},{24,16},{1,9},{9,1},{17,25},{25,17},{2,10},{10... | collective-permute-start | bytes 294920 | tf_op jit(solution)/shard_map/ppermute | solution.py:401
  26.0 5.8 %collective-permute-start.8 = (bf16[2,192,128]{2,1,0:T(8,128)(2,1)S(1)}, bf16[2,192,128]{2,1,0:T(8,128)(2,1)S(1)}, u32[]{:S(2)}, u32[]{:S(2)}) collective-permute-start(bf16[2,192,128]{2,1,0:T(8,128)(2,1)S(1)} %get-tuple-element.65), channel_id=1, source_target_pairs={{0,16},{8,24},{16,0},{24,8},{1,17},{9,25},{17,1},{25,9},{2,18},{10... | collective-permute-start | bytes 294920 | tf_op jit(solution)/shard_map/ppermute | solution.py:401
  26.0 5.8 %collective-permute-start.9 = (bf16[2,192,128]{2,1,0:T(8,128)(2,1)S(1)}, bf16[2,192,128]{2,1,0:T(8,128)(2,1)S(1)}, u32[]{:S(2)}, u32[]{:S(2)}) collective-permute-start(bf16[2,192,128]{2,1,0:T(8,128)(2,1)S(1)} %get-tuple-element.66), channel_id=1, source_target_pairs={{0,24},{8,16},{16,8},{24,0},{1,25},{9,17},{17,9},{25,1},{2,26},{10... | collective-permute-start | bytes 294920 | tf_op jit(solution)/shard_map/ppermute | solution.py:401
  35.8 21.2 %collective-permute-start.13 = (bf16[3,384,128]{2,1,0:T(8,128)(2,1)S(1)}, bf16[3,384,128]{2,1,0:T(8,128)(2,1)S(1)}, u32[]{:S(2)}, u32[]{:S(2)}) collective-permute-start(bf16[3,384,128]{2,1,0:T(8,128)(2,1)S(1)} %get-tuple-element.79), channel_id=1, source_target_pairs={{0,8},{8,0},{16,24},{24,16},{1,9},{9,1},{17,25},{25,17},{2,10},{10... | collective-permute-start | bytes 884744 | tf_op jit(solution)/shard_map/ppermute | solution.py:401
  37.2 19.8 %collective-permute-start.14 = (bf16[3,384,128]{2,1,0:T(8,128)(2,1)S(1)}, bf16[3,384,128]{2,1,0:T(8,128)(2,1)S(1)}, u32[]{:S(2)}, u32[]{:S(2)}) collective-permute-start(bf16[3,384,128]{2,1,0:T(8,128)(2,1)S(1)} %get-tuple-element.80), channel_id=1, source_target_pairs={{0,16},{8,24},{16,0},{24,8},{1,17},{9,25},{17,1},{25,9},{2,18},{10... | collective-permute-start | bytes 884744 | tf_op jit(solution)/shard_map/ppermute | solution.py:401
  39.0 17.9 %collective-permute-start.15 = (bf16[3,384,128]{2,1,0:T(8,128)(2,1)S(1)}, bf16[3,384,128]{2,1,0:T(8,128)(2,1)S(1)}, u32[]{:S(2)}, u32[]{:S(2)}) collective-permute-start(bf16[3,384,128]{2,1,0:T(8,128)(2,1)S(1)} %get-tuple-element.81), channel_id=1, source_target_pairs={{0,24},{8,16},{16,8},{24,0},{1,25},{9,17},{17,9},{25,1},{2,26},{10... | collective-permute-start | bytes 884744 | tf_op jit(solution)/shard_map/ppermute | solution.py:401
  39.3 1.2 %collective-permute-start.16 = (f32[8,384]{1,0:T(8,128)S(1)}, f32[8,384]{1,0:T(8,128)S(1)}, u32[]{:S(2)}, u32[]{:S(2)}) collective-permute-start(f32[8,384]{1,0:T(8,128)S(1)} %get-tuple-element.83), channel_id=1, source_target_pairs={{0,1},{1,0},{2,3},{3,2},{4,5},{5,4},{6,7},{7,6},{8,9},{9,8},{10,11... | collective-permute-start | bytes 36872 | tf_op jit(solution)/shard_map/ppermute | solution.py:401
  40.5 3.7 %collective-permute-start.17 = (f32[8,384]{1,0:T(8,128)S(1)}, f32[8,384]{1,0:T(8,128)S(1)}, u32[]{:S(2)}, u32[]{:S(2)}) collective-permute-start(f32[8,384]{1,0:T(8,128)S(1)} %add.10), channel_id=1, source_target_pairs={{0,2},{1,3},{2,0},{3,1},{4,6},{5,7},{6,4},{7,5},{8,10},{9,11},{10,... | collective-permute-start | bytes 36872 | tf_op jit(solution)/shard_map/ppermute | solution.py:401
  44.2 4.6 %collective-permute-start.18 = (f32[8,384]{1,0:T(8,128)S(1)}, f32[8,384]{1,0:T(8,128)S(1)}, u32[]{:S(2)}, u32[]{:S(2)}) collective-permute-start(f32[8,384]{1,0:T(8,128)S(1)} %add.11.refs_0_), channel_id=1, source_target_pairs={{0,4},{1,5},{2,6},{3,7},{4,0},{5,1},{6,2},{7,3},{8,12},{9,13},{10,... | collective-permute-start | bytes 36872 | tf_op jit(solution)/shard_map/ppermute | solution.py:401
  48.8 3.6 %collective-permute-start.19 = (f32[4,384]{1,0:T(4,128)S(1)}, f32[4,384]{1,0:T(4,128)S(1)}, u32[]{:S(2)}, u32[]{:S(2)}) collective-permute-start(f32[4,384]{1,0:T(4,128)S(1)} %get-tuple-element.85), channel_id=1, source_target_pairs={{0,8},{8,0},{16,24},{24,16},{1,9},{9,1},{17,25},{25,17},{2,10},{10... | collective-permute-start | bytes 18440 | tf_op jit(solution)/shard_map/ppermute | solution.py:401
  50.2 4.9 %collective-permute-start.20 = (f32[4,384]{1,0:T(4,128)S(1)}, f32[4,384]{1,0:T(4,128)S(1)}, u32[]{:S(2)}, u32[]{:S(2)}) collective-permute-start(f32[4,384]{1,0:T(4,128)S(1)} %get-tuple-element.86), channel_id=1, source_target_pairs={{0,16},{8,24},{16,0},{24,8},{1,17},{9,25},{17,1},{25,9},{2,18},{10... | collective-permute-start | bytes 18440 | tf_op jit(solution)/shard_map/ppermute | solution.py:401
  52.5 4.5 %collective-permute-start.21 = (f32[4,384]{1,0:T(4,128)S(1)}, f32[4,384]{1,0:T(4,128)S(1)}, u32[]{:S(2)}, u32[]{:S(2)}) collective-permute-start(f32[4,384]{1,0:T(4,128)S(1)} %get-tuple-element.87), channel_id=1, source_target_pairs={{0,24},{8,16},{16,8},{24,0},{1,25},{9,17},{17,9},{25,1},{2,26},{10... | collective-permute-start | bytes 18440 | tf_op jit(solution)/shard_map/ppermute | solution.py:401
